TPU v7x, 32 devices: a whole 2x2x4 slice. The times are simulated.
32 devices in a mesh: dp: 4 (over x, core), fsdp: 8 (over z, y).
Axes of the slice: x: 2, y: 2, z: 4, core: 2. Of those that a mesh axis runs over, the one named last changes fastest.
Arguments:
- tokens: bfloat16 [8192, 2048], P(('dp', 'fsdp')), may hold values from -6 to 6
- w_q: bfloat16 [2048, 2048], P(('dp', 'fsdp')), may hold values from -0.125 to 0.125
- w_kv: bfloat16 [2048, 256], P(('dp', 'fsdp')), may hold values from -0.125 to 0.125
- g_attn: bfloat16 [2048], P(('dp', 'fsdp')), may hold values from 0.25 to 1.75
- g_mlp: bfloat16 [2048], P(('dp', 'fsdp')), may hold values from 0.25 to 1.75
- w_o: bfloat16 [2048, 2048], P(('dp', 'fsdp')), may hold values from -0.75 to 0.75
- w_gu: bfloat16 [5632, 2, 2048], P(('dp', 'fsdp')), may hold values from -0.125 to 0.125
- w_down: bfloat16 [5632, 2048], P(('dp', 'fsdp')), may hold values from -0.078125 to 0.078125
- grad_out: bfloat16 [8192, 2048], P(('dp', 'fsdp')), may hold values from -6 to 6
- grad_kv: bfloat16 [8192, 256], P(('dp', 'fsdp')), may hold values from -4 to 4
- group_id: int32 [32], P(('dp', 'fsdp')), may hold values from 0 to 7
- group_size: int32 [8], replicated, may hold values from 1 to 4
- group_weight: float32 [8], replicated, may hold values from 1 to 4
Outputs:
- output: bfloat16 [8192, 2048], P(('dp', 'fsdp'))
- d_tokens: float32 [8192, 2048], P(('dp', 'fsdp'))
- kv_out: bfloat16 [8192, 256], P(('dp', 'fsdp'))
- d_kv: float32 [8192, 256], P(('dp', 'fsdp'))
- d_w_q: float32 [2048, 2048], P(('dp', 'fsdp'))
- d_w_kv: float32 [2048, 256], P(('dp', 'fsdp'))
- d_g_attn: float32 [2048], P(('dp', 'fsdp'))
- d_g_mlp: float32 [2048], P(('dp', 'fsdp'))
- d_w_o: float32 [2048, 2048], P(('dp', 'fsdp'))
- d_w_gu: float32 [5632, 2, 2048], P(('dp', 'fsdp'))
- d_w_down: float32 [5632, 2048], P(('dp', 'fsdp'))
All inputs are finite; a program needn't handle non-finite values.
Results may differ from a plain program's by a relative error of at most 0.015.
Values may be sent and summed in bfloat16 or wider, within the bound.
No kernel may reach another device: no remote copies, remote signals or barrier semaphores. Data moves between devices by JAX's collectives and lax.ppermute only.
A program may use at most 256 MiB of HBM per device.

v0:
```python
import jax
import jax.numpy as jnp
from jax import lax
from jax.sharding import PartitionSpec as P

epsilon = 1e-05
theta_base = 10000.0


def rope_tables(length, width):
    halfway = width // 2
    freqs = theta_base ** (-(jnp.arange(halfway, dtype=jnp.float32) * 2.0 / width))
    angles = jnp.arange(length, dtype=jnp.float32)[:, None] * freqs[None, :]
    return (jnp.cos(angles), jnp.sin(angles))


def rotate(vectors, cosines, sine_part):
    halfway = vectors.shape[-1] // 2
    front = vectors[..., :halfway]
    behind = vectors[..., halfway:]
    return jnp.concatenate(
        [front * cosines - behind * sine_part, behind * cosines + front * sine_part], axis=-1
    )


def contract_last(left, right):
    return lax.dot_general(
        left,
        right,
        (((left.ndim - 1,), (right.ndim - 1,)), ((), ())),
        preferred_element_type=jnp.float32,
    )


def contract_first(left, right):
    return lax.dot_general(
        left, right, (((0,), (0,)), ((), ())), preferred_element_type=jnp.float32
    )


def local(
    tokens,
    w_q,
    w_kv,
    g_attn,
    g_mlp,
    w_o,
    w_gu,
    w_down,
    grad_out,
    grad_kv,
    group_id,
    group_size,
    group_weight,
):
    length, width = tokens.shape
    head_dim = grad_kv.shape[1] // 2
    q_width = w_q.shape[1]
    head_count = q_width // head_dim
    matches = jnp.arange(group_size.shape[0], dtype=jnp.int32) == group_id[0]
    factor = jnp.sum(jnp.where(matches, group_weight / group_size.astype(jnp.float32), 0.0))
    cosines, sine_part = rope_tables(length, head_dim)
    x_full = tokens.astype(jnp.float32)
    inv_one = lax.rsqrt(jnp.mean(x_full * x_full, axis=-1, keepdims=True) + epsilon)
    normed_one = x_full * inv_one
    wq_piece = lax.all_gather(w_q, ("dp", "fsdp"), axis=0, tiled=True)
    wkv_piece = lax.all_gather(w_kv, ("dp", "fsdp"), axis=0, tiled=True)
    gain_piece = lax.all_gather(g_attn, ("dp", "fsdp"), axis=0, tiled=True)
    mlp_gain_piece = lax.all_gather(g_mlp, ("dp", "fsdp"), axis=0, tiled=True)
    normed_cols = normed_one
    h_cols = (normed_cols * gain_piece.astype(jnp.float32)).astype(jnp.bfloat16)
    q_acc = jnp.dot(h_cols, wq_piece, preferred_element_type=jnp.float32)
    kv_acc = jnp.dot(h_cols, wkv_piece, preferred_element_type=jnp.float32)
    gain_two = mlp_gain_piece.astype(jnp.float32)
    q_pre, kv_pre, gain_two, h_one = (q_acc, kv_acc, gain_two, h_cols)
    q_low = rotate(
        q_pre.reshape(length, head_count, head_dim), cosines[:, None, :], sine_part[:, None, :]
    ).astype(jnp.bfloat16)
    k_low = rotate(kv_pre[:, :head_dim], cosines, sine_part).astype(jnp.bfloat16)
    v_low = kv_pre[:, head_dim:].astype(jnp.bfloat16)
    score_scale = head_dim ** (-0.5)
    causal = jnp.arange(length)[:, None] >= jnp.arange(length)[None, :]

    def logits_of(queries, keys):
        raw_scores = jnp.einsum("thd,sd->hts", queries, keys, preferred_element_type=jnp.float32)
        return jnp.where(causal[None], raw_scores * score_scale, -1e30)

    logits = logits_of(q_low, k_low)
    row_top = jnp.max(logits, axis=-1, keepdims=True)
    exp_vals = jnp.exp(logits - row_top)
    row_total = jnp.sum(exp_vals, axis=-1, keepdims=True)
    prob_full = exp_vals / row_total
    log_total = row_top + jnp.log(row_total)
    prob_low = prob_full.astype(jnp.bfloat16)
    attended = jnp.einsum("hts,sd->thd", prob_low, v_low, preferred_element_type=jnp.float32)
    attn_low = attended.reshape(length, q_width).astype(jnp.bfloat16)
    branch = jnp.dot(
        attn_low,
        lax.all_gather(w_o, ("dp", "fsdp"), axis=0, tiled=True),
        preferred_element_type=jnp.float32,
    )
    x_mid = x_full + branch
    inv_two = lax.rsqrt(jnp.mean(x_mid * x_mid, axis=-1, keepdims=True) + epsilon)
    normed_two = x_mid * inv_two
    h_two = (normed_two * gain_two).astype(jnp.bfloat16)
    grad_top = grad_out.astype(jnp.float32) * factor
    grad_low = grad_top.astype(jnp.bfloat16)
    ff_rows, grad_rows = (
        lax.all_gather(h_two, "dp", axis=0, tiled=True),
        lax.all_gather(grad_low, "dp", axis=0, tiled=True),
    )
    gu_piece = lax.all_gather(w_gu, "fsdp", axis=0, tiled=True)
    down_piece = lax.all_gather(w_down, "fsdp", axis=0, tiled=True)
    both_proj = jnp.einsum("td,fkd->tkf", ff_rows, gu_piece, preferred_element_type=jnp.float32)
    gate_vals = both_proj[:, 0]
    up_vals = both_proj[:, 1]
    hid_cols = (jax.nn.silu(gate_vals) * up_vals).astype(jnp.bfloat16)
    mlp_out = jnp.dot(hid_cols, down_piece, preferred_element_type=jnp.float32)
    mlp_part = mlp_out
    gate_all = gate_vals
    up_all = up_vals
    mlp_out = lax.psum_scatter(
        mlp_part.astype(jnp.bfloat16), "dp", scatter_dimension=0, tiled=True
    ).astype(jnp.float32)
    gu_piece = lax.all_gather(w_gu, "fsdp", axis=0, tiled=True)
    down_piece = lax.all_gather(w_down, "fsdp", axis=0, tiled=True)
    gate_vals = gate_all
    up_vals = up_all
    d_hid = contract_last(grad_rows, down_piece)
    sigmoid_vals = jax.nn.sigmoid(gate_vals)
    d_gate = d_hid * up_vals * sigmoid_vals * (1.0 + gate_vals * (1.0 - sigmoid_vals))
    d_up = d_hid * gate_vals * sigmoid_vals
    d_both = jnp.stack([d_gate, d_up], axis=1).astype(jnp.bfloat16)
    d_h_two = jnp.einsum("tkf,fkd->td", d_both, gu_piece, preferred_element_type=jnp.float32)
    d_h_part = d_h_two
    d_h_two = lax.psum_scatter(
        d_h_part.astype(jnp.bfloat16), "dp", scatter_dimension=0, tiled=True
    ).astype(jnp.float32)
    d_w_down = lax.psum_scatter(
        contract_first(hid_cols, grad_rows).astype(jnp.bfloat16),
        "fsdp",
        scatter_dimension=0,
        tiled=True,
    ).astype(jnp.float32)
    d_w_gu = lax.psum_scatter(
        jnp.einsum("tkf,td->fkd", d_both, ff_rows, preferred_element_type=jnp.float32).astype(
            jnp.bfloat16
        ),
        "fsdp",
        scatter_dimension=0,
        tiled=True,
    ).astype(jnp.float32)
    output = (x_mid + mlp_out).astype(jnp.bfloat16)
    d_gain_two = jnp.sum(d_h_two * normed_two, axis=0)
    d_normed_two = d_h_two * gain_two
    d_mid = grad_top + inv_two * (
        d_normed_two - normed_two * jnp.mean(d_normed_two * normed_two, axis=-1, keepdims=True)
    )
    d_mid_low = d_mid.astype(jnp.bfloat16)
    d_attended = contract_last(d_mid_low, lax.all_gather(w_o, ("dp", "fsdp"), axis=0, tiled=True))
    d_att_low = d_attended.astype(jnp.bfloat16).reshape(length, head_count, head_dim)
    d_w_o = lax.psum_scatter(
        contract_first(attn_low, d_mid_low), ("dp", "fsdp"), scatter_dimension=0, tiled=True
    )
    prob_back = jnp.exp(logits_of(q_low, k_low) - log_total)
    prob_back_low = prob_back.astype(jnp.bfloat16)
    d_probs = jnp.einsum("thd,sd->hts", d_att_low, v_low, preferred_element_type=jnp.float32)
    d_v_own = jnp.einsum(
        "hts,thd->sd", prob_back_low, d_att_low, preferred_element_type=jnp.float32
    )
    d_logit = prob_back * (d_probs - jnp.sum(prob_back * d_probs, axis=-1, keepdims=True))
    d_raw = (d_logit * score_scale).astype(jnp.bfloat16)
    d_q_rot = jnp.einsum("hts,sd->thd", d_raw, k_low, preferred_element_type=jnp.float32)
    d_k_own = jnp.einsum("hts,thd->sd", d_raw, q_low, preferred_element_type=jnp.float32)
    kv_extra = grad_kv.astype(jnp.float32) * factor
    d_k_total = d_k_own + kv_extra[:, :head_dim]
    d_v_total = d_v_own + kv_extra[:, head_dim:]
    d_kv = jnp.concatenate([d_k_total, d_v_total], axis=1)
    d_kv_low = jnp.concatenate([rotate(d_k_total, cosines, -sine_part), d_v_total], axis=1).astype(
        jnp.bfloat16
    )
    d_q_low = (
        rotate(d_q_rot, cosines[:, None, :], -sine_part[:, None, :])
        .reshape(length, q_width)
        .astype(jnp.bfloat16)
    )
    wq_piece = lax.all_gather(w_q, ("dp", "fsdp"), axis=0, tiled=True)
    wkv_piece = lax.all_gather(w_kv, ("dp", "fsdp"), axis=0, tiled=True)
    gain_piece = lax.all_gather(g_attn, ("dp", "fsdp"), axis=0, tiled=True)
    d_h_cols = contract_last(d_q_low, wq_piece) + contract_last(d_kv_low, wkv_piece)
    normed_cols = normed_one
    d_normed = d_h_cols * gain_piece.astype(jnp.float32)
    d_gain = jnp.sum(d_h_cols * normed_cols, axis=0)
    d_tokens = d_mid + inv_one * (
        d_normed - normed_one * jnp.mean(d_normed * normed_one, axis=-1, keepdims=True)
    )
    joined = jnp.concatenate([d_q_low, d_kv_low], axis=1)
    d_w_in = lax.psum_scatter(
        contract_first(h_one, joined), ("dp", "fsdp"), scatter_dimension=0, tiled=True
    )
    d_g_attn, d_g_mlp = (
        lax.psum_scatter(d_gain, ("dp", "fsdp"), scatter_dimension=0, tiled=True),
        lax.psum_scatter(d_gain_two, ("dp", "fsdp"), scatter_dimension=0, tiled=True),
    )
    kv_out = jnp.concatenate([k_low, v_low], axis=1)
    return (
        output,
        d_tokens,
        kv_out,
        d_kv,
        d_w_in[:, :q_width],
        d_w_in[:, q_width:],
        d_g_attn,
        d_g_mlp,
        d_w_o,
        d_w_gu,
        d_w_down,
    )


def solution(mesh):
    placed = (
        P(("dp", "fsdp"), None),
        P(("dp", "fsdp"), None),
        P(("dp", "fsdp"), None),
        P(("dp", "fsdp")),
        P(("dp", "fsdp")),
        P(("dp", "fsdp"), None),
        P(("dp", "fsdp"), None, None),
        P(("dp", "fsdp"), None),
        P(("dp", "fsdp"), None),
        P(("dp", "fsdp"), None),
        P(("dp", "fsdp")),
        P(),
        P(),
    )
    return jax.shard_map(
        local,
        mesh=mesh,
        in_specs=placed,
        out_specs=(
            P(("dp", "fsdp"), None),
            P(("dp", "fsdp"), None),
            P(("dp", "fsdp"), None),
            P(("dp", "fsdp"), None),
            P(("dp", "fsdp"), None),
            P(("dp", "fsdp"), None),
            P(("dp", "fsdp")),
            P(("dp", "fsdp")),
            P(("dp", "fsdp"), None),
            P(("dp", "fsdp"), None, None),
            P(("dp", "fsdp"), None),
        ),
        check_vma=False,
    )
```

profile of v0, /device:TPU:0, one launch (start us, length us, event | category | flops | bytes accessed | tf_op | source)
XLA Modules:
  0.0 1734.8 jit_solution(2765132462502652689)
XLA Ops:
  13.1 42.2 %all-reduce.6 = (bf16[2048]{0:T(1024)(128)(2,1)S(1)}, bf16[2048]{0:T(1024)(128)(2,1)S(1)}) all-reduce(bf16[2048]{0:T(1024)(128)(2,1)S(1)} %dynamic-update-slice, bf16[2048]{0:T(1024)(128)(2,1)S(1)} %dynamic-update-slice.1), channel_id=1, replica_groups=mesh['dp'=4,'fsdp'=8] {'dp','fsdp'}, use_global_device_ids=true, to_apply=%add | all-reduce | flops 4096 | bytes 16384
  55.6 12.1 all-gather.8.cloned.1.call-done
  70.2 76.8 %all-gather.10.cloned.1.call-done = bf16[2048,2048]{1,0:T(8,128)(2,1)} async-done(((bf16[64,2048]{1,0:T(8,128)(2,1)}), bf16[2048,2048]{1,0:T(8,128)(2,1)}) %all-gather.10.cloned.1.call-update) | async-done | bytes 8388624 | tf_op jit(solution)/shard_map/all_gather | solution.py:66
  160.6 65.3 %all-gather.12.cloned.1.call-done = bf16[2048,2048]{1,0:T(8,128)(2,1)} async-done(((bf16[64,2048]{1,0:T(8,128)(2,1)}), bf16[2048,2048]{1,0:T(8,128)(2,1)}) %all-gather.12.cloned.1.call-update) | async-done | bytes 8388624 | tf_op jit(solution)/shard_map/all_gather | solution.py:99
  239.1 151.7 %all-gather.16.cloned.1.call-done = bf16[1408,2,2048]{2,0,1:T(8,128)(2,1)} async-done(((bf16[176,2,2048]{2,0,1:T(8,128)(2,1)}), bf16[1408,2,2048]{2,0,1:T(8,128)(2,1)}) %all-gather.16.cloned.1.call-update) | async-done | bytes 11534352 | tf_op jit(solution)/shard_map/all_gather | solution.py:112
  390.8 34.7 %all-gather.14.cloned.1.call-done = bf16[1024,2048]{1,0:T(8,128)(2,1)} async-done(((bf16[256,2048]{1,0:T(8,128)(2,1)}), bf16[1024,2048]{1,0:T(8,128)(2,1)}) %all-gather.14.cloned.1.call-update) | async-done | bytes 4194320 | tf_op jit(solution)/shard_map/all_gather | solution.py:109
  425.5 18.8 %convolution_bitcast_fusion = f32[1024,2,1408]{2,0,1:T(8,128)} fusion(bf16[1408,2,2048]{2,0,1:T(8,128)(2,1)} %all-gather.16.cloned.1.call-done, bf16[1024,2048]{1,0:T(8,128)(2,1)} %all-gather.14.cloned.1.call-done), kind=kOutput, calls=%fused_computation.4 | convolution fusion | flops 11811160064 | bytes 27262976 | tf_op jit(solution)/shard_map/td,fkd->tkf/dot_general | solution.py:114
  444.3 17.7 %all-gather.20.cloned.1.call-done = bf16[1024,2048]{1,0:T(8,128)(2,1)} async-done(((bf16[256,2048]{1,0:T(8,128)(2,1)}), bf16[1024,2048]{1,0:T(8,128)(2,1)}) %all-gather.20.cloned.1.call-update) | async-done | bytes 4194320 | tf_op jit(solution)/shard_map/all_gather | solution.py:110
  462.0 94.9 %all-gather.18.cloned.1.call-done = bf16[1408,2048]{1,0:T(8,128)(2,1)} async-done(((bf16[176,2048]{1,0:T(8,128)(2,1)}), bf16[1408,2048]{1,0:T(8,128)(2,1)}) %all-gather.18.cloned.1.call-update) | async-done | bytes 5767184 | tf_op jit(solution)/shard_map/all_gather | solution.py:113
  556.9 15.6 fusion.13
  575.0 16.3 bitcast_convert_fusion
  591.6 10.9 convolution_convert_fusion.1
  602.6 10.5 convolution_convert_fusion
  613.2 18.3 %convert_bitcast_fusion = bf16[1408,2,2048]{0,2,1:T(8,128)(2,1)} fusion(bf16[1024,2048]{1,0:T(8,128)(2,1)} %all-gather.14.cloned.1.call-done, bf16[1024,1,1408]{2,0,1:T(8,128)(2,1)} %copy-done.31, bf16[1024,1,1408]{2,0,1:T(8,128)(2,1)} %copy-done.30), kind=kOutput, calls=%fused_computation.1 | convolution fusion | flops 11828461568 | bytes 21495808 | tf_op jit(solution)/shard_map/tkf,td->fkd/dot_general | solution.py:146
  631.6 29.4 %copy.89 = bf16[1408,2,2048]{2,1,0:T(2,128)(2,1)} copy(bf16[1408,2,2048]{0,2,1:T(8,128)(2,1)} %convert_bitcast_fusion) | data formatting | bytes 23068672 | tf_op jit(solution)/shard_map/convert_element_type | solution.py:146
  668.8 12.7 reduce-scatter.6.cloned.1.call-done
  697.2 9.2 fusion.49
  707.8 9.5 fusion.35
  727.6 8.2 fusion.37
  737.4 9.3 fusion.53
  760.6 42.5 %all-reduce.5 = (f32[2048]{0:T(1024)S(1)}, f32[2048]{0:T(1024)S(1)}) all-reduce(f32[2048]{0:T(1024)S(1)} %get-tuple-element.46, f32[2048]{0:T(1024)S(1)} %copy-done.21), channel_id=5, replica_groups=mesh['dp'=4,'fsdp'=8] {'dp','fsdp'}, use_global_device_ids=true, to_apply=%region_12.13.clone | all-reduce | flops 4096 | bytes 32768
  810.8 345.1 %all-reduce.9.cloned.1.call-done = bf16[1408,2,2048]{2,1,0:T(2,128)(2,1)} async-done(((bf16[1408,2,2048]{2,1,0:T(2,128)(2,1)}), bf16[1408,2,2048]{2,1,0:T(2,128)(2,1)}) %all-reduce.9.cloned.1.call-update) | async-done | bytes 11534352
  1160.5 207.4 %reduce-scatter.10.cloned.1.call-done = f32[64,2304]{1,0:T(8,128)} async-done(((f32[2048,2304]{1,0:T(8,128)}), f32[64,2304]{1,0:T(8,128)}) %reduce-scatter.10.cloned.1.call-update) | async-done | bytes 589840 | tf_op jit(solution)/shard_map/reduce_scatter | solution.py:198
  1371.3 356.5 %reduce-scatter.12.cloned.1.call-done = f32[64,2048]{1,0:T(8,128)} async-done(((f32[2048,2048]{1,0:T(8,128)}), f32[64,2048]{1,0:T(8,128)}) %reduce-scatter.12.cloned.1.call-update) | async-done | bytes 524304 | tf_op jit(solution)/shard_map/reduce_scatter | solution.py:162
  (150 shorter events, 102.8 us)
Async XLA Ops:
  7.2 48.1 %copy-start.1 = (bf16[256,2048]{1,0:T(8,128)(2,1)S(1)}, bf16[256,2048]{1,0:T(8,128)(2,1)}, u32[]{:S(2)}) copy-start(bf16[256,2048]{1,0:T(8,128)(2,1)} %param.13) | copy-start | bytes 3145732
  7.2 60.6 %all-gather.8.cloned.1.call-start = ((), (), s32[]{:S(2)}) async-start(), calls=%async_computation.5 | async-start | bytes 1081344 | tf_op jit(solution)/shard_map/all_gather | solution.py:67
  7.9 139.1 %all-gather.10.cloned.1.call-start = ((), (), s32[]{:S(2)}) async-start(), calls=%async_computation.6 | async-start | bytes 8650752 | tf_op jit(solution)/shard_map/all_gather | solution.py:66
  8.7 217.2 %all-gather.12.cloned.1.call-start = ((), (), s32[]{:S(2)}) async-start(), calls=%async_computation.7 | async-start | bytes 8650752 | tf_op jit(solution)/shard_map/all_gather | solution.py:99
  9.4 381.4 %all-gather.16.cloned.1.call-start = ((), (), s32[]{:S(2)}) async-start(), calls=%async_computation.9 | async-start | bytes 12976128 | tf_op jit(solution)/shard_map/all_gather | solution.py:112
  12.5 413.0 %all-gather.14.cloned.1.call-start = ((), (), s32[]{:S(2)}) async-start(), calls=%async_computation.8 | async-start | bytes 5242880 | tf_op jit(solution)/shard_map/all_gather | solution.py:109
  55.3 14.7 copy-start.23
  55.6 97.2 %copy-start.19 = (f32[256]{0:T(256)}, f32[256]{0:T(256)S(1)}, u32[]{:S(2)}) copy-start(f32[256]{0:T(256)S(1)} %add_rsqrt_fusion.1) | copy-start | bytes 3076
  69.6 87.6 %copy-start.11 = (f32[256,256]{0,1:T(8,128)}, f32[256,256]{0,1:T(8,128)S(1)}, u32[]{:S(2)}) copy-start(f32[256,256]{0,1:T(8,128)S(1)} %fusion.81) | copy-start | bytes 786436
  70.0 85.3 %copy-start.12 = (bf16[256,64]{0,1:T(8,128)(2,1)}, bf16[256,64]{0,1:T(8,128)(2,1)S(1)}, u32[]{:S(2)}) copy-start(bf16[256,64]{0,1:T(8,128)(2,1)S(1)} %get-tuple-element.63) | copy-start | bytes 98308
  70.0 85.3 %copy-start.14 = (bf16[256,64]{0,1:T(8,128)(2,1)}, bf16[256,64]{0,1:T(8,128)(2,1)S(1)}, u32[]{:S(2)}) copy-start(bf16[256,64]{0,1:T(8,128)(2,1)S(1)} %get-tuple-element.64) | copy-start | bytes 98308
  232.1 5.8 copy-start.22
  233.4 228.6 %all-gather.20.cloned.1.call-start = ((), (), s32[]{:S(2)}) async-start(), calls=%async_computation.12 | async-start | bytes 5242880 | tf_op jit(solution)/shard_map/all_gather | solution.py:110
  237.9 318.9 %all-gather.18.cloned.1.call-start = ((), (), s32[]{:S(2)}) async-start(), calls=%async_computation.10 | async-start | bytes 6488064 | tf_op jit(solution)/shard_map/all_gather | solution.py:113
  238.7 427.0 %reduce-scatter.8.cloned.1.call-start = ((), (), s32[]{:S(2)}) async-start(), calls=%async_computation.13 | async-start | bytes 5242880 | tf_op jit(solution)/shard_map/reduce_scatter | solution.py:136
  591.4 90.1 %reduce-scatter.6.cloned.1.call-start = ((), (), s32[]{:S(2)}) async-start(), calls=%async_computation.11 | async-start | bytes 5242880 | tf_op jit(solution)/shard_map/reduce_scatter | solution.py:122
  602.6 205.8 %reduce-scatter.14.cloned.1.call-start = ((), (), s32[]{:S(2)}) async-start(), calls=%async_computation.16 | async-start | bytes 6488064 | tf_op jit(solution)/shard_map/reduce_scatter | solution.py:139
  613.2 542.7 %all-reduce.9.cloned.1.call-start = ((), (), s32[]{:S(2)}) async-start(), calls=%async_computation.17 | async-start | bytes 23068672
  661.0 706.9 %reduce-scatter.10.cloned.1.call-start = ((), (), s32[]{:S(2)}) async-start(), calls=%async_computation.14 | async-start | bytes 19464192 | tf_op jit(solution)/shard_map/reduce_scatter | solution.py:198
  664.2 33.0 %copy-start.9 = (f32[256,256]{0,1:T(8,128)}, f32[256,256]{0,1:T(8,128)S(1)}, u32[]{:S(2)}) copy-start(f32[256,256]{0,1:T(8,128)S(1)} %convert_multiply_fusion.5) | copy-start | bytes 786436
  697.2 9.3 copy-start.24
  723.5 12.3 copy-start.7
  735.8 992.0 %reduce-scatter.12.cloned.1.call-start = ((), (), s32[]{:S(2)}) async-start(), calls=%async_computation.15 | async-start | bytes 17301504 | tf_op jit(solution)/shard_map/reduce_scatter | solution.py:162
  752.2 6.2 copy-start.8
  (21 other events, 53.1 us)
Sparse Core Ops, SparseCore 0:
  11.1 56.5 all-gather.7
  70.7 76.2 all-gather.9
  150.0 75.8 all-gather.11
  228.5 162.2 all-gather.15
  392.8 32.6 all-gather.13
  427.5 34.4 all-gather.19
  464.2 92.6 all-gather.17
  591.5 42.6 reduce-scatter.7
  636.9 44.5 reduce-scatter.5
  685.0 111.5 reduce-scatter.13
  800.5 355.3 all-reduce.8
  1162.1 205.7 reduce-scatter.9
  1370.8 356.9 reduce-scatter.11
where the time goes:
time: 1750 us; the launch traced here: 1730 us
  waiting for transfers between devices  1380 us (79%)
  matrix products  166 us (9%)
  blocking collectives  84.7 us (5%)
  local copies, waits for them, and re-layouts  52.5 us (3%)
  other arithmetic  36.2 us (2%)
    reduce_scatter x1, waiting for transfers between devices, local(): lax.psum_scatter(contract_first(attn_low, d_mid_low), ('dp', 'fsdp'), sca...  357 us
    unnamed x14, waiting for transfers between devices  348 us
    reduce_scatter x1, waiting for transfers between devices, local(): lax.psum_scatter(contract_first(h_one, joined), ('dp', 'fsdp'), scatter_d...  207 us
    all_gather x1, waiting for transfers between devices, local(): gu_piece = lax.all_gather(w_gu, 'fsdp', axis=0, tiled=True)  152 us
    all_gather x1, waiting for transfers between devices, local(): down_piece = lax.all_gather(w_down, 'fsdp', axis=0, tiled=True)  94.9 us
    unnamed x2, blocking collectives  84.7 us
    all_gather x1, waiting for transfers between devices, local(): wq_piece = lax.all_gather(w_q, ('dp', 'fsdp'), axis=0, tiled=True)  76.8 us
    all_gather x1, waiting for transfers between devices, local(): lax.all_gather(w_o, ('dp', 'fsdp'), axis=0, tiled=True)  65.3 us
  transfers between devices with their start and end apart: 13, of which 11 were waited for; matrix products, arithmetic and copies ran while one was open for 12% of the time, Pallas kernels for 0%

commit v1 on v0

v1 whole, which is shorter than its diff:
```python
import jax
import jax.numpy as jnp
from jax import lax
from jax.sharding import PartitionSpec as P

epsilon = 1e-05
theta_base = 10000.0
bf16 = jnp.bfloat16
f32 = jnp.float32


def rope_tables(length, width):
    halfway = width // 2
    freqs = theta_base ** (-(jnp.arange(halfway, dtype=jnp.float32) * 2.0 / width))
    angles = jnp.arange(length, dtype=jnp.float32)[:, None] * freqs[None, :]
    return (jnp.cos(angles), jnp.sin(angles))


def rotate(vectors, cosines, sine_part):
    halfway = vectors.shape[-1] // 2
    front = vectors[..., :halfway]
    behind = vectors[..., halfway:]
    return jnp.concatenate(
        [front * cosines - behind * sine_part, behind * cosines + front * sine_part], axis=-1
    )


def contract_last(left, right):
    return lax.dot_general(
        left,
        right,
        (((left.ndim - 1,), (right.ndim - 1,)), ((), ())),
        preferred_element_type=jnp.float32,
    )


def contract_first(left, right):
    return lax.dot_general(
        left, right, (((0,), (0,)), ((), ())), preferred_element_type=jnp.float32
    )


class Grid:
    def __init__(self, dp, fsdp):
        self.dp, self.fsdp = dp, fsdp
        self.depth = fsdp // 2
        self.groups = [[f for f in range(fsdp) if f % 2 == y] for y in range(2)]
        self.dp_index = lax.axis_index("dp")
        self.fsdp_index = lax.axis_index("fsdp")
        self.y = self.fsdp_index % 2

    def core(self, value):
        return lax.ppermute(value, "dp", [(i, i ^ 1) for i in range(self.dp)])

    def x_swap(self, value):
        return lax.ppermute(value, "dp", [(i, i ^ 2) for i in range(self.dp)])

    def y_swap(self, value):
        return lax.ppermute(value, "fsdp", [(i, i ^ 1) for i in range(self.fsdp)])

    def gather_outer(self, value):
        return lax.all_gather(
            value, "fsdp", axis=0, tiled=True, axis_index_groups=self.groups
        )

    def scatter_outer(self, value):
        return lax.psum_scatter(
            value, "fsdp", scatter_dimension=0, tiled=True, axis_index_groups=self.groups
        )

    def spread(self, first, second):
        first_x = self.x_swap(first)
        second_y = self.y_swap(second)
        first_y = self.y_swap(first)
        second_x = self.x_swap(second)
        first_xy = self.y_swap(first_x)
        second_xy = self.x_swap(second_y)
        return {
            (0, 0): (first, second),
            (1, 0): (first_x, second_x),
            (0, 1): (first_y, second_y),
            (1, 1): (first_xy, second_xy),
        }

    def collect(self, parts):
        first_xy = self.y_swap(parts[1, 1][0])
        second_xy = self.x_swap(parts[1, 1][1])
        first_y = self.y_swap(parts[0, 1][0])
        second_x = self.x_swap(parts[1, 0][1])
        wide = lambda *terms: sum(term.astype(f32) for term in terms)
        first_x = self.x_swap(wide(parts[1, 0][0], first_xy).astype(bf16))
        second_y = self.y_swap(wide(parts[0, 1][1], second_xy).astype(bf16))
        return (
            wide(parts[0, 0][0], first_y, first_x),
            wide(parts[0, 0][1], second_x, second_y),
        )

    def assemble(self, shard):
        rows, columns = shard.shape
        column = self.gather_outer(shard).reshape(self.depth, rows, columns)
        cut = self.depth // 2
        pieces = self.spread(column[:cut], column[cut:])
        whole = jnp.zeros((self.dp, self.depth, 2, rows, columns), shard.dtype)
        for flip in range(2):
            for (dx, dy), halves in pieces.items():
                for place, half in ((0, halves[0]), (cut, halves[1])):
                    if flip:
                        half = self.core(half)
                    whole = lax.dynamic_update_slice(
                        whole,
                        half[None, :, None],
                        (self.dp_index ^ (2 * dx + flip), place, self.y ^ dy, 0, 0),
                    )
        return whole.reshape(self.dp * self.depth * 2 * rows, columns)

    def relative_order(self, total):
        rows = total // (self.dp * self.fsdp)
        place = jnp.arange(total, dtype=jnp.int32)
        row = place % rows
        rest = place // rows
        outer = rest % self.depth
        rest = rest // self.depth
        dy, dx, flip = rest % 2, (rest // 2) % 2, rest // 4
        source = (
            ((self.dp_index ^ (2 * dx + flip)) * self.depth + outer) * 2 + (self.y ^ dy)
        ) * rows + row
        return (place[:, None] == source[None, :]).astype(bf16)

    def reduce_rows(self, kept, received, rows):
        columns = kept.shape[1]
        cut = self.depth // 2
        shape = (2, 2, self.depth, rows, columns)
        mine, theirs = kept.reshape(shape), received.reshape(shape)

        def part(dx, dy, low, high):
            both = mine[dx, dy, low:high].astype(f32) + theirs[dx, dy, low:high].astype(f32)
            return both.astype(bf16)

        parts = {
            (dx, dy): (part(dx, dy, 0, cut), part(dx, dy, cut, self.depth))
            for dx in range(2)
            for dy in range(2)
        }
        first, second = self.collect(parts)
        column = jnp.concatenate([first, second], axis=0).astype(bf16)
        return self.scatter_outer(column.reshape(self.depth * rows, columns)).astype(f32)


def local(
    tokens,
    w_q,
    w_kv,
    g_attn,
    g_mlp,
    w_o,
    w_gu,
    w_down,
    grad_out,
    grad_kv,
    group_id,
    group_size,
    group_weight,
):
    grid = Grid(lax.axis_size("dp"), lax.axis_size("fsdp"))
    length, width = tokens.shape
    head_dim = grad_kv.shape[1] // 2
    q_width = w_q.shape[1]
    kv_width = w_kv.shape[1]
    shard_rows = w_q.shape[0]
    head_count = q_width // head_dim
    hidden_rows = w_down.shape[0]
    half = length // 2
    lanes = 128

    gains = jnp.stack([g_attn, g_mlp], axis=1)
    w_in = jnp.concatenate(
        [w_q, w_kv, jnp.pad(gains, ((0, 0), (0, lanes - 2)))], axis=1
    )
    w_in_all = grid.assemble(w_in)
    w_o_all = grid.assemble(w_o)
    gu_mine = grid.gather_outer(w_gu)
    down_mine = grid.gather_outer(w_down)
    gu_other = grid.core(gu_mine)
    down_other = grid.core(down_mine)

    matches = jnp.arange(group_size.shape[0], dtype=jnp.int32) == group_id[0]
    factor = jnp.sum(jnp.where(matches, group_weight / group_size.astype(jnp.float32), 0.0))
    grad_top = grad_out.astype(jnp.float32) * factor
    grad_low = grad_top.astype(jnp.bfloat16)

    def rows_of_plane(value):
        pieces = grid.spread(value[:half], value[half:])
        return jnp.concatenate(
            [piece for key in ((0, 0), (1, 0), (0, 1), (1, 1)) for piece in pieces[key]], axis=0
        )

    def sum_of_plane(partial):
        parts = {}
        for place, key in enumerate(((0, 0), (1, 0), (0, 1), (1, 1))):
            start = place * length
            parts[key] = (partial[start : start + half], partial[start + half : start + length])
        return jnp.concatenate(grid.collect(parts), axis=0)

    grad_rows = rows_of_plane(grad_low)
    order = grid.relative_order(width)
    order_o = order if q_width == width else grid.relative_order(q_width)

    cosines, sine_part = rope_tables(length, head_dim)
    x_full = tokens.astype(jnp.float32)
    inv_one = lax.rsqrt(jnp.mean(x_full * x_full, axis=-1, keepdims=True) + epsilon)
    normed_one = x_full * inv_one
    pick = (jnp.arange(8)[:, None] == jnp.arange(lanes)[None, :]).astype(bf16)
    gain_rows = contract_last(pick, w_in_all[:, q_width + kv_width :])
    gain_one, gain_two = gain_rows[0], gain_rows[1]
    h_one = (normed_one * gain_one).astype(jnp.bfloat16)
    wq_all = w_in_all[:, :q_width]
    wkv_all = w_in_all[:, q_width : q_width + kv_width]
    q_pre = jnp.dot(h_one, wq_all, preferred_element_type=jnp.float32)
    kv_pre = jnp.dot(h_one, wkv_all, preferred_element_type=jnp.float32)
    q_low = rotate(
        q_pre.reshape(length, head_count, head_dim), cosines[:, None, :], sine_part[:, None, :]
    ).astype(jnp.bfloat16)
    k_low = rotate(kv_pre[:, :head_dim], cosines, sine_part).astype(jnp.bfloat16)
    v_low = kv_pre[:, head_dim:].astype(jnp.bfloat16)
    score_scale = head_dim ** (-0.5)
    causal = jnp.arange(length)[:, None] >= jnp.arange(length)[None, :]

    def logits_of(queries, keys):
        raw_scores = jnp.einsum("thd,sd->hts", queries, keys, preferred_element_type=jnp.float32)
        return jnp.where(causal[None], raw_scores * score_scale, -1e30)

    logits = logits_of(q_low, k_low)
    row_top = jnp.max(logits, axis=-1, keepdims=True)
    exp_vals = jnp.exp(logits - row_top)
    row_total = jnp.sum(exp_vals, axis=-1, keepdims=True)
    prob_full = exp_vals / row_total
    log_total = row_top + jnp.log(row_total)
    prob_low = prob_full.astype(jnp.bfloat16)
    attended = jnp.einsum("hts,sd->thd", prob_low, v_low, preferred_element_type=jnp.float32)
    attn_low = attended.reshape(length, q_width).astype(jnp.bfloat16)
    branch = jnp.dot(attn_low, w_o_all, preferred_element_type=jnp.float32)
    x_mid = x_full + branch
    inv_two = lax.rsqrt(jnp.mean(x_mid * x_mid, axis=-1, keepdims=True) + epsilon)
    normed_two = x_mid * inv_two
    h_two = (normed_two * gain_two).astype(jnp.bfloat16)

    ff_rows = rows_of_plane(h_two)
    mlp_out = 0.0
    d_h_two = 0.0
    kept = []
    for gu_piece, down_piece in ((gu_mine, down_mine), (gu_other, down_other)):
        both_proj = jnp.einsum(
            "td,fkd->tkf", ff_rows, gu_piece, preferred_element_type=jnp.float32
        )
        gate_vals = both_proj[:, 0]
        up_vals = both_proj[:, 1]
        hid_cols = (jax.nn.silu(gate_vals) * up_vals).astype(jnp.bfloat16)
        mlp_out = mlp_out + jnp.dot(hid_cols, down_piece, preferred_element_type=jnp.float32)
        d_hid = contract_last(grad_rows, down_piece)
        sigmoid_vals = jax.nn.sigmoid(gate_vals)
        d_gate = d_hid * up_vals * sigmoid_vals * (1.0 + gate_vals * (1.0 - sigmoid_vals))
        d_up = d_hid * gate_vals * sigmoid_vals
        d_both = jnp.stack([d_gate, d_up], axis=1).astype(jnp.bfloat16)
        d_h_two = d_h_two + jnp.einsum(
            "tkf,fkd->td", d_both, gu_piece, preferred_element_type=jnp.float32
        )
        kept.append((hid_cols, d_both[:, 0], d_both[:, 1]))
    d_h_two = sum_of_plane(d_h_two.astype(bf16))
    mlp_out = sum_of_plane(mlp_out.astype(bf16))

    def weight_sum(index, rows):
        theirs = contract_first(kept[1][index], rows).astype(bf16)
        arrived = grid.core(theirs)
        mine = contract_first(kept[0][index], rows)
        return grid.scatter_outer((mine + arrived.astype(f32)).astype(bf16)).astype(f32)

    d_w_down = weight_sum(0, grad_rows)
    d_w_gate = weight_sum(1, ff_rows)
    d_w_up = weight_sum(2, ff_rows)
    d_w_gu = jnp.stack([d_w_gate, d_w_up], axis=1)

    output = (x_mid + mlp_out).astype(jnp.bfloat16)
    d_gain_two = jnp.sum(d_h_two * normed_two, axis=0)
    d_normed_two = d_h_two * gain_two
    d_mid = grad_top + inv_two * (
        d_normed_two - normed_two * jnp.mean(d_normed_two * normed_two, axis=-1, keepdims=True)
    )
    d_mid_low = d_mid.astype(jnp.bfloat16)
    d_attended = contract_last(d_mid_low, w_o_all)
    d_att_low = d_attended.astype(jnp.bfloat16).reshape(length, head_count, head_dim)

    def row_sums(left, right, extra, matrix):
        moved = jnp.dot(left, matrix, preferred_element_type=jnp.float32).astype(bf16)
        middle = left.shape[1] // 2
        halves = []
        for low in (middle, 0):
            block = contract_first(moved[:, low : low + middle], right).astype(bf16)
            if extra is not None:
                columns = contract_first(matrix[:, low : low + middle], extra).astype(bf16)
                block = jnp.concatenate([block, columns], axis=1)
            halves.append(block)
        return grid.reduce_rows(halves[1], grid.core(halves[0]), shard_rows)

    d_w_o = row_sums(attn_low, d_mid_low, None, order_o)
    prob_back = jnp.exp(logits_of(q_low, k_low) - log_total)
    prob_back_low = prob_back.astype(jnp.bfloat16)
    d_probs = jnp.einsum("thd,sd->hts", d_att_low, v_low, preferred_element_type=jnp.float32)
    d_v_own = jnp.einsum(
        "hts,thd->sd", prob_back_low, d_att_low, preferred_element_type=jnp.float32
    )
    d_logit = prob_back * (d_probs - jnp.sum(prob_back * d_probs, axis=-1, keepdims=True))
    d_raw = (d_logit * score_scale).astype(jnp.bfloat16)
    d_q_rot = jnp.einsum("hts,sd->thd", d_raw, k_low, preferred_element_type=jnp.float32)
    d_k_own = jnp.einsum("hts,thd->sd", d_raw, q_low, preferred_element_type=jnp.float32)
    kv_extra = grad_kv.astype(jnp.float32) * factor
    d_k_total = d_k_own + kv_extra[:, :head_dim]
    d_v_total = d_v_own + kv_extra[:, head_dim:]
    d_kv = jnp.concatenate([d_k_total, d_v_total], axis=1)
    d_kv_low = jnp.concatenate([rotate(d_k_total, cosines, -sine_part), d_v_total], axis=1).astype(
        jnp.bfloat16
    )
    d_q_low = (
        rotate(d_q_rot, cosines[:, None, :], -sine_part[:, None, :])
        .reshape(length, q_width)
        .astype(jnp.bfloat16)
    )
    d_h_one = contract_last(d_q_low, wq_all) + contract_last(d_kv_low, wkv_all)
    d_normed = d_h_one * gain_one
    d_gain = jnp.sum(d_h_one * normed_one, axis=0)
    d_tokens = d_mid + inv_one * (
        d_normed - normed_one * jnp.mean(d_normed * normed_one, axis=-1, keepdims=True)
    )
    joined = jnp.concatenate([d_q_low, d_kv_low], axis=1)
    gain_sums = jnp.pad(jnp.stack([d_gain, d_gain_two], axis=1), ((0, 0), (0, lanes - 2)))
    d_w_in = row_sums(h_one, joined, gain_sums.astype(bf16), order)
    kv_out = jnp.concatenate([k_low, v_low], axis=1)
    return (
        output,
        d_tokens,
        kv_out,
        d_kv,
        d_w_in[:, :q_width],
        d_w_in[:, q_width : q_width + kv_width],
        d_w_in[:, q_width + kv_width],
        d_w_in[:, q_width + kv_width + 1],
        d_w_o,
        d_w_gu,
        d_w_down,
    )


def solution(mesh):
    placed = (
        P(("dp", "fsdp"), None),
        P(("dp", "fsdp"), None),
        P(("dp", "fsdp"), None),
        P(("dp", "fsdp")),
        P(("dp", "fsdp")),
        P(("dp", "fsdp"), None),
        P(("dp", "fsdp"), None, None),
        P(("dp", "fsdp"), None),
        P(("dp", "fsdp"), None),
        P(("dp", "fsdp"), None),
        P(("dp", "fsdp")),
        P(),
        P(),
    )
    return jax.shard_map(
        local,
        mesh=mesh,
        in_specs=placed,
        out_specs=(
            P(("dp", "fsdp"), None),
            P(("dp", "fsdp"), None),
            P(("dp", "fsdp"), None),
            P(("dp", "fsdp"), None),
            P(("dp", "fsdp"), None),
            P(("dp", "fsdp"), None),
            P(("dp", "fsdp")),
            P(("dp", "fsdp")),
            P(("dp", "fsdp"), None),
            P(("dp", "fsdp"), None, None),
            P(("dp", "fsdp"), None),
        ),
        check_vma=False,
    )
```

time: 1750 us -> 665 us (0.38)
  waiting for transfers between devices: 1380 us -> 251 us
  blocking collectives: 84.7 us -> 0 us
  starting transfers between devices: 1.51 us -> 61.8 us
  other arithmetic: 36.2 us -> 71.6 us
  local copies, waits for them, and re-layouts: 52.5 us -> 73.4 us
    reduce_scatter x5, waiting for transfers between devices: 577 us -> 12.9 us  [scatter_outer(): lax.psum_scatter(value, 'fsdp', scatter_dimension=0, tiled=True, axis_ind...]
    all_gather x7 -> x4, waiting for transfers between devices: 453 us -> 28.6 us  [gather_outer(): lax.all_gather(value, 'fsdp', axis=0, tiled=True, axis_index_groups=self....]
    unnamed x14 -> x9, waiting for transfers between devices: 348 us -> 0.81 us
    ppermute x0 -> x71, waiting for transfers between devices: none -> 208 us  [the longest x24 111 us: y_swap(): return lax.ppermute(value, 'fsdp', [(i, i ^ 1) for i in range(self.fsdp)])]
    unnamed x2 -> x0, blocking collectives: 84.7 us -> none
    ppermute x0 -> x71, starting transfers between devices: none -> 60.9 us  [the longest x24 28.9 us: y_swap(): return lax.ppermute(value, 'fsdp', [(i, i ^ 1) for i in range(self.fsdp)])]
    convert_element_type x1 -> x0, local copies, waits for them, and re-layouts: 29.4 us -> none  [local(): jnp.einsum('tkf,td->fkd', d_both, ff_rows, preferred_element_type=jnp.flo...]
    dynamic_update_slice x0 -> x32, local copies, waits for them, and re-layouts: none -> 17.9 us  [assemble(): lax.dynamic_update_slice(whole, half[None, :, None], (self.dp_index ^ 2 *...]
  transfers between devices with their start and end apart: 13 -> 80, of which waited for: 11 -> 33; matrix products, arithmetic and copies ran while one was open for 12% -> 45% of each run, Pallas kernels for 0% -> 0%
where the time goes in v1:
time: 665 us; the launch traced here: 653 us
  waiting for transfers between devices  251 us (38%)
  matrix products  180 us (27%)
  local copies, waits for them, and re-layouts  73.4 us (11%)
  other arithmetic  71.6 us (11%)
  starting transfers between devices  61.8 us (9%)
  between operations  16.1 us (2%)
    ppermute x24, waiting for transfers between devices, y_swap(): return lax.ppermute(value, 'fsdp', [(i, i ^ 1) for i in range(self.fsdp)])  111 us
    ppermute x24, waiting for transfers between devices, x_swap(): return lax.ppermute(value, 'dp', [(i, i ^ 2) for i in range(self.dp)])  94.5 us
    dot_general x12, matrix products, contract_first(): lax.dot_general(left, right, (((0,), (0,)), ((), ())), preferred_element_...  45.5 us
    ppermute x24, starting transfers between devices, y_swap(): return lax.ppermute(value, 'fsdp', [(i, i ^ 1) for i in range(self.fsdp)])  28.9 us
    all_gather x4, waiting for transfers between devices, gather_outer(): lax.all_gather(value, 'fsdp', axis=0, tiled=True, axis_index_groups=self....  28.6 us
    ppermute x24, starting transfers between devices, x_swap(): return lax.ppermute(value, 'dp', [(i, i ^ 2) for i in range(self.dp)])  28.6 us
    unnamed x151, local copies, waits for them, and re-layouts  27.6 us
    dot_general x6, matrix products, contract_last(): lax.dot_general(left, right, (((left.ndim - 1,), (right.ndim - 1,)), ((),...  26.9 us
  transfers between devices with their start and end apart: 80, of which 33 were waited for; matrix products, arithmetic and copies ran while one was open for 45% of the time, Pallas kernels for 0%

profile of v1, /device:TPU:0, one launch (start us, length us, event | category | flops | bytes accessed | tf_op | source)
XLA Modules:
  0.0 653.4 jit_solution(16272638687089018653)
XLA Ops:
  35.9 11.2 %collective-permute-done.45 = bf16[128,2048]{1,0:T(8,128)(2,1)S(1)} collective-permute-done((bf16[128,2048]{1,0:T(8,128)(2,1)}, bf16[128,2048]{1,0:T(8,128)(2,1)S(1)}, u32[]{:S(2)}, u32[]{:S(2)}) %collective-permute-start.45) | collective-permute-done | bytes 524320 | tf_op jit(solution)/shard_map/ppermute | solution.py:59
  92.0 8.7 %collective-permute-done = bf16[2,64,2432]{2,1,0:T(8,128)(2,1)S(1)} collective-permute-done((bf16[2,64,2432]{2,1,0:T(8,128)(2,1)S(1)}, bf16[2,64,2432]{2,1,0:T(8,128)(2,1)S(1)}, u32[]{:S(2)}, u32[]{:S(2)}) %collective-permute-start) | collective-permute-done | bytes 622624 | tf_op jit(solution)/shard_map/ppermute | solution.py:56
  102.3 8.2 %collective-permute-done.1 = bf16[2,64,2432]{2,1,0:T(8,128)(2,1)S(1)} collective-permute-done((bf16[2,64,2432]{2,1,0:T(8,128)(2,1)S(1)}, bf16[2,64,2432]{2,1,0:T(8,128)(2,1)S(1)}, u32[]{:S(2)}, u32[]{:S(2)}) %collective-permute-start.1) | collective-permute-done | bytes 622624 | tf_op jit(solution)/shard_map/ppermute | solution.py:56
  113.3 11.7 %collective-permute-done.18 = bf16[2,64,2048]{2,1,0:T(8,128)(2,1)S(1)} collective-permute-done((bf16[2,64,2048]{2,1,0:T(8,128)(2,1)S(1)}, bf16[2,64,2048]{2,1,0:T(8,128)(2,1)S(1)}, u32[]{:S(2)}, u32[]{:S(2)}) %collective-permute-start.18) | collective-permute-done | bytes 524320 | tf_op jit(solution)/shard_map/ppermute | solution.py:59
  136.0 12.1 %collective-permute-done.4 = bf16[2,64,2432]{2,1,0:T(8,128)(2,1)S(1)} collective-permute-done((bf16[2,64,2432]{2,1,0:T(8,128)(2,1)S(1)}, bf16[2,64,2432]{2,1,0:T(8,128)(2,1)S(1)}, u32[]{:S(2)}, u32[]{:S(2)}) %collective-permute-start.4) | collective-permute-done | bytes 622624 | tf_op jit(solution)/shard_map/ppermute | solution.py:59
  183.7 15.1 %fusion.35 = bf16[256,2048]{1,0:T(8,128)(2,1)} fusion(s32[2048]{0:T(1024)S(1)} %fusion.147, bf16[256,2048]{1,0:T(8,128)(2,1)S(1)} %copy-done.4, f32[2048]{0:T(1024)S(1)} %bitcast.377, f32[256]{0:T(256)S(1)} %copy-done.47), kind=kOutput, calls=%fused_computation.71 | convolution fusion | flops 2154299392 | bytes 2114560 | tf_op jit(solution)/shard_map/dot_general | solution.py:293
  214.8 25.6 %all-gather.11.cloned.1.call-done = bf16[704,2048]{1,0:T(8,128)(2,1)} async-done(((bf16[176,2048]{1,0:T(8,128)(2,1)}), bf16[704,2048]{1,0:T(8,128)(2,1)}) %all-gather.11.cloned.1.call-update) | async-done | bytes 2883600 | tf_op jit(solution)/shard_map/all_gather | solution.py:62
  244.2 9.6 %fusion.37 = f32[1024,2,704]{0,2,1:T(8,128)S(1)} fusion(bf16[704,2,2048]{2,0,1:T(8,128)(2,1)} %all-gather.9.cloned.1.call-done, bf16[1024,2048]{1,0:T(8,128)(2,1)} %constant_dynamic-update-slice_fusion), kind=kOutput, calls=%fused_computation.74 | convolution fusion | flops 5905580032 | bytes 15728640 | tf_op jit(solution)/shard_map/td,fkd->tkf/dot_general | solution.py:252
  264.1 9.3 %fusion.25 = f32[1024,2048,1]{1,0,2:T(8,128)} fusion(bf16[704,2,2048]{2,0,1:T(8,128)(2,1)S(1)} %bitcast.381, bf16[1024,1,704]{0,2,1:T(8,128)(2,1)S(1)} %bitcast.385, bf16[1024,1,704]{0,2,1:T(8,128)(2,1)S(1)} %bitcast.384), kind=kOutput, calls=%fused_computation.55 | convolution fusion | flops 5907021824 | bytes 17039360 | tf_op jit(solution)/shard_map/tkf,fkd->td/dot_general | solution.py:264
  273.4 8.6 %fusion.40 = f32[1024,2,704]{0,2,1:T(8,128)S(1)} fusion(bf16[704,2,2048]{2,0,1:T(8,128)(2,1)} %collective-permute-done.34, bf16[1024,2048]{1,0:T(8,128)(2,1)S(1)} %copy-done.29), kind=kOutput, calls=%fused_computation.75 | convolution fusion | flops 5905580032 | bytes 15728640 | tf_op jit(solution)/shard_map/td,fkd->tkf/dot_general | solution.py:252
  290.9 11.0 %fusion.3 = bf16[1024,2048]{1,0:T(8,128)(2,1)S(1)} fusion(f32[1024,2048,1]{1,0,2:T(8,128)} %fusion.25, bf16[704,2,2048]{2,0,1:T(8,128)(2,1)} %collective-permute-done.34, bf16[1024,1,704]{0,2,1:T(8,128)(2,1)S(1)} %bitcast.387, bf16[1024,1,704]{0,2,1:T(8,128)(2,1)S(1)} %bitcast.386), kind=kOutput, calls=%fused_computation.5 | convolution fusion | flops 5911216128 | bytes 21233664 | tf_op jit(solution)/shard_map/tkf,fkd->td/dot_general | solution.py:264
  342.5 19.9 %collective-permute-done.50 = bf16[128,2048]{1,0:T(8,128)(2,1)} collective-permute-done((bf16[128,2048]{1,0:T(8,128)(2,1)}, bf16[128,2048]{1,0:T(8,128)(2,1)}, u32[]{:S(2)}, u32[]{:S(2)}) %collective-permute-start.50) | collective-permute-done | bytes 524320 | tf_op jit(solution)/shard_map/ppermute | solution.py:56
  366.0 7.4 %collective-permute-done.40 = bf16[128,2048]{1,0:T(8,128)(2,1)S(1)} collective-permute-done((bf16[128,2048]{1,0:T(8,128)(2,1)}, bf16[128,2048]{1,0:T(8,128)(2,1)S(1)}, u32[]{:S(2)}, u32[]{:S(2)}) %collective-permute-start.40) | collective-permute-done | bytes 524320 | tf_op jit(solution)/shard_map/ppermute | solution.py:56
  373.5 21.4 %collective-permute-done.38 = bf16[128,2048]{1,0:T(8,128)(2,1)S(1)} collective-permute-done((bf16[128,2048]{1,0:T(8,128)(2,1)}, bf16[128,2048]{1,0:T(8,128)(2,1)S(1)}, u32[]{:S(2)}, u32[]{:S(2)}) %collective-permute-start.38) | collective-permute-done | bytes 524320 | tf_op jit(solution)/shard_map/ppermute | solution.py:56
  398.8 11.0 %collective-permute-done.53 = bf16[128,2048]{1,0:T(8,128)(2,1)S(1)} collective-permute-done((bf16[128,2048]{1,0:T(8,128)(2,1)S(1)}, bf16[128,2048]{1,0:T(8,128)(2,1)S(1)}, u32[]{:S(2)}, u32[]{:S(2)}) %collective-permute-start.53) | collective-permute-done | bytes 524320 | tf_op jit(solution)/shard_map/ppermute | solution.py:59
  437.4 9.4 %fusion.59 = f32[256,16,128]{2,0,1:T(8,128)} fusion(f32[256,256,16]{1,0,2:T(8,128)} %fusion.126, f32[16,256,256]{1,2,0:T(8,128)} %copy-done, f32[16,256]{1,0:T(8,128)S(1)} %copy-done.38, bf16[256,64]{0,1:T(8,128)(2,1)S(1)} %get-tuple-element.97, bf16[256,64]{0,1:T(8,128)(2,1)S(1)} %get-tuple-element.98), kind=kOutput, calls=%fused_computation.103 | convolution fusion | flops 275910912 | bytes 10567680 | tf_op jit(solution)/shard_map/hts,sd->thd/dot_general | solution.py:313
  453.6 8.3 %add_convert_fusion.3 = bf16[704,2048]{1,0:T(8,128)(2,1)} fusion(bf16[704,2048]{1,0:T(8,128)(2,1)} %collective-permute-done.68, bf16[1024,704]{0,1:T(8,128)(2,1)} %copy-done.57, bf16[1024,2048]{1,0:T(8,128)(2,1)} %constant_dynamic-update-slice_fusion), kind=kOutput, calls=%fused_computation.17 | convolution fusion | flops 2957115392 | bytes 11403264 | tf_op jit(solution)/shard_map/dot_general | solution.py:38
  466.7 8.9 %fusion.76 = f32[256,128]{0,1:T(8,128)S(1)} fusion(f32[256,256,16]{1,0,2:T(8,128)} %fusion.126, f32[16,256,256]{1,2,0:T(8,128)} %copy-done, f32[16,256]{1,0:T(8,128)S(1)} %copy-done.38, bf16[256,16,64]{2,0,1:T(8,128)(2,1)} %copy-done.6, bf16[256,16,64]{2,0,1:T(8,128)(2,1)} %copy-done.5, f32[256,256]{0,1:T(8,128)S(1)} %copy-done.15), kind=kOutput, calls=%fused_computation.131 | convolution fusion | flops 277909760 | bytes 19169280 | tf_op jit(solution)/shard_map/hts,thd->sd/dot_general | solution.py:314
  482.6 8.3 %fusion.48 = (bf16[2048]{0:T(1024)(128)(2,1)S(1)}, f32[256]{0:T(256)}, f32[256,2048]{1,0:T(8,128)}) fusion(bf16[256,2048]{1,0:T(8,128)(2,1)S(1)} %copy-done.4, f32[256]{0:T(256)S(1)} %copy-done.48, f32[2048]{0:T(1024)S(1)} %bitcast.378, f32[256,2048]{1,0:T(8,128)S(1)} %fusion.88, bf16[256,2048]{0,1:T(8,128)(2,1)S(1)} %bitcast.367, ...), kind=kOutput, calls=%fused_computation.81 | convolution fusion | flops 2151675648 | bytes 14694400 | tf_op jit(solution)/shard_map/dot_general | solution.py:29
  517.4 9.2 %collective-permute-done.63 = bf16[2,64,2048]{2,1,0:T(8,128)(2,1)S(1)} collective-permute-done((bf16[2,64,2048]{2,1,0:T(8,128)(2,1)S(1)}, bf16[2,64,2048]{2,1,0:T(8,128)(2,1)S(1)}, u32[]{:S(2)}, u32[]{:S(2)}) %collective-permute-start.63) | collective-permute-done | bytes 524320 | tf_op jit(solution)/shard_map/ppermute | solution.py:59
  556.4 18.9 %collective-permute-done.67 = bf16[2,64,2048]{2,1,0:T(8,128)(2,1)S(1)} collective-permute-done((bf16[2,64,2048]{2,1,0:T(8,128)(2,1)S(1)}, bf16[2,64,2048]{2,1,0:T(8,128)(2,1)S(1)}, u32[]{:S(2)}, u32[]{:S(2)}) %collective-permute-start.67) | collective-permute-done | bytes 524320 | tf_op jit(solution)/shard_map/ppermute | solution.py:59
  578.1 14.3 %collective-permute-done.57 = bf16[2,64,2432]{2,1,0:T(8,128)(2,1)} collective-permute-done((bf16[2,64,2432]{2,1,0:T(8,128)(2,1)}, bf16[2,64,2432]{2,1,0:T(8,128)(2,1)}, u32[]{:S(2)}, u32[]{:S(2)}) %collective-permute-start.57) | collective-permute-done | bytes 622624 | tf_op jit(solution)/shard_map/ppermute | solution.py:56
  596.6 12.9 %collective-permute-done.60 = bf16[2,64,2432]{2,1,0:T(8,128)(2,1)S(1)} collective-permute-done((bf16[2,64,2432]{2,1,0:T(8,128)(2,1)S(1)}, bf16[2,64,2432]{2,1,0:T(8,128)(2,1)S(1)}, u32[]{:S(2)}, u32[]{:S(2)}) %collective-permute-start.60) | collective-permute-done | bytes 622624 | tf_op jit(solution)/shard_map/ppermute | solution.py:59
  628.9 12.9 %reduce-scatter.6.cloned.1.call-done = bf16[64,2432]{1,0:T(8,128)(2,1)} async-done(((bf16[256,2432]{1,0:T(8,128)(2,1)}), bf16[64,2432]{1,0:T(8,128)(2,1)}) %reduce-scatter.6.cloned.1.call-update) | async-done | bytes 311312 | tf_op jit(solution)/shard_map/reduce_scatter | solution.py:67
  (436 shorter events, 343.6 us)
Async XLA Ops:
  7.2 51.8 %all-gather.7.cloned.1.call-start = ((), (), s32[]{:S(2)}) async-start(), calls=%async_computation.6 | async-start | bytes 1310720 | tf_op jit(solution)/shard_map/all_gather | solution.py:62
  7.9 65.6 %all-gather.5.cloned.1.call-start = ((), (), s32[]{:S(2)}) async-start(), calls=%async_computation.5 | async-start | bytes 1556480 | tf_op jit(solution)/shard_map/all_gather | solution.py:62
  10.5 202.4 %all-gather.9.cloned.1.call-start = ((), (), s32[]{:S(2)}) async-start(), calls=%async_computation.7 | async-start | bytes 7208960 | tf_op jit(solution)/shard_map/all_gather | solution.py:62
  13.6 226.8 %all-gather.11.cloned.1.call-start = ((), (), s32[]{:S(2)}) async-start(), calls=%async_computation.8 | async-start | bytes 3604480 | tf_op jit(solution)/shard_map/all_gather | solution.py:62
  22.9 596.5 %reduce-scatter.12.cloned.1.call-start = ((), (), s32[]{:S(2)}) async-start(), calls=%async_computation.12 | async-start | bytes 3604480 | tf_op jit(solution)/shard_map/reduce_scatter | solution.py:67
  64.4 63.1 %collective-permute-start.20 = (bf16[2,64,2048]{2,1,0:T(8,128)(2,1)S(1)}, bf16[2,64,2048]{2,1,0:T(8,128)(2,1)}, u32[]{:S(2)}, u32[]{:S(2)}) collective-permute-start(bf16[2,64,2048]{2,1,0:T(8,128)(2,1)S(1)} %bitcast.363), channel_id=1, source_target_pairs={{0,8},{8,0},{16,24},{24,16},{1,9},{9,1},{17,25},{25,17},{2,10},{10... | collective-permute-start | bytes 1572872 | tf_op jit(solution)/shard_map/ppermute | solution.py:53
  76.2 53.7 %collective-permute-start.21 = (bf16[2,64,2048]{2,1,0:T(8,128)(2,1)S(1)}, bf16[2,64,2048]{2,1,0:T(8,128)(2,1)S(1)}, u32[]{:S(2)}, u32[]{:S(2)}) collective-permute-start(bf16[2,64,2048]{2,1,0:T(8,128)(2,1)S(1)} %bitcast.360), channel_id=1, source_target_pairs={{0,8},{8,0},{16,24},{24,16},{1,9},{9,1},{17,25},{25,17},{2,10},{10... | collective-permute-start | bytes 1572872 | tf_op jit(solution)/shard_map/ppermute | solution.py:53
  110.5 39.5 %collective-permute-start.6 = (bf16[2,64,2432]{2,1,0:T(8,128)(2,1)S(1)}, bf16[2,64,2432]{2,1,0:T(8,128)(2,1)S(1)}, u32[]{:S(2)}, u32[]{:S(2)}) collective-permute-start(bf16[2,64,2432]{2,1,0:T(8,128)(2,1)S(1)} %bitcast.356), channel_id=1, source_target_pairs={{0,8},{8,0},{16,24},{24,16},{1,9},{9,1},{17,25},{25,17},{2,10},{10... | collective-permute-start | bytes 1867784 | tf_op jit(solution)/shard_map/ppermute | solution.py:53
  205.5 36.8 %collective-permute-start.33 = (bf16[128,2048]{1,0:T(8,128)(2,1)}, bf16[128,2048]{1,0:T(8,128)(2,1)}, u32[]{:S(2)}, u32[]{:S(2)}) collective-permute-start(bf16[128,2048]{1,0:T(8,128)(2,1)} %collective-permute-done.31), channel_id=1, source_target_pairs={{0,16},{8,24},{16,0},{24,8},{1,17},{9,25},{17,1},{25,9},{2,18},{10... | collective-permute-start | bytes 1572872 | tf_op jit(solution)/shard_map/ppermute | solution.py:56
  212.9 60.5 %collective-permute-start.34 = (bf16[704,2,2048]{2,0,1:T(8,128)(2,1)}, bf16[704,2,2048]{2,0,1:T(8,128)(2,1)}, u32[]{:S(2)}, u32[]{:S(2)}) collective-permute-start(bf16[704,2,2048]{2,0,1:T(8,128)(2,1)} %all-gather.9.cloned.1.call-done), channel_id=1, source_target_pairs={{0,8},{8,0},{16,24},{24,16},{1,9},{9,1},{17,25},{25,17},{2,10},{10... | collective-permute-start | bytes 17301512 | tf_op jit(solution)/shard_map/ppermute | solution.py:53
  240.4 41.6 %collective-permute-start.35 = (bf16[704,2048]{1,0:T(8,128)(2,1)}, bf16[704,2048]{1,0:T(8,128)(2,1)S(1)}, u32[]{:S(2)}, u32[]{:S(2)}) collective-permute-start(bf16[704,2048]{1,0:T(8,128)(2,1)} %all-gather.11.cloned.1.call-done), channel_id=1, source_target_pairs={{0,8},{8,0},{16,24},{24,16},{1,9},{9,1},{17,25},{25,17},{2,10},{10... | collective-permute-start | bytes 8650760 | tf_op jit(solution)/shard_map/ppermute | solution.py:53
  326.2 71.9 %collective-permute-start.51 = (bf16[128,2048]{1,0:T(8,128)(2,1)}, bf16[128,2048]{1,0:T(8,128)(2,1)}, u32[]{:S(2)}, u32[]{:S(2)}) collective-permute-start(bf16[128,2048]{1,0:T(8,128)(2,1)} %get-tuple-element.67), channel_id=1, source_target_pairs={{0,16},{8,24},{16,0},{24,8},{1,17},{9,25},{17,1},{25,9},{2,18},{10... | collective-permute-start | bytes 1572872 | tf_op jit(solution)/shard_map/ppermute | solution.py:56
  338.9 280.5 %reduce-scatter.10.cloned.1.call-start = ((), (), s32[]{:S(2)}) async-start(), calls=%async_computation.11 | async-start | bytes 3604480 | tf_op jit(solution)/shard_map/reduce_scatter | solution.py:67
  341.9 70.5 %collective-permute-start.39 = (bf16[128,2048]{1,0:T(8,128)(2,1)}, bf16[128,2048]{1,0:T(8,128)(2,1)S(1)}, u32[]{:S(2)}, u32[]{:S(2)}) collective-permute-start(bf16[128,2048]{1,0:T(8,128)(2,1)} %get-tuple-element.73), channel_id=1, source_target_pairs={{0,16},{8,24},{16,0},{24,8},{1,17},{9,25},{17,1},{25,9},{2,18},{10... | collective-permute-start | bytes 1572872 | tf_op jit(solution)/shard_map/ppermute | solution.py:56
  365.9 87.6 %collective-permute-start.68 = (bf16[704,2048]{1,0:T(8,128)(2,1)}, bf16[704,2048]{1,0:T(8,128)(2,1)}, u32[]{:S(2)}, u32[]{:S(2)}) collective-permute-start(bf16[704,2048]{1,0:T(8,128)(2,1)} %convolution_convert_fusion.6), channel_id=1, source_target_pairs={{0,8},{8,0},{16,24},{24,16},{1,9},{9,1},{17,25},{25,17},{2,10},{10... | collective-permute-start | bytes 8650760 | tf_op jit(solution)/shard_map/ppermute | solution.py:53
  373.5 124.4 %collective-permute-start.70 = (bf16[704,2048]{1,0:T(8,128)(2,1)}, bf16[704,2048]{1,0:T(8,128)(2,1)}, u32[]{:S(2)}, u32[]{:S(2)}) collective-permute-start(bf16[704,2048]{1,0:T(8,128)(2,1)} %convolution_convert_fusion.4), channel_id=1, source_target_pairs={{0,8},{8,0},{16,24},{24,16},{1,9},{9,1},{17,25},{25,17},{2,10},{10... | collective-permute-start | bytes 8650760 | tf_op jit(solution)/shard_map/ppermute | solution.py:53
  461.9 162.8 %reduce-scatter.14.cloned.1.call-start = ((), (), s32[]{:S(2)}) async-start(), calls=%async_computation.13 | async-start | bytes 3604480 | tf_op jit(solution)/shard_map/reduce_scatter | solution.py:67
  466.7 42.5 %collective-permute-start.61 = (bf16[1024,2048]{1,0:T(8,128)(2,1)}, bf16[1024,2048]{1,0:T(8,128)(2,1)}, u32[]{:S(2)}, u32[]{:S(2)}) collective-permute-start(bf16[1024,2048]{1,0:T(8,128)(2,1)} %convolution_convert_fusion.2), channel_id=1, source_target_pairs={{0,8},{8,0},{16,24},{24,16},{1,9},{9,1},{17,25},{25,17},{2,10},{10... | collective-permute-start | bytes 12582920 | tf_op jit(solution)/shard_map/ppermute | solution.py:53
  505.1 122.0 %reduce-scatter.8.cloned.1.call-start = ((), (), s32[]{:S(2)}) async-start(), calls=%async_computation.10 | async-start | bytes 1310720 | tf_op jit(solution)/shard_map/reduce_scatter | solution.py:67
  537.8 40.3 %collective-permute-start.55 = (bf16[2,64,2432]{2,1,0:T(8,128)(2,1)}, bf16[2,64,2432]{2,1,0:T(8,128)(2,1)}, u32[]{:S(2)}, u32[]{:S(2)}) collective-permute-start(bf16[2,64,2432]{2,1,0:T(8,128)(2,1)} %get-tuple-element.45), channel_id=1, source_target_pairs={{0,1},{1,0},{2,3},{3,2},{4,5},{5,4},{6,7},{7,6},{8,9},{9,8},{10,11... | collective-permute-start | bytes 1867784 | tf_op jit(solution)/shard_map/ppermute | solution.py:59
  539.4 38.7 %collective-permute-start.59 = (bf16[2,64,2432]{2,1,0:T(8,128)(2,1)}, bf16[2,64,2432]{2,1,0:T(8,128)(2,1)}, u32[]{:S(2)}, u32[]{:S(2)}) collective-permute-start(bf16[2,64,2432]{2,1,0:T(8,128)(2,1)} %get-tuple-element.46), channel_id=1, source_target_pairs={{0,16},{8,24},{16,0},{24,8},{1,17},{9,25},{17,1},{25,9},{2,18},{10... | collective-permute-start | bytes 1867784 | tf_op jit(solution)/shard_map/ppermute | solution.py:56
  542.8 53.8 %collective-permute-start.58 = (bf16[2,64,2432]{2,1,0:T(8,128)(2,1)}, bf16[2,64,2432]{2,1,0:T(8,128)(2,1)}, u32[]{:S(2)}, u32[]{:S(2)}) collective-permute-start(bf16[2,64,2432]{2,1,0:T(8,128)(2,1)} %get-tuple-element.47), channel_id=1, source_target_pairs={{0,16},{8,24},{16,0},{24,8},{1,17},{9,25},{17,1},{25,9},{2,18},{10... | collective-permute-start | bytes 1867784 | tf_op jit(solution)/shard_map/ppermute | solution.py:56
  554.9 37.4 %collective-permute-start.57 = (bf16[2,64,2432]{2,1,0:T(8,128)(2,1)}, bf16[2,64,2432]{2,1,0:T(8,128)(2,1)}, u32[]{:S(2)}, u32[]{:S(2)}) collective-permute-start(bf16[2,64,2432]{2,1,0:T(8,128)(2,1)} %fusion.67), channel_id=1, source_target_pairs={{0,16},{8,24},{16,0},{24,8},{1,17},{9,25},{17,1},{25,9},{2,18},{10... | collective-permute-start | bytes 1867784 | tf_op jit(solution)/shard_map/ppermute | solution.py:56
  577.8 64.0 %reduce-scatter.6.cloned.1.call-start = ((), (), s32[]{:S(2)}) async-start(), calls=%async_computation.9 | async-start | bytes 1556480 | tf_op jit(solution)/shard_map/reduce_scatter | solution.py:67
  (123 other events, 2691.8 us)
Sparse Core Ops, SparseCore 0:
  9.6 30.6 all-gather.6
  42.4 31.0 all-gather.4
  75.7 105.7 all-gather.8
  182.9 57.4 all-gather.10
  339.0 53.0 reduce-scatter.11
  462.0 54.8 reduce-scatter.9
  519.2 56.0 reduce-scatter.13
  577.9 26.6 reduce-scatter.7
  612.6 29.1 reduce-scatter.5

commit v2 on v0

v2 whole, which is shorter than its diff:
```python
import functools

import jax
import jax.numpy as jnp
from jax import lax
from jax.experimental import pallas as pl
from jax.experimental.pallas import tpu as pltpu
from jax.sharding import PartitionSpec as P

epsilon = 1e-05
theta_base = 10000.0
bf16 = jnp.bfloat16
f32 = jnp.float32
lanes = 128
step = 256
vmem_limit = 60 * 1024 * 1024


def rope_tables(length, width):
    halfway = width // 2
    freqs = theta_base ** (-(jnp.arange(halfway, dtype=jnp.float32) * 2.0 / width))
    angles = jnp.arange(length, dtype=jnp.float32)[:, None] * freqs[None, :]
    cosines, sine_part = jnp.cos(angles), jnp.sin(angles)
    return (
        jnp.concatenate([cosines, cosines], axis=1),
        jnp.concatenate([-sine_part, sine_part], axis=1),
    )


def contract(left, right, left_axis, right_axis):
    return lax.dot_general(
        left, right, (((left_axis,), (right_axis,)), ((), ())), preferred_element_type=jnp.float32
    )


def contract_last(left, right):
    return contract(left, right, left.ndim - 1, right.ndim - 1)


def contract_first(left, right):
    return contract(left, right, 0, 0)


def after(value, token):
    value, _ = lax.optimization_barrier((value, token))
    return value


def vmem_spec():
    return pl.BlockSpec(memory_space=pltpu.VMEM)


def any_spec():
    return pl.BlockSpec(memory_space=pl.ANY)


def smem_spec():
    return pl.BlockSpec(memory_space=pltpu.SMEM)


def kernel_call(body, out_shapes, scratch, in_specs):
    def run(*operands):
        known, late = len(in_specs), len(operands) - len(in_specs)

        def whole_body(*refs):
            body(*refs[:known], *refs[known + late :])

        return pl.pallas_call(
            whole_body,
            out_shape=out_shapes,
            in_specs=in_specs + [any_spec()] * late,
            out_specs=jax.tree.map(lambda _: vmem_spec(), out_shapes),
            scratch_shapes=scratch,
            compiler_params=pltpu.CompilerParams(vmem_limit_bytes=vmem_limit),
            cost_estimate=pl.CostEstimate(flops=1, bytes_accessed=1, transcendentals=0),
        )(*operands)

    return run


class Pieces:
    def __init__(self, depth, rows, columns, arrays):
        self.depth, self.rows, self.columns, self.arrays = depth, rows, columns, arrays

    def start(self, refs, spot, whole, sem):
        cut = self.depth // 2
        place = 0
        for flip in range(2):
            for dx in range(2):
                for dy in range(2):
                    for low, high in ((0, cut), (cut, self.depth)):
                        for outer in range(low, high):
                            block = (
                                (spot[0] ^ (2 * dx + flip)) * self.depth + outer
                            ) * 2 + (spot[1] ^ dy)
                            row = pl.multiple_of(block * self.rows, self.rows)
                            pltpu.make_async_copy(
                                refs[place].at[outer - low], whole.at[pl.ds(row, self.rows)], sem
                            ).start()
                        place += 1

    def wait(self, whole, sem):
        pltpu.make_async_copy(whole, whole, sem).wait()


def swap_halves(value):
    return pltpu.roll(value, value.shape[-1] // 2, 1)


def relative_place(block, spot, depth):
    side = block % 2
    outer = (block // 2) % depth
    flips = (block // (2 * depth)) ^ spot[0]
    return (((flips % 2) * 2 + flips // 2) * 2 + (side ^ spot[1])) * depth + outer


def put_in_order(source, target, spot, depth, rows):
    @pl.loop(0, source.shape[0] // rows)
    def _(block):
        place = pl.multiple_of(relative_place(block, spot, depth) * rows, rows)
        target[pl.ds(place, rows), :] = source[pl.ds(pl.multiple_of(block * rows, rows), rows), :]


def project_body(pieces, q_width, kv_width, head_dim, *refs):
    count = len(pieces.arrays)
    spot, tokens, cosines, sines = refs[:4]
    shards = refs[4 : 4 + count]
    h_turned, q_out, kv_out, gain_out = refs[4 + count : 8 + count]
    whole, h_low, flat, sem = refs[8 + count :]
    pieces.start(shards, spot, whole, sem)
    width = tokens.shape[1]
    x_full = tokens[...].astype(f32)
    inverse = lax.rsqrt(jnp.mean(x_full * x_full, axis=-1, keepdims=True) + epsilon)
    pieces.wait(whole, sem)
    pick = (
        lax.broadcasted_iota(jnp.int32, (8, lanes), 0) == lax.broadcasted_iota(jnp.int32, (8, lanes), 1)
    ).astype(bf16)
    gains = contract_last(pick, whole[:, q_width + kv_width :])
    gain_out[...] = gains
    h_low[...] = (x_full * inverse * gains[0:1]).astype(bf16)
    cos, sin = cosines[...], sines[...]
    kv_pre = jnp.dot(h_low[...], whole[:, q_width : q_width + kv_width], preferred_element_type=f32)
    key_part = kv_pre[:, :head_dim]
    kv_out[:, :head_dim] = (key_part * cos + swap_halves(key_part) * sin).astype(bf16)
    kv_out[:, head_dim:] = kv_pre[:, head_dim:].astype(bf16)

    @pl.loop(0, q_width // step)
    def _(block):
        start = pl.multiple_of(block * step, step)
        q_pre = jnp.dot(h_low[...], whole[:, pl.ds(start, step)], preferred_element_type=f32)
        for head in range(step // head_dim):
            own = q_pre[:, head * head_dim : (head + 1) * head_dim]
            column = pl.multiple_of(start + head * head_dim, head_dim)
            q_out[:, pl.ds(column, head_dim)] = (own * cos + swap_halves(own) * sin).astype(bf16)

    @pl.loop(0, width // step)
    def _(block):
        start = pl.multiple_of(block * step, step)
        flat[pl.ds(start, step), :] = h_low[:, pl.ds(start, step)].T

    put_in_order(flat, h_turned, spot, pieces.depth, pieces.rows)


def project(spot, tokens, cosines, sines, pieces, q_width, kv_width, head_dim, late=()):
    length, width = tokens.shape
    count = len(pieces.arrays)
    shape = jax.ShapeDtypeStruct
    return kernel_call(
        functools.partial(project_body, pieces, q_width, kv_width, head_dim),
        (
            shape((width, length), bf16),
            shape((length, q_width), bf16),
            shape((length, kv_width), bf16),
            shape((8, width), f32),
        ),
        [
            pltpu.VMEM((width, pieces.columns), bf16),
            pltpu.VMEM((length, width), bf16),
            pltpu.VMEM((width, length), bf16),
            pltpu.SemaphoreType.DMA,
        ],
        [smem_spec(), vmem_spec(), vmem_spec(), vmem_spec()] + [any_spec()] * count,
    )(spot, tokens, cosines, sines, *pieces.arrays, *late)


def attend_body(depth, rows, head_dim, spot, q_low, kv_low, prob_out, attended_out, turned, flat):
    length, q_width = q_low.shape
    scale = head_dim ** (-0.5)
    keys = kv_low[:, :head_dim]
    values_turned = kv_low[:, head_dim:].T
    allowed = lax.broadcasted_iota(jnp.int32, (length, length), 0) <= lax.broadcasted_iota(
        jnp.int32, (length, length), 1
    )
    heads = step // head_dim

    @pl.loop(0, q_width // step)
    def _(block):
        for head in range(heads):
            column = pl.multiple_of(block * step + head * head_dim, head_dim)
            queries = q_low[:, pl.ds(column, head_dim)]
            logits = jnp.where(allowed, contract_last(keys, queries) * scale, -1e30)
            exp_vals = jnp.exp(logits - jnp.max(logits, axis=0, keepdims=True))
            prob = (exp_vals / jnp.sum(exp_vals, axis=0, keepdims=True)).astype(bf16)
            prob_out[block * heads + head] = prob
            mixed = jnp.dot(values_turned, prob, preferred_element_type=f32)
            flat[pl.ds(column, head_dim), :] = mixed.astype(bf16)
            attended_out[:, pl.ds(column, head_dim)] = mixed.T.astype(bf16)

    put_in_order(flat, turned, spot, depth, rows)


def attend(spot, q_low, kv_low, depth, rows, late=()):
    length, q_width = q_low.shape
    head_dim = kv_low.shape[1] // 2
    shape = jax.ShapeDtypeStruct
    return kernel_call(
        functools.partial(attend_body, depth, rows, head_dim),
        (
            shape((q_width // head_dim, length, length), bf16),
            shape((length, q_width), bf16),
            shape((q_width, length), bf16),
        ),
        [pltpu.VMEM((q_width, length), bf16)],
        [smem_spec(), vmem_spec(), vmem_spec()],
    )(spot, q_low, kv_low, *late)


def mix_body(pieces, *refs):
    count = len(pieces.arrays)
    spot, tokens, attended, gains = refs[:4]
    shards = refs[4 : 4 + count]
    mid_out, first_out, second_out = refs[4 + count : 7 + count]
    whole, sem = refs[7 + count :]
    pieces.start(shards, spot, whole, sem)
    length, width = tokens.shape
    pieces.wait(whole, sem)

    def add(block, total):
        start = pl.multiple_of(block * step, step)
        branch = jnp.dot(attended[...], whole[:, pl.ds(start, step)], preferred_element_type=f32)
        x_mid = tokens[:, pl.ds(start, step)].astype(f32) + branch
        mid_out[:, pl.ds(start, step)] = x_mid
        return total + jnp.sum(x_mid * x_mid, axis=-1, keepdims=True)

    total = lax.fori_loop(0, width // step, add, jnp.zeros((length, 1), f32))
    inverse = lax.rsqrt(total / width + epsilon)
    h_two = (mid_out[...] * inverse * gains[1:2, :]).astype(bf16)
    first_out[...] = h_two[: length // 2]
    second_out[...] = h_two[length // 2 :]


def mix(spot, tokens, attended, gains, pieces, late=()):
    length, width = tokens.shape
    shape = jax.ShapeDtypeStruct
    half = shape((length // 2, width), bf16)
    rows = attended.shape[1]
    return kernel_call(
        functools.partial(mix_body, pieces),
        (shape((length, width), f32), half, half),
        [pltpu.VMEM((rows, width), bf16), pltpu.SemaphoreType.DMA],
        [smem_spec(), vmem_spec(), vmem_spec(), vmem_spec()] + [any_spec()] * len(pieces.arrays),
    )(spot, tokens, attended, gains, *pieces.arrays, *late)


def norm_back_body(factor, mid, gains, grad_out, *refs):
    sums = refs[:6]
    d_mid_out, d_mid_low, gain_out = refs[6:]
    length = mid.shape[0]
    half = length // 2
    for part in range(2):
        rows = pl.ds(part * half, half)
        terms = sums[3 * part : 3 * part + 3]
        d_h = terms[0][...].astype(f32) + terms[1][...].astype(f32) + terms[2][...].astype(f32)
        x_mid = mid[rows, :]
        inverse = lax.rsqrt(jnp.mean(x_mid * x_mid, axis=-1, keepdims=True) + epsilon)
        normed = x_mid * inverse
        product = d_h * normed
        gain_sum = jnp.broadcast_to(jnp.sum(product, axis=0, keepdims=True), gain_out.shape)
        if part == 0:
            gain_out[...] = gain_sum
        else:
            gain_out[...] += gain_sum
        gain = gains[1:2, :]
        mean = jnp.mean(product * gain, axis=-1, keepdims=True)
        grad_top = grad_out[rows, :].astype(f32) * factor[0]
        d_mid = grad_top + inverse * (d_h * gain - normed * mean)
        d_mid_out[rows, :] = d_mid
        d_mid_low[rows, :] = d_mid.astype(bf16)


def norm_back(factor, mid, gains, grad_out, sums, late=()):
    length, width = mid.shape
    shape = jax.ShapeDtypeStruct
    return kernel_call(
        norm_back_body,
        (shape((length, width), f32), shape((length, width), bf16), shape((8, width), f32)),
        [],
        [smem_spec()] + [vmem_spec()] * 9,
    )(factor, mid, gains, grad_out, *sums, *late)


def attend_back_body(pieces, head_dim, *refs):
    count = len(pieces.arrays)
    (spot, factor, d_mid_low, grad_kv, q_low, kv_low, prob_ref, cosines, sines) = refs[:9]
    shards = refs[9 : 9 + count]
    joined, d_kv_out = refs[9 + count : 11 + count]
    whole, sem = refs[11 + count :]
    pieces.start(shards, spot, whole, sem)
    length = d_mid_low.shape[0]
    q_width = q_low.shape[1]
    scale = head_dim ** (-0.5)
    cos, sin = cosines[...], sines[...]
    keys, values = kv_low[:, :head_dim], kv_low[:, head_dim:]
    d_kv_out[...] = grad_kv[...].astype(f32) * factor[0]
    pieces.wait(whole, sem)
    heads = step // head_dim

    @pl.loop(0, q_width // step)
    def _(block):
        start = pl.multiple_of(block * step, step)
        d_att = contract_last(d_mid_low[...], whole[pl.ds(start, step), :]).astype(bf16)
        d_k = jnp.zeros((length, head_dim), f32)
        d_v = jnp.zeros((length, head_dim), f32)
        for head in range(heads):
            own = d_att[:, head * head_dim : (head + 1) * head_dim]
            column = pl.multiple_of(start + head * head_dim, head_dim)
            low = prob_ref[block * heads + head]
            prob = low.astype(f32)
            d_prob = contract_last(values, own)
            centre = jnp.sum(prob * d_prob, axis=0, keepdims=True)
            d_raw = (prob * (d_prob - centre) * scale).astype(bf16)
            d_v += jnp.dot(low, own, preferred_element_type=f32)
            d_k += jnp.dot(d_raw, q_low[:, pl.ds(column, head_dim)], preferred_element_type=f32)
            d_q = contract_first(d_raw, keys)
            joined[:, pl.ds(column, head_dim)] = (d_q * cos - swap_halves(d_q) * sin).astype(bf16)
        d_kv_out[:, :head_dim] += d_k
        d_kv_out[:, head_dim:] += d_v

    d_k = d_kv_out[:, :head_dim]
    joined[:, q_width : q_width + head_dim] = (d_k * cos - swap_halves(d_k) * sin).astype(bf16)
    joined[:, q_width + head_dim :] = d_kv_out[:, head_dim:].astype(bf16)


def attend_back(spot, factor, d_mid_low, grad_kv, q_low, kv_low, prob, cosines, sines, pieces, late=()):
    length, width = d_mid_low.shape
    q_width, kv_width = q_low.shape[1], kv_low.shape[1]
    head_dim = kv_width // 2
    shape = jax.ShapeDtypeStruct
    return kernel_call(
        functools.partial(attend_back_body, pieces, head_dim),
        (shape((length, q_width + kv_width), bf16), shape((length, kv_width), f32)),
        [pltpu.VMEM((q_width, width), bf16), pltpu.SemaphoreType.DMA],
        [smem_spec()] * 2 + [vmem_spec()] * 7 + [any_spec()] * len(pieces.arrays),
    )(spot, factor, d_mid_low, grad_kv, q_low, kv_low, prob, cosines, sines, *pieces.arrays, *late)


def finish_body(pieces, *refs):
    count = len(pieces.arrays)
    spot, tokens, gains, joined, d_mid = refs[:5]
    shards = refs[5 : 5 + count]
    d_tokens, gain_out = refs[5 + count : 7 + count]
    whole, sem = refs[7 + count :]
    pieces.start(shards, spot, whole, sem)
    length, width = tokens.shape
    used = joined.shape[1]
    x_full = tokens[...].astype(f32)
    inverse = lax.rsqrt(jnp.mean(x_full * x_full, axis=-1, keepdims=True) + epsilon)
    pieces.wait(whole, sem)

    def add(block, total):
        start = pl.multiple_of(block * step, step)
        columns = pl.ds(start, step)
        d_h = contract_last(joined[...], whole[columns, :used])
        normed = tokens[:, columns].astype(f32) * inverse
        gain_out[:, columns] = jnp.broadcast_to(
            jnp.sum(d_h * normed, axis=0, keepdims=True), (8, step)
        )
        d_normed = d_h * gains[0:1, columns]
        d_tokens[:, columns] = d_normed
        return total + jnp.sum(d_normed * normed, axis=-1, keepdims=True)

    total = lax.fori_loop(0, width // step, add, jnp.zeros((length, 1), f32))
    d_tokens[...] = d_mid[...] + inverse * (d_tokens[...] - x_full * inverse * (total / width))


def finish(spot, tokens, gains, joined, d_mid, pieces, late=()):
    length, width = tokens.shape
    shape = jax.ShapeDtypeStruct
    return kernel_call(
        functools.partial(finish_body, pieces),
        (shape((length, width), f32), shape((8, width), f32)),
        [pltpu.VMEM((width, pieces.columns), bf16), pltpu.SemaphoreType.DMA],
        [smem_spec()] + [vmem_spec()] * 4 + [any_spec()] * len(pieces.arrays),
    )(spot, tokens, gains, joined, d_mid, *pieces.arrays, *late)


def fetch_rows(parts, whole, sem):
    start = 0
    for part in parts:
        pltpu.make_async_copy(part, whole.at[pl.ds(start, part.shape[0])], sem).start()
        start += part.shape[0]
    return pltpu.make_async_copy(whole, whole, sem).wait


def fetch_gate_up(both, shard, first, second, first_sem, second_sem):
    waits = []
    for place, (whole, sem) in enumerate(((first, first_sem), (second, second_sem))):
        for outer in range(both.shape[0] // (2 * shard)):
            source = both.at[pl.ds((2 * outer + place) * shard, shard)]
            pltpu.make_async_copy(source, whole.at[pl.ds(outer * shard, shard)], sem).start()
        waits.append(pltpu.make_async_copy(whole, whole, sem).wait)
    return waits


def gate_body(shard, count, *refs):
    parts, both = refs[:count], refs[count]
    hid, by_gate, by_up = refs[count + 1 : count + 4]
    rows, gate_w, up_w, row_sem, gate_sem, up_sem = refs[count + 4 :]
    waits = fetch_gate_up(both, shard, gate_w, up_w, gate_sem, up_sem)
    waits.append(fetch_rows(parts, rows, row_sem))
    for wait in waits:
        wait()

    @pl.loop(0, rows.shape[0] // step)
    def _(block):
        own = pl.ds(pl.multiple_of(block * step, step), step)
        gate = contract_last(rows[own, :], gate_w[...])
        up = contract_last(rows[own, :], up_w[...])
        sigma = 1.0 / (1.0 + jnp.exp(-gate))
        silu = gate * sigma
        hid[own, :] = (silu * up).astype(bf16)
        by_gate[own, :] = (up * sigma * (1.0 + gate * (1.0 - sigma))).astype(bf16)
        by_up[own, :] = silu.astype(bf16)


def gate(parts, both, shard, late=()):
    total, width = sum(part.shape[0] for part in parts), parts[0].shape[1]
    hidden = both.shape[0] // 2
    out = jax.ShapeDtypeStruct((total, hidden), bf16)
    return kernel_call(
        functools.partial(gate_body, shard, len(parts)),
        (out, out, out),
        [pltpu.VMEM((total, width), bf16)]
        + [pltpu.VMEM((hidden, width), bf16)] * 2
        + [pltpu.SemaphoreType.DMA] * 3,
        [any_spec()] * (len(parts) + 1),
    )(*parts, both, *late)


def d_hidden(rows, weight, scales, grads):
    @pl.loop(0, rows.shape[0] // step)
    def _(block):
        own = pl.ds(pl.multiple_of(block * step, step), step)
        d_hid = contract_last(rows[own, :], weight[...])
        for scale, grad in zip(scales, grads):
            grad[own, :] = (d_hid * scale[own, :].astype(f32)).astype(bf16)


def gate_back_body(count, *refs):
    parts, weight, scales, grads = refs[:count], refs[count], refs[count + 1 : count + 3], refs[count + 3 : count + 5]
    rows, sem = refs[count + 5 :]
    fetch_rows(parts, rows, sem)()
    d_hidden(rows, weight, scales, grads)


def gate_back(parts, weight, scales, late=()):
    count = len(parts)
    total, width = sum(part.shape[0] for part in parts), parts[0].shape[1]
    grad = jax.ShapeDtypeStruct((total, weight.shape[0]), bf16)
    return kernel_call(
        functools.partial(gate_back_body, count),
        (grad, grad),
        [pltpu.VMEM((total, width), bf16), pltpu.SemaphoreType.DMA],
        [any_spec()] * count + [vmem_spec()] * 3,
    )(*parts, weight, *scales, *late)


def rows_back_body(shard, count, *refs):
    parts, weight, scales, others, boths = (
        refs[:count], refs[count], refs[count + 1 : count + 3], refs[count + 3 : count + 5],
        refs[count + 5 : count + 7],
    )
    refs = refs[count + 7 :]
    grads, outs = refs[:2], refs[2 : 2 + count]
    rows, weights, sems = refs[2 + count], refs[3 + count : 7 + count], refs[7 + count]
    row_wait = fetch_rows(parts, rows, sems.at[0])
    waits = []
    for place in range(2):
        waits += fetch_gate_up(
            boths[place], shard, weights[2 * place], weights[2 * place + 1],
            sems.at[1 + 2 * place], sems.at[2 + 2 * place],
        )
    row_wait()
    d_hidden(rows, weight, scales, grads)
    for wait in waits:
        wait()
    size = outs[0].shape[0]
    for place, out in enumerate(outs):
        own = pl.ds(place * size, size)
        total = jnp.dot(grads[0][own, :], weights[0][...], preferred_element_type=f32)
        for grad, piece in zip((grads[1], *others), weights[1:]):
            total += jnp.dot(grad[own, :], piece[...], preferred_element_type=f32)
        out[...] = total.astype(bf16)


def rows_back(parts, weight, scales, others, boths, shard, late=()):
    count = len(parts)
    total, width = sum(part.shape[0] for part in parts), parts[0].shape[1]
    hidden = weight.shape[0]
    shape = jax.ShapeDtypeStruct
    outs = kernel_call(
        functools.partial(rows_back_body, shard, count),
        (shape((total, hidden), bf16),) * 2 + tuple(shape(part.shape, bf16) for part in parts),
        [pltpu.VMEM((total, width), bf16)]
        + [pltpu.VMEM((hidden, width), bf16)] * 4
        + [pltpu.SemaphoreType.DMA((5,))],
        [any_spec()] * count + [vmem_spec()] * 5 + [any_spec()] * 2,
    )(*parts, weight, *scales, *others, *boths, *late)
    return outs[:2], outs[2:]


def down_body(count, *refs):
    hids, downs, outs = refs[:2], refs[2:4], refs[4:]
    size = outs[0].shape[0]
    for place, out in enumerate(outs):
        own = pl.ds(place * size, size)
        total = jnp.dot(hids[0][own, :], downs[0][...], preferred_element_type=f32)
        total += jnp.dot(hids[1][own, :], downs[1][...], preferred_element_type=f32)
        out[...] = total.astype(bf16)


def down(hids, downs, count, late=()):
    total, width = hids[0].shape[0], downs[0].shape[1]
    return kernel_call(
        functools.partial(down_body, count),
        (jax.ShapeDtypeStruct((total // count, width), bf16),) * count,
        [],
        [vmem_spec()] * 4,
    )(*hids, *downs, *late)


def hidden_sums_body(count, pairs, shard, received, *refs):
    lefts, parts = refs[:pairs], refs[pairs : pairs + count]
    other = refs[pairs + count] if received else None
    out, rows, sem = refs[-3], refs[-2], refs[-1]
    fetch_rows(parts, rows, sem)()
    for place, left in enumerate(lefts):
        product = contract_first(left[...], rows[...])
        for outer in range(left.shape[1] // shard):
            target = pl.ds((pairs * outer + place) * shard, shard)
            own = product[outer * shard : (outer + 1) * shard]
            if received:
                own = own + other[target, :].astype(f32)
            out[target, :] = own.astype(bf16)


def hidden_sums(lefts, parts, shard, other=None, late=()):
    total, width = lefts[0].shape[0], parts[0].shape[1]
    hidden = lefts[0].shape[1] * len(lefts)
    received = other is not None
    return kernel_call(
        functools.partial(hidden_sums_body, len(parts), len(lefts), shard, received),
        jax.ShapeDtypeStruct((hidden, width), bf16),
        [pltpu.VMEM((total, width), bf16), pltpu.SemaphoreType.DMA],
        [vmem_spec()] * len(lefts) + [any_spec()] * len(parts) + [vmem_spec()] * received,
    )(*lefts, *parts, *((other,) if received else ()), *late)


def send_sums_body(turned, right, out):
    middle = turned.shape[0] // 2

    @pl.loop(0, middle // step)
    def _(block):
        start = pl.multiple_of(block * step, step)
        product = jnp.dot(turned[pl.ds(middle + start, step), :], right[...], preferred_element_type=f32)
        out[pl.ds(start, step), :] = product.astype(bf16)


def send_sums(turned, right, late=()):
    return kernel_call(
        send_sums_body,
        jax.ShapeDtypeStruct((turned.shape[0] // 2, right.shape[1]), bf16),
        [],
        [vmem_spec()] * 2,
    )(turned, right, *late)


def keep_sums_body(turned, right, other, *outs):
    size = outs[0].shape[0]
    for place, out in enumerate(outs):
        own = pl.ds(place * size, size)
        product = jnp.dot(turned[own, :], right[...], preferred_element_type=f32)
        out[...] = (product + other[own, :].astype(f32)).astype(bf16)


def keep_sums(turned, right, other, late=()):
    size = turned.shape[0] // 16
    outs = kernel_call(
        keep_sums_body,
        (jax.ShapeDtypeStruct((size, right.shape[1]), bf16),) * 8,
        [],
        [vmem_spec()] * 3,
    )(turned, right, other, *late)
    return {
        (dx, dy): (outs[4 * dx + 2 * dy], outs[4 * dx + 2 * dy + 1])
        for dx in range(2)
        for dy in range(2)
    }


def pass_body(a, b, c, d, first, second):
    first[...] = (a[...].astype(f32) + b[...].astype(f32)).astype(bf16)
    second[...] = (c[...].astype(f32) + d[...].astype(f32)).astype(bf16)


def add_pairs(a, b, c, d, late=()):
    shape = jax.ShapeDtypeStruct
    return kernel_call(
        pass_body, (shape(a.shape, bf16), shape(c.shape, bf16)), [], [vmem_spec()] * 4
    )(a, b, c, d, *late)


class Grid:
    def __init__(self, dp, fsdp):
        self.dp, self.fsdp = dp, fsdp
        self.depth = fsdp // 2
        self.groups = [[f for f in range(fsdp) if f % 2 == y] for y in range(2)]
        self.dp_index = lax.axis_index("dp")
        self.y = lax.axis_index("fsdp") % 2
        self.spot = jnp.stack([self.dp_index, self.y]).astype(jnp.int32)
        self.outer = lax.axis_index("fsdp") // 2

    def core(self, value):
        return lax.ppermute(value, "dp", [(i, i ^ 1) for i in range(self.dp)])

    def echo(self, value, times):
        corner = value[:8, :lanes]
        for _ in range(times):
            corner = self.core(corner)
        return corner

    def x_swap(self, value):
        return lax.ppermute(value, "dp", [(i, i ^ 2) for i in range(self.dp)])

    def y_swap(self, value):
        return lax.ppermute(value, "fsdp", [(i, i ^ 1) for i in range(self.fsdp)])

    def shift(self, value, low, high, by):
        pairs = [
            (2 * outer + y, 2 * (outer + by) + y) for outer in range(low, high) for y in range(2)
        ]
        return lax.ppermute(value, "fsdp", pairs)

    def gather_outer(self, value):
        return lax.all_gather(value, "fsdp", axis=0, tiled=True, axis_index_groups=self.groups)

    def scatter_outer(self, value):
        return lax.psum_scatter(
            value, "fsdp", scatter_dimension=0, tiled=True, axis_index_groups=self.groups
        )

    def spread_first(self, first, second):
        return first, second, self.x_swap(first), self.y_swap(second)

    def spread_second(self, first, second, first_x, second_y):
        first, second, first_x, second_y = lax.optimization_barrier(
            (first, second, first_x, second_y)
        )
        first_xy = self.y_swap(first_x)
        second_xy = self.x_swap(second_y)
        first_y = self.y_swap(first)
        second_x = self.x_swap(second)
        return {
            (0, 0): (first, second),
            (1, 0): (first_x, second_x),
            (0, 1): (first_y, second_y),
            (1, 1): (first_xy, second_xy),
        }

    def collect_first(self, parts, late=()):
        first_xy = self.y_swap(parts[1, 1][0])
        second_xy = self.x_swap(parts[1, 1][1])
        first_y = self.y_swap(parts[0, 1][0])
        second_x = self.x_swap(parts[1, 0][1])
        for_x, for_y = add_pairs(parts[1, 0][0], first_xy, parts[0, 1][1], second_xy, late)
        return for_x, for_y, first_y, second_x

    def collect_second(self, parts, passed):
        for_x, for_y, first_y, second_x = passed
        return (
            (parts[0, 0][0], first_y, self.x_swap(for_x)),
            (parts[0, 0][1], second_x, self.y_swap(for_y)),
        )

    def pieces(self, planes, rows, token=None):
        keys = [(dx, dy) for dx in range(2) for dy in range(2)]
        mine = [half for key in keys for half in planes[key]]
        sent = mine if token is None else after(mine, token)
        theirs = [self.core(half) for half in sent]
        return Pieces(self.depth, rows, mine[0].shape[-1], mine + theirs)

    def column(self, sums):
        halves = [sum(term.astype(f32) for term in terms) for terms in sums]
        column = jnp.concatenate(halves, axis=0).astype(bf16)
        return column.reshape(-1, column.shape[-1])


def local(
    tokens,
    w_q,
    w_kv,
    g_attn,
    g_mlp,
    w_o,
    w_gu,
    w_down,
    grad_out,
    grad_kv,
    group_id,
    group_size,
    group_weight,
):
    grid = Grid(lax.axis_size("dp"), lax.axis_size("fsdp"))
    length, width = tokens.shape
    kv_width = w_kv.shape[1]
    head_dim = kv_width // 2
    q_width = w_q.shape[1]
    shard_rows = w_q.shape[0]
    hidden_rows = w_down.shape[0]
    half = length // 2

    matches = jnp.arange(group_size.shape[0], dtype=jnp.int32) == group_id[0]
    factor = jnp.sum(jnp.where(matches, group_weight / group_size.astype(jnp.float32), 0.0))
    grad_low = (grad_out.astype(jnp.float32) * factor).astype(jnp.bfloat16)
    cosines, sines = rope_tables(length, head_dim)

    plane_keys = ((0, 0), (1, 0), (0, 1), (1, 1))

    def in_order(planes):
        return [piece for key in plane_keys for piece in planes[key]]

    def by_key(blocks):
        return {key: (blocks[2 * i], blocks[2 * i + 1]) for i, key in enumerate(plane_keys)}

    gains = jnp.stack([g_attn, g_mlp], axis=1)
    w_in = jnp.concatenate([w_q, w_kv, jnp.pad(gains, ((0, 0), (0, lanes - 2)))], axis=1)
    w_in_column = grid.gather_outer(w_in)
    w_o_column = grid.gather_outer(after(w_o, w_in))
    grad_first = grid.spread_first(grad_low[:half], grad_low[half:])
    pairs = jnp.swapaxes(w_gu, 0, 1).reshape(2 * hidden_rows, width)
    gu_mine = grid.gather_outer(after(pairs, grad_first[2:]))
    grad_planes = grid.spread_second(*grad_first)
    grad_rows = in_order(grad_planes)
    cut = grid.depth // 2
    w_in_column = after(w_in_column, grad_planes[1, 1]).reshape(grid.depth, shard_rows, -1)
    in_planes = grid.spread_second(*grid.spread_first(w_in_column[:cut], w_in_column[cut:]))
    in_pieces = grid.pieces(in_planes, shard_rows)
    down_mine = grid.gather_outer(after(w_down, in_planes[1, 1]))
    w_o_column = after(w_o_column, in_planes[1, 1]).reshape(grid.depth, shard_rows, -1)
    o_first = grid.spread_first(w_o_column[:cut], w_o_column[cut:])
    h_turned, q_low, kv_out, gain_rows = project(
        grid.spot, tokens, cosines, sines, in_pieces, q_width, kv_width, head_dim
    )
    o_planes = grid.spread_second(*after(o_first, q_low))
    prob, attended, turned = attend(grid.spot, q_low, kv_out, grid.depth, shard_rows)
    o_pieces = grid.pieces(o_planes, shard_rows, attended)
    x_mid, h_first, h_second = mix(grid.spot, tokens, attended, gain_rows, o_pieces)

    ff_rows = in_order(grid.spread_second(*grid.spread_first(h_first, h_second)))
    gu_mine = after(gu_mine, ff_rows)
    by_shard = hidden_rows % 8 == 0
    run_rows = hidden_rows if by_shard else grid.depth * hidden_rows

    def turn(both, rows):
        return both.reshape(-1, rows, hidden_rows, width).swapaxes(0, 1).reshape(both.shape)

    if not by_shard:
        gu_mine = turn(gu_mine, 2)
    gu_other = grid.core(gu_mine)
    hid_mine, *scales_mine = gate(ff_rows, gu_mine, run_rows)
    hid_other, *scales_other = gate(ff_rows, gu_other, run_rows, [hid_mine])
    sent = hidden_sums([hid_other], grad_rows, run_rows, late=[down_mine])
    down_sum = hidden_sums([hid_mine], grad_rows, run_rows, grid.core(sent), [sent])
    d_w_down = grid.scatter_outer(down_sum).astype(f32)
    down_other = grid.core(down_mine)
    pair_other = gate_back(grad_rows, down_other, scales_other, [down_sum])
    sent = hidden_sums(pair_other, ff_rows, run_rows)
    pair_mine, d_h_blocks = rows_back(
        grad_rows, down_mine, scales_mine, pair_other, (gu_mine, gu_other), run_rows, [sent]
    )
    d_h_parts = by_key(d_h_blocks)
    pair_sum = hidden_sums(pair_mine, ff_rows, run_rows, grid.core(sent))
    d_w_gu = grid.scatter_outer(pair_sum if by_shard else turn(pair_sum, grid.depth)).astype(f32)
    d_h_passed = grid.collect_first(d_h_parts, [pair_sum, grid.echo(d_w_down, 2)])
    d_h_first, d_h_second = grid.collect_second(d_h_parts, d_h_passed)
    d_h_sums = [*d_h_first, *d_h_second]

    d_mid, d_mid_low, gain_two_sum = norm_back(
        factor.reshape(1), x_mid, gain_rows, grad_out, d_h_sums
    )
    sent = send_sums(turned, d_mid_low)
    o_parts = keep_sums(turned, d_mid_low, grid.core(sent))
    joined, d_kv = attend_back(
        grid.spot, factor.reshape(1), d_mid_low, grad_kv, q_low, kv_out,
        prob, cosines, sines, o_pieces, [o_parts[0, 0][0]],
    )
    o_passed = grid.collect_first(o_parts, [joined])
    sent = send_sums(h_turned, joined)
    d_w_o = grid.scatter_outer(grid.column(grid.collect_second(o_parts, o_passed))).astype(f32)
    d_tokens, gain_one_sum = finish(grid.spot, tokens, gain_rows, joined, d_mid, in_pieces, [sent])
    in_parts = keep_sums(
        h_turned, joined, grid.core(sent), [o_passed[0], gain_one_sum, grid.echo(d_w_gu, 2)]
    )
    in_passed = grid.collect_first(in_parts)
    d_w_in = grid.column(grid.collect_second(in_parts, in_passed))
    d_w_gu = jnp.stack([d_w_gu[:hidden_rows], d_w_gu[hidden_rows:]], axis=1)
    mlp_parts = by_key(
        down((hid_mine, hid_other), (down_mine, down_other), len(ff_rows), [in_passed[0]])
    )
    mlp_sum = grid.collect_second(mlp_parts, grid.collect_first(mlp_parts))
    mlp_sum = jnp.concatenate([sum(term.astype(f32) for term in terms) for terms in mlp_sum], axis=0)
    output = (x_mid + mlp_sum).astype(jnp.bfloat16)
    gain_sums = jnp.stack([gain_one_sum[0], gain_two_sum[0]], axis=0)
    for swap in (grid.core, grid.x_swap, grid.y_swap):
        gain_sums = gain_sums + swap(gain_sums)
    own_gains = lax.dynamic_slice(
        gain_sums.reshape(2, grid.dp, grid.depth, 2, shard_rows),
        (0, grid.dp_index, 0, grid.y, 0),
        (2, 1, grid.depth, 1, shard_rows),
    ).reshape(2, grid.depth * shard_rows)
    extra = jnp.pad(own_gains.T, ((0, 0), (0, lanes - 2))).astype(bf16)
    d_w_in = grid.scatter_outer(jnp.concatenate([d_w_in, extra], axis=1)).astype(f32)
    return (
        output,
        d_tokens,
        kv_out,
        d_kv,
        d_w_in[:, :q_width],
        d_w_in[:, q_width : q_width + kv_width],
        d_w_in[:, q_width + kv_width],
        d_w_in[:, q_width + kv_width + 1],
        d_w_o,
        d_w_gu,
        d_w_down,
    )


def solution(mesh):
    placed = (
        P(("dp", "fsdp"), None),
        P(("dp", "fsdp"), None),
        P(("dp", "fsdp"), None),
        P(("dp", "fsdp")),
        P(("dp", "fsdp")),
        P(("dp", "fsdp"), None),
        P(("dp", "fsdp"), None, None),
        P(("dp", "fsdp"), None),
        P(("dp", "fsdp"), None),
        P(("dp", "fsdp"), None),
        P(("dp", "fsdp")),
        P(),
        P(),
    )
    return jax.shard_map(
        local,
        mesh=mesh,
        in_specs=placed,
        out_specs=(
            P(("dp", "fsdp"), None),
            P(("dp", "fsdp"), None),
            P(("dp", "fsdp"), None),
            P(("dp", "fsdp"), None),
            P(("dp", "fsdp"), None),
            P(("dp", "fsdp"), None),
            P(("dp", "fsdp")),
            P(("dp", "fsdp")),
            P(("dp", "fsdp"), None),
            P(("dp", "fsdp"), None, None),
            P(("dp", "fsdp"), None),
        ),
        check_vma=False,
    )
```

time: 1750 us -> 602 us (0.34)
  waiting for transfers between devices: 1380 us -> 248 us
  Pallas kernels: 0 us -> 228 us
  matrix products: 166 us -> 0 us
  blocking collectives: 84.7 us -> 0 us
  starting transfers between devices: 1.51 us -> 57.1 us
  local copies, waits for them, and re-layouts: 52.5 us -> 25.6 us
    reduce_scatter x5 -> x4, waiting for transfers between devices: 577 us -> 12.8 us  [scatter_outer(): lax.psum_scatter(value, 'fsdp', scatter_dimension=0, tiled=True, axis_ind...]
    all_gather x7 -> x4, waiting for transfers between devices: 453 us -> 27.1 us  [gather_outer(): lax.all_gather(value, 'fsdp', axis=0, tiled=True, axis_index_groups=self....]
    unnamed x14 -> x8, waiting for transfers between devices: 348 us -> 0.81 us
    pallas_call x0 -> x23, Pallas kernels: none -> 228 us  [run(): pl.pallas_call(whole_body, out_shape=out_shapes, in_specs=in_specs + [any...]
    ppermute x0 -> x77, waiting for transfers between devices: none -> 207 us  [the longest x25 94.9 us: y_swap(): return lax.ppermute(value, 'fsdp', [(i, i ^ 1) for i in range(self.fsdp)])]
    dot_general x20 -> x0, matrix products: 166 us -> none  [the longest x4 29.8 us: contract_last(): lax.dot_general(left, right, (((left.ndim - 1,), (right.ndim - 1,)), ((),...]
    unnamed x2 -> x0, blocking collectives: 84.7 us -> none
    ppermute x0 -> x77, starting transfers between devices: none -> 56.3 us  [the longest x25 26.4 us: x_swap(): return lax.ppermute(value, 'dp', [(i, i ^ 2) for i in range(self.dp)])]
  transfers between devices with their start and end apart: 13 -> 85, of which waited for: 11 -> 43; matrix products, arithmetic and copies ran while one was open for 12% -> 5% of each run, Pallas kernels for 0% -> 33%
where the time goes in v2:
time: 602 us; the launch traced here: 595 us
  waiting for transfers between devices  248 us (41%)
  Pallas kernels  228 us (38%)
  starting transfers between devices  57.1 us (9%)
  local copies, waits for them, and re-layouts  25.6 us (4%)
  other arithmetic  20.1 us (3%)
  between operations  15.9 us (3%)
    pallas_call x23, Pallas kernels, run(): pl.pallas_call(whole_body, out_shape=out_shapes, in_specs=in_specs + [any...  228 us
    ppermute x25, waiting for transfers between devices, y_swap(): return lax.ppermute(value, 'fsdp', [(i, i ^ 1) for i in range(self.fsdp)])  94.9 us
    ppermute x25, waiting for transfers between devices, x_swap(): return lax.ppermute(value, 'dp', [(i, i ^ 2) for i in range(self.dp)])  88.6 us
    all_gather x4, waiting for transfers between devices, gather_outer(): lax.all_gather(value, 'fsdp', axis=0, tiled=True, axis_index_groups=self....  27.1 us
    ppermute x25, starting transfers between devices, x_swap(): return lax.ppermute(value, 'dp', [(i, i ^ 2) for i in range(self.dp)])  26.4 us
    ppermute x25, starting transfers between devices, y_swap(): return lax.ppermute(value, 'fsdp', [(i, i ^ 1) for i in range(self.fsdp)])  26.3 us
    ppermute x27, waiting for transfers between devices, core(): return lax.ppermute(value, 'dp', [(i, i ^ 1) for i in range(self.dp)])  24 us
    unnamed x119, local copies, waits for them, and re-layouts  13.2 us
  transfers between devices with their start and end apart: 85, of which 43 were waited for; matrix products, arithmetic and copies ran while one was open for 5% of the time, Pallas kernels for 33%

profile of v2, /device:TPU:0, one launch (start us, length us, event | category | flops | bytes accessed | tf_op | source)
XLA Modules:
  0.0 595.0 jit_solution(12712238954053507132)
XLA Ops:
  33.4 10.6 %collective-permute-done.2.refs_7_.refs_6_ = bf16[128,2048]{1,0:T(8,128)(2,1)S(1)} collective-permute-done((bf16[128,2048]{1,0:T(8,128)(2,1)S(1)}, bf16[128,2048]{1,0:T(8,128)(2,1)S(1)}, u32[]{:S(2)}, u32[]{:S(2)}) %collective-permute-start.2) | collective-permute-done | bytes 524320 | tf_op jit(solution)/shard_map/ppermute | solution.py:646
  48.8 12.3 %collective-permute-done.4.refs_8_.refs_9_ = bf16[2,64,2432]{2,1,0:T(8,128)(2,1)} collective-permute-done((bf16[2,64,2432]{2,1,0:T(8,128)(2,1)S(1)}, bf16[2,64,2432]{2,1,0:T(8,128)(2,1)}, u32[]{:S(2)}, u32[]{:S(2)}) %collective-permute-start.4) | collective-permute-done | bytes 622624 | tf_op jit(solution)/shard_map/ppermute | solution.py:643
  66.5 12.8 %collective-permute-done.6.refs_6_.refs_7_ = bf16[2,64,2432]{2,1,0:T(8,128)(2,1)} collective-permute-done((bf16[2,64,2432]{2,1,0:T(8,128)(2,1)S(1)}, bf16[2,64,2432]{2,1,0:T(8,128)(2,1)}, u32[]{:S(2)}, u32[]{:S(2)}) %collective-permute-start.6) | collective-permute-done | bytes 622624 | tf_op jit(solution)/shard_map/ppermute | solution.py:646
  81.0 11.2 %collective-permute-done.8.refs_10_.refs_11_ = bf16[2,64,2432]{2,1,0:T(8,128)(2,1)} collective-permute-done((bf16[2,64,2432]{2,1,0:T(8,128)(2,1)}, bf16[2,64,2432]{2,1,0:T(8,128)(2,1)}, u32[]{:S(2)}, u32[]{:S(2)}) %collective-permute-start.8) | collective-permute-done | bytes 622624 | tf_op jit(solution)/shard_map/ppermute | solution.py:646
  99.5 13.1 %shard_map.212 = (bf16[2048,256]{1,0:T(8,128)(2,1)}, bf16[256,2048]{1,0:T(8,128)(2,1)}, bf16[256,256]{1,0:T(8,128)(2,1)}, f32[8,2048]{1,0:T(8,128)}) custom-call(s32[2]{0:T(128)} %pad_add_fusion.refs_0_, bf16[256,2048]{1,0:T(8,128)(2,1)} %refs_1_.5, f32[256,128]{1,0:T(8,128)} %get-tuple-element.248.refs_2_.refs_7_, ...), custom_call_target="tpu_custom_call" | custom-call | flops 1 | bytes 1 | tf_op jit(solution)/shard_map/pallas_call | solution.py:68
  116.8 11.0 %shard_map.213 = (bf16[16,256,256]{2,1,0:T(8,128)(2,1)}, bf16[256,2048]{1,0:T(8,128)(2,1)}, bf16[2048,256]{1,0:T(8,128)(2,1)}) custom-call(s32[2]{0:T(128)} %pad_add_fusion.refs_0_, bf16[256,2048]{1,0:T(8,128)(2,1)} %get-tuple-element.119.refs_1_.refs_4_, bf16[256,256]{1,0:T(8,128)(2,1)} %get-tuple-element.226.refs_2_.refs_5_), custom_call_target="tpu_custom_call" | custom-call | flops 1 | bytes 1 | tf_op jit(solution)/shard_map/pallas_call | solution.py:68
  129.0 9.5 %collective-permute-done.23.refs_11_.refs_16_ = bf16[2,64,2048]{2,1,0:T(8,128)(2,1)} collective-permute-done((bf16[2,64,2048]{2,1,0:T(8,128)(2,1)S(1)}, bf16[2,64,2048]{2,1,0:T(8,128)(2,1)}, u32[]{:S(2)}, u32[]{:S(2)}) %collective-permute-start.23) | collective-permute-done | bytes 524320 | tf_op jit(solution)/shard_map/ppermute | solution.py:643
  147.3 10.9 %shard_map.214 = (f32[256,2048]{1,0:T(8,128)}, bf16[128,2048]{1,0:T(8,128)(2,1)}, bf16[128,2048]{1,0:T(8,128)(2,1)}) custom-call(s32[2]{0:T(128)} %pad_add_fusion.refs_0_, bf16[256,2048]{1,0:T(8,128)(2,1)} %refs_1_.5, bf16[256,2048]{1,0:T(8,128)(2,1)} %get-tuple-element.121.refs_2_, f32[8,2048]{1,0:T(8,128)} %get-tuple-element.122.refs_3_.refs_2_, ...), custom_call_target="tpu_custom_call" | custom-call | flops 1 | bytes 1 | tf_op jit(solution)/shard_map/pallas_call | solution.py:68
  160.4 12.1 %collective-permute-done.32.refs_2_.refs_4_ = bf16[128,2048]{1,0:T(8,128)(2,1)S(1)} collective-permute-done((bf16[128,2048]{1,0:T(8,128)(2,1)}, bf16[128,2048]{1,0:T(8,128)(2,1)S(1)}, u32[]{:S(2)}, u32[]{:S(2)}) %collective-permute-start.32) | collective-permute-done | bytes 524320 | tf_op jit(solution)/shard_map/ppermute | solution.py:643
  177.7 11.0 %collective-permute-done.35.refs_4_.refs_6_ = bf16[128,2048]{1,0:T(8,128)(2,1)S(1)} collective-permute-done((bf16[128,2048]{1,0:T(8,128)(2,1)}, bf16[128,2048]{1,0:T(8,128)(2,1)S(1)}, u32[]{:S(2)}, u32[]{:S(2)}) %collective-permute-start.35) | collective-permute-done | bytes 524320 | tf_op jit(solution)/shard_map/ppermute | solution.py:646
  200.9 14.1 %shard_map.215 = (bf16[1024,704]{1,0:T(8,128)(2,1)}, bf16[1024,704]{1,0:T(8,128)(2,1)}, bf16[1024,704]{1,0:T(8,128)(2,1)}) custom-call(bf16[128,2048]{1,0:T(8,128)(2,1)} %get-tuple-element.144.refs_0_.refs_2_, bf16[128,2048]{1,0:T(8,128)(2,1)} %get-tuple-element.145.refs_1_.refs_3_, bf16[128,2048]{1,0:T(8,128)(2,1)} %copy-done.3, ...), custom_call_target="tpu_custom_call" | custom-call | flops 1 | bytes 1 | tf_op jit(solution)/shard_map/pallas_call | solution.py:68
  215.0 14.0 %shard_map.216 = (bf16[1024,704]{1,0:T(8,128)(2,1)}, bf16[1024,704]{1,0:T(8,128)(2,1)}, bf16[1024,704]{1,0:T(8,128)(2,1)}) custom-call(bf16[128,2048]{1,0:T(8,128)(2,1)} %get-tuple-element.144.refs_0_.refs_2_, bf16[128,2048]{1,0:T(8,128)(2,1)} %get-tuple-element.145.refs_1_.refs_3_, bf16[128,2048]{1,0:T(8,128)(2,1)} %copy-done.3, ...), custom_call_target="tpu_custom_call" | custom-call | flops 1 | bytes 1 | tf_op jit(solution)/shard_map/pallas_call | solution.py:68
  229.9 27.1 %all-gather.11.cloned.1.call-done.refs_9_.refs_8_.refs_2_ = bf16[704,2048]{1,0:T(8,128)(2,1)} async-done(((bf16[176,2048]{1,0:T(8,128)(2,1)}), bf16[704,2048]{1,0:T(8,128)(2,1)}) %all-gather.11.cloned.1.call-update) | async-done | bytes 2883600 | tf_op jit(solution)/shard_map/all_gather | solution.py:655
  283.5 10.8 %shard_map.219 = (bf16[1024,704]{1,0:T(8,128)(2,1)}, bf16[1024,704]{1,0:T(8,128)(2,1)}) custom-call(bf16[128,2048]{1,0:T(8,128)(2,1)} %copy-done.2, bf16[128,2048]{1,0:T(8,128)(2,1)} %copy-done.1, bf16[128,2048]{1,0:T(8,128)(2,1)} %copy-done.10, bf16[128,2048]{1,0:T(8,128)(2,1)} %collective-permute-done.40.refs_4_.refs_3_, bf16[128,2048]{1,0:T(8,128)(2,1)} %copy-done.12, ...), custom_call_target="tpu_custom_call" | custom-call | flops 1 | bytes 1 | tf_op jit(solution)/shard_map/pallas_call | solution.py:68
  294.3 12.7 %shard_map.220.refs_15_ = bf16[1408,2048]{1,0:T(8,128)(2,1)} custom-call(bf16[1024,704]{1,0:T(8,128)(2,1)} %get-tuple-element.160.refs_0_.refs_11_, bf16[1024,704]{1,0:T(8,128)(2,1)} %get-tuple-element.161.refs_1_.refs_12_, bf16[128,2048]{1,0:T(8,128)(2,1)} %get-tuple-element.144.refs_0_.refs_2_, bf16[128,2048]{1,0:T(8,128)(2,1)} %get-tuple-element.145.refs_1_.refs_3_, ...), custom_call_target="tpu_custom_call" | custom-call | flops 1 | bytes 1 | tf_op jit(solution)/shard_map/pallas_call | solution.py:68
  307.2 25.2 %shard_map.221 = (bf16[1024,704]{1,0:T(8,128)(2,1)}, bf16[1024,704]{1,0:T(8,128)(2,1)}, bf16[128,2048]{1,0:T(8,128)(2,1)}, bf16[128,2048]{1,0:T(8,128)(2,1)}, bf...) custom-call(bf16[128,2048]{1,0:T(8,128)(2,1)} %copy-done.2, ...), custom_call_target="tpu_custom_call" | custom-call | flops 1 | bytes 1 | tf_op jit(solution)/shard_map/pallas_call | solution.py:68
  332.4 14.4 %shard_map.222.refs_4_ = bf16[1408,2048]{1,0:T(8,128)(2,1)} custom-call(bf16[1024,704]{1,0:T(8,128)(2,1)} %get-tuple-element.168.refs_0_, bf16[1024,704]{1,0:T(8,128)(2,1)} %get-tuple-element.169.refs_1_, bf16[128,2048]{1,0:T(8,128)(2,1)} %get-tuple-element.144.refs_0_.refs_2_, bf16[128,2048]{1,0:T(8,128)(2,1)} %get-tuple-element.145.refs_1_.refs_3_, ...), custom_call_target="tpu_custom_call" | custom-call | flops 1 | bytes 1 | tf_op jit(solution)/shard_map/pallas_call | solution.py:68
  349.9 12.3 %reduce-scatter.5.cloned.1.call-done = bf16[176,2048]{1,0:T(8,128)(2,1)} async-done(((bf16[704,2048]{1,0:T(8,128)(2,1)}), bf16[176,2048]{1,0:T(8,128)(2,1)}) %reduce-scatter.5.cloned.1.call-update) | async-done | bytes 720912 | tf_op jit(solution)/shard_map/reduce_scatter | solution.py:658
  380.5 10.3 %collective-permute-done.49.refs_6_ = bf16[128,2048]{1,0:T(8,128)(2,1)S(1)} collective-permute-done((bf16[128,2048]{1,0:T(8,128)(2,1)}, bf16[128,2048]{1,0:T(8,128)(2,1)S(1)}, u32[]{:S(2)}, u32[]{:S(2)}) %collective-permute-start.49) | collective-permute-done | bytes 524320 | tf_op jit(solution)/shard_map/ppermute | solution.py:643
  417.1 20.8 %shard_map.227 = (bf16[256,2304]{1,0:T(8,128)(2,1)}, f32[256,256]{1,0:T(8,128)}) custom-call(s32[2]{0:T(128)} %pad_add_fusion.refs_0_, f32[1]{0:T(128)} %bitcast.11.refs_0_.refs_1_, bf16[256,2048]{1,0:T(8,128)(2,1)} %get-tuple-element.174.refs_1_.refs_2_, bf16[256,256]{1,0:T(8,128)(2,1)} %refs_3_.3, bf16[256,2048]{1,0:T(8,128)(2,1)} %get-tuple-element.119.refs_1_.refs_4_, ...), custom_call_target="tpu_custom_call" | custom-call | flops 1 | bytes 1 | tf_op jit(solution)/shard_map/pallas_call | solution.py:68
  448.1 12.8 %shard_map.230 = (f32[256,2048]{1,0:T(8,128)}, f32[8,2048]{1,0:T(8,128)}) custom-call(s32[2]{0:T(128)} %pad_add_fusion.refs_0_, bf16[256,2048]{1,0:T(8,128)(2,1)} %refs_1_.5, f32[8,2048]{1,0:T(8,128)} %get-tuple-element.122.refs_3_.refs_2_, bf16[256,2304]{1,0:T(8,128)(2,1)} %get-tuple-element.178.refs_1_.refs_4_.refs_3_, ...), custom_call_target="tpu_custom_call" | custom-call | flops 1 | bytes 1 | tf_op jit(solution)/shard_map/pallas_call | solution.py:68
  481.3 10.5 %collective-permute-done.75 = bf16[128,2048]{1,0:T(8,128)(2,1)} collective-permute-done((bf16[128,2048]{1,0:T(8,128)(2,1)}, bf16[128,2048]{1,0:T(8,128)(2,1)}, u32[]{:S(2)}, u32[]{:S(2)}) %collective-permute-start.75) | collective-permute-done | bytes 524320 | tf_op jit(solution)/shard_map/ppermute | solution.py:643
  514.5 11.1 %shard_map.233 = (bf16[128,2048]{1,0:T(8,128)(2,1)}, bf16[128,2048]{1,0:T(8,128)(2,1)}, bf16[128,2048]{1,0:T(8,128)(2,1)}, bf16[128,2048]{1,0:T(8,128)(2,1)}, bf...) custom-call(bf16[1024,704]{1,0:T(8,128)(2,1)} %get-tuple-element.150, ...), custom_call_target="tpu_custom_call" | custom-call | flops 1 | bytes 1 | tf_op jit(solution)/shard_map/pallas_call | solution.py:68
  536.0 13.8 %collective-permute-done.69 = bf16[128,2304]{1,0:T(8,128)(2,1)S(1)} collective-permute-done((bf16[128,2304]{1,0:T(8,128)(2,1)}, bf16[128,2304]{1,0:T(8,128)(2,1)S(1)}, u32[]{:S(2)}, u32[]{:S(2)}) %collective-permute-start.69) | collective-permute-done | bytes 589856 | tf_op jit(solution)/shard_map/ppermute | solution.py:646
  (336 shorter events, 254.9 us)
Async XLA Ops:
  7.2 37.6 %all-gather.5.cloned.1.call-start = ((), (), s32[]{:S(2)}) async-start(), calls=%async_computation.4 | async-start | bytes 1556480 | tf_op jit(solution)/shard_map/all_gather | solution.py:655
  9.8 82.5 %all-gather.7.cloned.1.call-start = ((), (), s32[]{:S(2)}) async-start(), calls=%async_computation.5 | async-start | bytes 1310720 | tf_op jit(solution)/shard_map/all_gather | solution.py:655
  10.5 188.3 %all-gather.9.cloned.1.call-start = ((), (), s32[]{:S(2)}) async-start(), calls=%async_computation.6 | async-start | bytes 7208960 | tf_op jit(solution)/shard_map/all_gather | solution.py:655
  31.2 225.7 %all-gather.11.cloned.1.call-start = ((), (), s32[]{:S(2)}) async-start(), calls=%async_computation.7 | async-start | bytes 3604480 | tf_op jit(solution)/shard_map/all_gather | solution.py:655
  64.4 27.9 %collective-permute-start.8 = (bf16[2,64,2432]{2,1,0:T(8,128)(2,1)}, bf16[2,64,2432]{2,1,0:T(8,128)(2,1)}, u32[]{:S(2)}, u32[]{:S(2)}) collective-permute-start(bf16[2,64,2432]{2,1,0:T(8,128)(2,1)} %collective-permute-done.4.refs_8_.refs_9_), channel_id=1, source_target_pairs={{0,1},{1,0},{2,3},{3,2},{4,5},{5,4},{6,7},{7,6},{8,9},{9,8},{10,11... | collective-permute-start | bytes 1867784 | tf_op jit(solution)/shard_map/ppermute | solution.py:646
  64.9 27.3 %collective-permute-start.11 = (bf16[2,64,2432]{2,1,0:T(8,128)(2,1)S(1)}, bf16[2,64,2432]{2,1,0:T(8,128)(2,1)}, u32[]{:S(2)}, u32[]{:S(2)}) collective-permute-start(bf16[2,64,2432]{2,1,0:T(8,128)(2,1)S(1)} %bitcast.22), channel_id=1, source_target_pairs={{0,8},{8,0},{16,24},{24,16},{1,9},{9,1},{17,25},{25,17},{2,10},{10... | collective-permute-start | bytes 1867784 | tf_op jit(solution)/shard_map/ppermute | solution.py:634
  64.9 28.7 %collective-permute-start.7 = (bf16[2,64,2432]{2,1,0:T(8,128)(2,1)S(1)}, bf16[2,64,2432]{2,1,0:T(8,128)(2,1)}, u32[]{:S(2)}, u32[]{:S(2)}) collective-permute-start(bf16[2,64,2432]{2,1,0:T(8,128)(2,1)S(1)} %bitcast.23), channel_id=1, source_target_pairs={{0,16},{8,24},{16,0},{24,8},{1,17},{9,25},{17,1},{25,9},{2,18},{10... | collective-permute-start | bytes 1867784 | tf_op jit(solution)/shard_map/ppermute | solution.py:643
  174.8 23.2 %collective-permute-start.36 = (bf16[128,2048]{1,0:T(8,128)(2,1)S(1)}, bf16[128,2048]{1,0:T(8,128)(2,1)S(1)}, u32[]{:S(2)}, u32[]{:S(2)}) collective-permute-start(bf16[128,2048]{1,0:T(8,128)(2,1)S(1)} %collective-permute-done.32.refs_2_.refs_4_), channel_id=1, source_target_pairs={{0,1},{1,0},{2,3},{3,2},{4,5},{5,4},{6,7},{7,6},{8,9},{9,8},{10,11... | collective-permute-start | bytes 1572872 | tf_op jit(solution)/shard_map/ppermute | solution.py:646
  198.9 163.4 %reduce-scatter.5.cloned.1.call-start = ((), (), s32[]{:S(2)}) async-start(), calls=%async_computation.8 | async-start | bytes 3604480 | tf_op jit(solution)/shard_map/reduce_scatter | solution.py:658
  199.1 29.9 %collective-permute-start.41 = (bf16[128,2048]{1,0:T(8,128)(2,1)S(1)}, bf16[128,2048]{1,0:T(8,128)(2,1)S(1)}, u32[]{:S(2)}, u32[]{:S(2)}) collective-permute-start(bf16[128,2048]{1,0:T(8,128)(2,1)S(1)} %get-tuple-element.154.refs_1_.refs_0_), channel_id=1, source_target_pairs={{0,1},{1,0},{2,3},{3,2},{4,5},{5,4},{6,7},{7,6},{8,9},{9,8},{10,11... | collective-permute-start | bytes 1572872 | tf_op jit(solution)/shard_map/ppermute | solution.py:646
  200.2 29.6 %collective-permute-start.40 = (bf16[128,2048]{1,0:T(8,128)(2,1)S(1)}, bf16[128,2048]{1,0:T(8,128)(2,1)}, u32[]{:S(2)}, u32[]{:S(2)}) collective-permute-start(bf16[128,2048]{1,0:T(8,128)(2,1)S(1)} %get-tuple-element.155.refs_2_.refs_1_), channel_id=1, source_target_pairs={{0,16},{8,24},{16,0},{24,8},{1,17},{9,25},{17,1},{25,9},{2,18},{10... | collective-permute-start | bytes 1572872 | tf_op jit(solution)/shard_map/ppermute | solution.py:643
  306.9 25.5 %collective-permute-start.46 = (bf16[1408,2048]{1,0:T(8,128)(2,1)}, bf16[1408,2048]{1,0:T(8,128)(2,1)}, u32[]{:S(2)}, u32[]{:S(2)}) collective-permute-start(bf16[1408,2048]{1,0:T(8,128)(2,1)} %shard_map.220.refs_15_), channel_id=1, source_target_pairs={{0,8},{8,0},{16,24},{24,16},{1,9},{9,1},{17,25},{25,17},{2,10},{10... | collective-permute-start | bytes 17301512 | tf_op jit(solution)/shard_map/ppermute | solution.py:634
  307.2 159.4 %reduce-scatter.7.cloned.1.call-start = ((), (), s32[]{:S(2)}) async-start(), calls=%async_computation.9 | async-start | bytes 7208960 | tf_op jit(solution)/shard_map/reduce_scatter | solution.py:658
  346.8 205.7 %reduce-scatter.11.cloned.1.call-start = ((), (), s32[]{:S(2)}) async-start(), calls=%async_computation.11 | async-start | bytes 1310720 | tf_op jit(solution)/shard_map/reduce_scatter | solution.py:658
  443.6 25.0 %collective-permute-start.53 = (bf16[1024,2304]{1,0:T(8,128)(2,1)}, bf16[1024,2304]{1,0:T(8,128)(2,1)}, u32[]{:S(2)}, u32[]{:S(2)}) collective-permute-start(bf16[1024,2304]{1,0:T(8,128)(2,1)} %shard_map.228.refs_21_), channel_id=1, source_target_pairs={{0,8},{8,0},{16,24},{24,16},{1,9},{9,1},{17,25},{25,17},{2,10},{10... | collective-permute-start | bytes 14155784 | tf_op jit(solution)/shard_map/ppermute | solution.py:634
  446.8 30.8 %collective-permute-start.73 = (bf16[128,2048]{1,0:T(8,128)(2,1)S(1)}, bf16[128,2048]{1,0:T(8,128)(2,1)S(1)}, u32[]{:S(2)}, u32[]{:S(2)}) collective-permute-start(bf16[128,2048]{1,0:T(8,128)(2,1)S(1)} %copy-done.50), channel_id=1, source_target_pairs={{0,1},{1,0},{2,3},{3,2},{4,5},{5,4},{6,7},{7,6},{8,9},{9,8},{10,11... | collective-permute-start | bytes 1572872 | tf_op jit(solution)/shard_map/ppermute | solution.py:646
  467.2 24.5 %collective-permute-start.75 = (bf16[128,2048]{1,0:T(8,128)(2,1)}, bf16[128,2048]{1,0:T(8,128)(2,1)}, u32[]{:S(2)}, u32[]{:S(2)}) collective-permute-start(bf16[128,2048]{1,0:T(8,128)(2,1)} %get-tuple-element.211), channel_id=1, source_target_pairs={{0,16},{8,24},{16,0},{24,8},{1,17},{9,25},{17,1},{25,9},{2,18},{10... | collective-permute-start | bytes 1572872 | tf_op jit(solution)/shard_map/ppermute | solution.py:643
  468.7 23.1 %collective-permute-start.76 = (bf16[128,2048]{1,0:T(8,128)(2,1)}, bf16[128,2048]{1,0:T(8,128)(2,1)}, u32[]{:S(2)}, u32[]{:S(2)}) collective-permute-start(bf16[128,2048]{1,0:T(8,128)(2,1)} %get-tuple-element.212), channel_id=1, source_target_pairs={{0,1},{1,0},{2,3},{3,2},{4,5},{5,4},{6,7},{7,6},{8,9},{9,8},{10,11... | collective-permute-start | bytes 1572872 | tf_op jit(solution)/shard_map/ppermute | solution.py:646
  471.3 37.5 %collective-permute-start.71 = (f32[2,2048]{1,0:T(2,128)S(1)}, f32[2,2048]{1,0:T(2,128)S(1)}, u32[]{:S(2)}, u32[]{:S(2)}) collective-permute-start(f32[2,2048]{1,0:T(2,128)S(1)} %fusion.9), channel_id=1, source_target_pairs={{0,16},{8,24},{16,0},{24,8},{1,17},{9,25},{17,1},{25,9},{2,18},{10... | collective-permute-start | bytes 49160 | tf_op jit(solution)/shard_map/ppermute | solution.py:643
  493.2 33.8 %collective-permute-start.66 = (bf16[128,2304]{1,0:T(8,128)(2,1)}, bf16[128,2304]{1,0:T(8,128)(2,1)S(1)}, u32[]{:S(2)}, u32[]{:S(2)}) collective-permute-start(bf16[128,2304]{1,0:T(8,128)(2,1)} %get-tuple-element.204), channel_id=1, source_target_pairs={{0,1},{1,0},{2,3},{3,2},{4,5},{5,4},{6,7},{7,6},{8,9},{9,8},{10,11... | collective-permute-start | bytes 1769480 | tf_op jit(solution)/shard_map/ppermute | solution.py:646
  508.5 74.4 %reduce-scatter.9.cloned.1.call-start = ((), (), s32[]{:S(2)}) async-start(), calls=%async_computation.10 | async-start | bytes 1556480 | tf_op jit(solution)/shard_map/reduce_scatter | solution.py:658
  512.9 23.1 %collective-permute-start.68 = (bf16[128,2304]{1,0:T(8,128)(2,1)}, bf16[128,2304]{1,0:T(8,128)(2,1)S(1)}, u32[]{:S(2)}, u32[]{:S(2)}) collective-permute-start(bf16[128,2304]{1,0:T(8,128)(2,1)} %get-tuple-element.206), channel_id=1, source_target_pairs={{0,16},{8,24},{16,0},{24,8},{1,17},{9,25},{17,1},{25,9},{2,18},{10... | collective-permute-start | bytes 1769480 | tf_op jit(solution)/shard_map/ppermute | solution.py:643
  525.6 30.9 %collective-permute-start.61 = (bf16[128,2048]{1,0:T(8,128)(2,1)}, bf16[128,2048]{1,0:T(8,128)(2,1)S(1)}, u32[]{:S(2)}, u32[]{:S(2)}) collective-permute-start(bf16[128,2048]{1,0:T(8,128)(2,1)} %get-tuple-element.194), channel_id=1, source_target_pairs={{0,1},{1,0},{2,3},{3,2},{4,5},{5,4},{6,7},{7,6},{8,9},{9,8},{10,11... | collective-permute-start | bytes 1572872 | tf_op jit(solution)/shard_map/ppermute | solution.py:646
  526.2 30.3 %collective-permute-start.62 = (bf16[128,2048]{1,0:T(8,128)(2,1)}, bf16[128,2048]{1,0:T(8,128)(2,1)}, u32[]{:S(2)}, u32[]{:S(2)}) collective-permute-start(bf16[128,2048]{1,0:T(8,128)(2,1)} %get-tuple-element.196), channel_id=1, source_target_pairs={{0,16},{8,24},{16,0},{24,8},{1,17},{9,25},{17,1},{25,9},{2,18},{10... | collective-permute-start | bytes 1572872 | tf_op jit(solution)/shard_map/ppermute | solution.py:643
  (119 other events, 1856.5 us)
Sparse Core Ops, SparseCore 0:
  10.2 34.2 all-gather.4
  46.0 26.9 all-gather.6
  75.2 106.1 all-gather.8
  199.0 57.9 all-gather.10
  307.3 54.9 reduce-scatter.4
  364.4 102.0 reduce-scatter.6
  508.6 26.2 reduce-scatter.10
  551.3 28.2 reduce-scatter.8

commit v3 on v2

--- a/solution.py
+++ b/solution.py
@@ -73,9 +73,39 @@
             scratch_shapes=scratch,
             compiler_params=pltpu.CompilerParams(vmem_limit_bytes=vmem_limit),
             cost_estimate=pl.CostEstimate(flops=1, bytes_accessed=1, transcendentals=0),
+            name=getattr(body, "func", body).__name__[: -len("_body")],
         )(*operands)
 
     return run
+
+
+def route(keys):
+    place = {(key, half): 2 * i + half for i, key in enumerate(keys) for half in range(2)}
+    own, x, y, both = (0, 0), (1, 0), (0, 1), (1, 1)
+    return (
+        (place[own, 0],),
+        (place[own, 1],),
+        (place[x, 0],),
+        (place[y, 1],),
+        (place[both, 1], place[x, 1]),
+        (place[both, 0], place[y, 0]),
+    )
+
+
+row_route = route(((0, 0), (1, 0), (0, 1), (1, 1)))
+column_route = route(((0, 0), (0, 1), (1, 0), (1, 1)))
+
+
+def routed(size, columns):
+    return tuple(
+        jax.ShapeDtypeStruct((size * len(blocks), columns), bf16) for blocks in row_route
+    )
+
+
+def store_routed(way, outs, size, block):
+    for blocks, out in zip(way, outs):
+        for spot, place in enumerate(blocks):
+            out[spot * size : (spot + 1) * size, :] = block(place).astype(bf16)
 
 
 class Pieces:
@@ -270,7 +300,7 @@
     for part in range(2):
         rows = pl.ds(part * half, half)
         terms = sums[3 * part : 3 * part + 3]
-        d_h = terms[0][...].astype(f32) + terms[1][...].astype(f32) + terms[2][...].astype(f32)
+        d_h = terms[0][...].astype(f32) + terms[1][half:, :].astype(f32) + terms[2][...].astype(f32)
         x_mid = mid[rows, :]
         inverse = lax.rsqrt(jnp.mean(x_mid * x_mid, axis=-1, keepdims=True) + epsilon)
         normed = x_mid * inverse
@@ -475,149 +505,141 @@
     )(*parts, weight, *scales, *late)
 
 
-def rows_back_body(shard, count, *refs):
-    parts, weight, scales, others, boths = (
-        refs[:count], refs[count], refs[count + 1 : count + 3], refs[count + 3 : count + 5],
-        refs[count + 5 : count + 7],
-    )
-    refs = refs[count + 7 :]
-    grads, outs = refs[:2], refs[2 : 2 + count]
-    rows, weights, sems = refs[2 + count], refs[3 + count : 7 + count], refs[7 + count]
-    row_wait = fetch_rows(parts, rows, sems.at[0])
+def rows_back_body(shard, size, *refs):
+    grads, boths, outs = refs[:4], refs[4:6], refs[6:12]
+    weights, sems = refs[12:16], refs[16]
     waits = []
     for place in range(2):
         waits += fetch_gate_up(
             boths[place], shard, weights[2 * place], weights[2 * place + 1],
-            sems.at[1 + 2 * place], sems.at[2 + 2 * place],
+            sems.at[2 * place], sems.at[2 * place + 1],
         )
-    row_wait()
-    d_hidden(rows, weight, scales, grads)
     for wait in waits:
         wait()
-    size = outs[0].shape[0]
-    for place, out in enumerate(outs):
+
+    def block(place):
         own = pl.ds(place * size, size)
         total = jnp.dot(grads[0][own, :], weights[0][...], preferred_element_type=f32)
-        for grad, piece in zip((grads[1], *others), weights[1:]):
+        for grad, piece in zip(grads[1:], weights[1:]):
             total += jnp.dot(grad[own, :], piece[...], preferred_element_type=f32)
-        out[...] = total.astype(bf16)
-
-
-def rows_back(parts, weight, scales, others, boths, shard, late=()):
-    count = len(parts)
-    total, width = sum(part.shape[0] for part in parts), parts[0].shape[1]
-    hidden = weight.shape[0]
-    shape = jax.ShapeDtypeStruct
-    outs = kernel_call(
-        functools.partial(rows_back_body, shard, count),
-        (shape((total, hidden), bf16),) * 2 + tuple(shape(part.shape, bf16) for part in parts),
-        [pltpu.VMEM((total, width), bf16)]
-        + [pltpu.VMEM((hidden, width), bf16)] * 4
-        + [pltpu.SemaphoreType.DMA((5,))],
-        [any_spec()] * count + [vmem_spec()] * 5 + [any_spec()] * 2,
-    )(*parts, weight, *scales, *others, *boths, *late)
-    return outs[:2], outs[2:]
-
-
-def down_body(count, *refs):
+        return total
+
+    store_routed(row_route, outs, size, block)
+
+
+def rows_back(grads, boths, shard, late=()):
+    total, hidden = grads[0].shape
+    width = boths[0].shape[1]
+    return kernel_call(
+        functools.partial(rows_back_body, shard, total // 8),
+        routed(total // 8, width),
+        [pltpu.VMEM((hidden, width), bf16)] * 4 + [pltpu.SemaphoreType.DMA((4,))],
+        [vmem_spec()] * 4 + [any_spec()] * 2,
+    )(*grads, *boths, *late)
+
+
+def down_body(size, *refs):
     hids, downs, outs = refs[:2], refs[2:4], refs[4:]
-    size = outs[0].shape[0]
-    for place, out in enumerate(outs):
+
+    def block(place):
         own = pl.ds(place * size, size)
         total = jnp.dot(hids[0][own, :], downs[0][...], preferred_element_type=f32)
-        total += jnp.dot(hids[1][own, :], downs[1][...], preferred_element_type=f32)
-        out[...] = total.astype(bf16)
-
-
-def down(hids, downs, count, late=()):
+        return total + jnp.dot(hids[1][own, :], downs[1][...], preferred_element_type=f32)
+
+    store_routed(row_route, outs, size, block)
+
+
+def down(hids, downs, late=()):
     total, width = hids[0].shape[0], downs[0].shape[1]
     return kernel_call(
-        functools.partial(down_body, count),
-        (jax.ShapeDtypeStruct((total // count, width), bf16),) * count,
-        [],
-        [vmem_spec()] * 4,
+        functools.partial(down_body, total // 8), routed(total // 8, width), [], [vmem_spec()] * 4
     )(*hids, *downs, *late)
 
 
-def hidden_sums_body(count, pairs, shard, received, *refs):
+def hidden_sums_body(count, pairs, shard, pieces, received, *refs):
     lefts, parts = refs[:pairs], refs[pairs : pairs + count]
-    other = refs[pairs + count] if received else None
-    out, rows, sem = refs[-3], refs[-2], refs[-1]
+    others = refs[pairs + count : pairs + count + pieces * received]
+    refs = refs[pairs + count + pieces * received :]
+    outs, rows, sem = refs[:-2], refs[-2], refs[-1]
     fetch_rows(parts, rows, sem)()
     for place, left in enumerate(lefts):
         product = contract_first(left[...], rows[...])
         for outer in range(left.shape[1] // shard):
-            target = pl.ds((pairs * outer + place) * shard, shard)
+            start = (pairs * outer + place) * shard
             own = product[outer * shard : (outer + 1) * shard]
             if received:
-                own = own + other[target, :].astype(f32)
-            out[target, :] = own.astype(bf16)
-
-
-def hidden_sums(lefts, parts, shard, other=None, late=()):
+                piece, row = start // others[0].shape[0], start % others[0].shape[0]
+                outs[0][start : start + shard, :] = (
+                    own + others[piece][row : row + shard, :].astype(f32)
+                ).astype(bf16)
+            else:
+                piece, row = start // outs[0].shape[0], start % outs[0].shape[0]
+                outs[piece][row : row + shard, :] = own.astype(bf16)
+
+
+def hidden_sums(lefts, parts, shard, pieces, others=None, late=()):
     total, width = lefts[0].shape[0], parts[0].shape[1]
     hidden = lefts[0].shape[1] * len(lefts)
-    received = other is not None
-    return kernel_call(
-        functools.partial(hidden_sums_body, len(parts), len(lefts), shard, received),
-        jax.ShapeDtypeStruct((hidden, width), bf16),
+    received = others is not None
+    count = 1 if received else pieces
+    outs = kernel_call(
+        functools.partial(hidden_sums_body, len(parts), len(lefts), shard, pieces, received),
+        (jax.ShapeDtypeStruct((hidden // count, width), bf16),) * count,
         [pltpu.VMEM((total, width), bf16), pltpu.SemaphoreType.DMA],
-        [vmem_spec()] * len(lefts) + [any_spec()] * len(parts) + [vmem_spec()] * received,
-    )(*lefts, *parts, *((other,) if received else ()), *late)
-
-
-def send_sums_body(turned, right, out):
-    middle = turned.shape[0] // 2
-
-    @pl.loop(0, middle // step)
-    def _(block):
-        start = pl.multiple_of(block * step, step)
-        product = jnp.dot(turned[pl.ds(middle + start, step), :], right[...], preferred_element_type=f32)
-        out[pl.ds(start, step), :] = product.astype(bf16)
+        [vmem_spec()] * len(lefts) + [any_spec()] * len(parts) + [vmem_spec()] * (pieces * received),
+    )(*lefts, *parts, *(others or ()), *late)
+    return outs[0] if received else outs
+
+
+def send_sums_body(turned, right, *outs):
+    middle, size = turned.shape[0] // 2, outs[0].shape[0]
+    for place, out in enumerate(outs):
+        own = pl.ds(middle + place * size, size)
+        out[...] = jnp.dot(turned[own, :], right[...], preferred_element_type=f32).astype(bf16)
 
 
 def send_sums(turned, right, late=()):
     return kernel_call(
         send_sums_body,
-        jax.ShapeDtypeStruct((turned.shape[0] // 2, right.shape[1]), bf16),
+        (jax.ShapeDtypeStruct((turned.shape[0] // 4, right.shape[1]), bf16),) * 2,
         [],
         [vmem_spec()] * 2,
     )(turned, right, *late)
 
 
-def keep_sums_body(turned, right, other, *outs):
-    size = outs[0].shape[0]
-    for place, out in enumerate(outs):
+def keep_sums_body(turned, right, *refs):
+    others, outs = refs[:2], refs[2:]
+    size = turned.shape[0] // 16
+
+    def block(place):
         own = pl.ds(place * size, size)
+        half = pl.ds((place % 4) * size, size)
         product = jnp.dot(turned[own, :], right[...], preferred_element_type=f32)
-        out[...] = (product + other[own, :].astype(f32)).astype(bf16)
-
-
-def keep_sums(turned, right, other, late=()):
-    size = turned.shape[0] // 16
-    outs = kernel_call(
+        return product + others[place // 4][half, :].astype(f32)
+
+    store_routed(column_route, outs, size, block)
+
+
+def keep_sums(turned, right, others, late=()):
+    return kernel_call(
         keep_sums_body,
-        (jax.ShapeDtypeStruct((size, right.shape[1]), bf16),) * 8,
+        routed(turned.shape[0] // 16, right.shape[1]),
         [],
-        [vmem_spec()] * 3,
-    )(turned, right, other, *late)
-    return {
-        (dx, dy): (outs[4 * dx + 2 * dy], outs[4 * dx + 2 * dy + 1])
-        for dx in range(2)
-        for dy in range(2)
-    }
-
-
-def pass_body(a, b, c, d, first, second):
-    first[...] = (a[...].astype(f32) + b[...].astype(f32)).astype(bf16)
-    second[...] = (c[...].astype(f32) + d[...].astype(f32)).astype(bf16)
-
-
-def add_pairs(a, b, c, d, late=()):
-    shape = jax.ShapeDtypeStruct
-    return kernel_call(
-        pass_body, (shape(a.shape, bf16), shape(c.shape, bf16)), [], [vmem_spec()] * 4
-    )(a, b, c, d, *late)
+        [vmem_spec()] * 4,
+    )(turned, right, *others, *late)
+
+
+def pass_body(keep_x, keep_y, from_x, from_y, for_x, for_y):
+    size = keep_x.shape[0]
+    for_x[...] = (keep_x[...].astype(f32) + from_y[:size, :].astype(f32)).astype(bf16)
+    for_y[...] = (keep_y[...].astype(f32) + from_x[:size, :].astype(f32)).astype(bf16)
+
+
+def pass_on(keep_x, keep_y, from_x, from_y, late=()):
+    out = jax.ShapeDtypeStruct(keep_x.shape, bf16)
+    return kernel_call(pass_body, (out, out), [], [vmem_spec()] * 4)(
+        keep_x, keep_y, from_x, from_y, *late
+    )
 
 
 class Grid:
@@ -633,17 +655,29 @@
     def core(self, value):
         return lax.ppermute(value, "dp", [(i, i ^ 1) for i in range(self.dp)])
 
+    def cores(self, values):
+        return [self.core(value) for value in values]
+
     def echo(self, value, times):
-        corner = value[:8, :lanes]
         for _ in range(times):
-            corner = self.core(corner)
-        return corner
+            value = self.core(value)
+        return value
 
     def x_swap(self, value):
         return lax.ppermute(value, "dp", [(i, i ^ 2) for i in range(self.dp)])
 
     def y_swap(self, value):
         return lax.ppermute(value, "fsdp", [(i, i ^ 1) for i in range(self.fsdp)])
+
+    def plane_sum(self, value):
+        value = value + self.core(value)
+        pairs = [
+            (dp * self.fsdp + f, (dp ^ 2) * self.fsdp + (f ^ 1))
+            for dp in range(self.dp)
+            for f in range(self.fsdp)
+        ]
+        across = lax.ppermute(value, ("dp", "fsdp"), pairs)
+        return value + self.x_swap(value) + self.y_swap(value) + across
 
     def shift(self, value, low, high, by):
         pairs = [
@@ -678,19 +712,13 @@
         }
 
     def collect_first(self, parts, late=()):
-        first_xy = self.y_swap(parts[1, 1][0])
-        second_xy = self.x_swap(parts[1, 1][1])
-        first_y = self.y_swap(parts[0, 1][0])
-        second_x = self.x_swap(parts[1, 0][1])
-        for_x, for_y = add_pairs(parts[1, 0][0], first_xy, parts[0, 1][1], second_xy, late)
-        return for_x, for_y, first_y, second_x
+        _, _, keep_x, keep_y, to_x, to_y = parts
+        from_x, from_y = self.x_swap(to_x), self.y_swap(to_y)
+        return (*pass_on(keep_x, keep_y, from_x, from_y, late), from_x, from_y)
 
     def collect_second(self, parts, passed):
-        for_x, for_y, first_y, second_x = passed
-        return (
-            (parts[0, 0][0], first_y, self.x_swap(for_x)),
-            (parts[0, 0][1], second_x, self.y_swap(for_y)),
-        )
+        for_x, for_y, from_x, from_y = passed
+        return (parts[0], from_y, self.x_swap(for_x)), (parts[1], from_x, self.y_swap(for_y))
 
     def pieces(self, planes, rows, token=None):
         keys = [(dx, dy) for dx in range(2) for dy in range(2)]
@@ -699,10 +727,12 @@
         theirs = [self.core(half) for half in sent]
         return Pieces(self.depth, rows, mine[0].shape[-1], mine + theirs)
 
-    def column(self, sums):
-        halves = [sum(term.astype(f32) for term in terms) for terms in sums]
-        column = jnp.concatenate(halves, axis=0).astype(bf16)
-        return column.reshape(-1, column.shape[-1])
+    def total(self, sums):
+        halves = []
+        for own, middle, last in sums:
+            middle = middle[own.shape[0] :]
+            halves.append(own.astype(f32) + middle.astype(f32) + last.astype(f32))
+        return jnp.concatenate(halves, axis=0)
 
 
 def local(
@@ -739,23 +769,20 @@
     def in_order(planes):
         return [piece for key in plane_keys for piece in planes[key]]
 
-    def by_key(blocks):
-        return {key: (blocks[2 * i], blocks[2 * i + 1]) for i, key in enumerate(plane_keys)}
-
     gains = jnp.stack([g_attn, g_mlp], axis=1)
     w_in = jnp.concatenate([w_q, w_kv, jnp.pad(gains, ((0, 0), (0, lanes - 2)))], axis=1)
     w_in_column = grid.gather_outer(w_in)
-    w_o_column = grid.gather_outer(after(w_o, w_in))
+    w_o_column = grid.gather_outer(w_o)
     grad_first = grid.spread_first(grad_low[:half], grad_low[half:])
     pairs = jnp.swapaxes(w_gu, 0, 1).reshape(2 * hidden_rows, width)
-    gu_mine = grid.gather_outer(after(pairs, grad_first[2:]))
+    gu_mine = grid.gather_outer(pairs)
     grad_planes = grid.spread_second(*grad_first)
     grad_rows = in_order(grad_planes)
     cut = grid.depth // 2
     w_in_column = after(w_in_column, grad_planes[1, 1]).reshape(grid.depth, shard_rows, -1)
     in_planes = grid.spread_second(*grid.spread_first(w_in_column[:cut], w_in_column[cut:]))
     in_pieces = grid.pieces(in_planes, shard_rows)
-    down_mine = grid.gather_outer(after(w_down, in_planes[1, 1]))
+    down_mine = grid.gather_outer(w_down)
     w_o_column = after(w_o_column, in_planes[1, 1]).reshape(grid.depth, shard_rows, -1)
     o_first = grid.spread_first(w_o_column[:cut], w_o_column[cut:])
     h_turned, q_low, kv_out, gain_rows = project(
@@ -779,50 +806,52 @@
     gu_other = grid.core(gu_mine)
     hid_mine, *scales_mine = gate(ff_rows, gu_mine, run_rows)
     hid_other, *scales_other = gate(ff_rows, gu_other, run_rows, [hid_mine])
-    sent = hidden_sums([hid_other], grad_rows, run_rows, late=[down_mine])
-    down_sum = hidden_sums([hid_mine], grad_rows, run_rows, grid.core(sent), [sent])
-    d_w_down = grid.scatter_outer(down_sum).astype(f32)
+    runs = grid.depth if by_shard else 1
+    sent = hidden_sums([hid_other], grad_rows, run_rows, runs)
+    down_sum = hidden_sums([hid_mine], grad_rows, run_rows, runs, grid.cores(sent), [sent[0]])
+    down_sum, down_mine = lax.optimization_barrier((down_sum, down_mine))
+    d_w_down = grid.scatter_outer(down_sum)
     down_other = grid.core(down_mine)
-    pair_other = gate_back(grad_rows, down_other, scales_other, [down_sum])
-    sent = hidden_sums(pair_other, ff_rows, run_rows)
-    pair_mine, d_h_blocks = rows_back(
-        grad_rows, down_mine, scales_mine, pair_other, (gu_mine, gu_other), run_rows, [sent]
-    )
-    d_h_parts = by_key(d_h_blocks)
-    pair_sum = hidden_sums(pair_mine, ff_rows, run_rows, grid.core(sent))
-    d_w_gu = grid.scatter_outer(pair_sum if by_shard else turn(pair_sum, grid.depth)).astype(f32)
-    d_h_passed = grid.collect_first(d_h_parts, [pair_sum, grid.echo(d_w_down, 2)])
+    pair_mine = gate_back(grad_rows, down_mine, scales_mine)
+    pair_other = gate_back(grad_rows, down_other, scales_other, [pair_mine[0]])
+    d_h_parts = rows_back((*pair_mine, *pair_other), (gu_mine, gu_other), run_rows)
+    sent = hidden_sums(pair_other, ff_rows, run_rows, 2*runs, late=[d_h_parts[0]])
+    d_h_passed = grid.collect_first(d_h_parts, [sent[0]])
+    pair_sum = hidden_sums(
+        pair_mine, ff_rows, run_rows, 2*runs, grid.cores(sent), [d_h_passed[0]]
+    )
+    pair_sum, d_w_down = lax.optimization_barrier((pair_sum, d_w_down))
+    d_w_gu = grid.scatter_outer(pair_sum if by_shard else turn(pair_sum, grid.depth))
     d_h_first, d_h_second = grid.collect_second(d_h_parts, d_h_passed)
     d_h_sums = [*d_h_first, *d_h_second]
 
     d_mid, d_mid_low, gain_two_sum = norm_back(
-        factor.reshape(1), x_mid, gain_rows, grad_out, d_h_sums
+        factor.reshape(1), x_mid, gain_rows, grad_out, d_h_sums, [pair_sum]
     )
     sent = send_sums(turned, d_mid_low)
-    o_parts = keep_sums(turned, d_mid_low, grid.core(sent))
+    o_parts = keep_sums(turned, d_mid_low, grid.cores(sent))
     joined, d_kv = attend_back(
         grid.spot, factor.reshape(1), d_mid_low, grad_kv, q_low, kv_out,
-        prob, cosines, sines, o_pieces, [o_parts[0, 0][0]],
+        prob, cosines, sines, o_pieces, [o_parts[0]],
     )
     o_passed = grid.collect_first(o_parts, [joined])
-    sent = send_sums(h_turned, joined)
-    d_w_o = grid.scatter_outer(grid.column(grid.collect_second(o_parts, o_passed))).astype(f32)
-    d_tokens, gain_one_sum = finish(grid.spot, tokens, gain_rows, joined, d_mid, in_pieces, [sent])
-    in_parts = keep_sums(
-        h_turned, joined, grid.core(sent), [o_passed[0], gain_one_sum, grid.echo(d_w_gu, 2)]
-    )
-    in_passed = grid.collect_first(in_parts)
-    d_w_in = grid.column(grid.collect_second(in_parts, in_passed))
-    d_w_gu = jnp.stack([d_w_gu[:hidden_rows], d_w_gu[hidden_rows:]], axis=1)
-    mlp_parts = by_key(
-        down((hid_mine, hid_other), (down_mine, down_other), len(ff_rows), [in_passed[0]])
-    )
-    mlp_sum = grid.collect_second(mlp_parts, grid.collect_first(mlp_parts))
-    mlp_sum = jnp.concatenate([sum(term.astype(f32) for term in terms) for terms in mlp_sum], axis=0)
+    sent = send_sums(h_turned, joined, [o_passed[0]])
+    d_w_o = grid.total(grid.collect_second(o_parts, o_passed)).astype(bf16)
+    d_w_o = grid.scatter_outer(d_w_o).astype(f32)
+    in_parts = keep_sums(h_turned, joined, grid.cores(sent), [o_passed[0]])
+    d_tokens, gain_one_sum = finish(
+        grid.spot, tokens, gain_rows, joined, d_mid, in_pieces, [in_parts[0]]
+    )
+    in_passed = grid.collect_first(in_parts, [gain_one_sum, d_w_gu])
+    d_w_in = grid.total(grid.collect_second(in_parts, in_passed)).astype(bf16)
+    d_w_gu = jnp.stack([d_w_gu[:hidden_rows], d_w_gu[hidden_rows:]], axis=1).astype(f32)
+    d_w_down = d_w_down.astype(f32)
+    mlp_parts = down((hid_mine, hid_other), (down_mine, down_other), [in_passed[0]])
+    d_w_in, mlp_parts = lax.optimization_barrier((d_w_in, mlp_parts))
+    mlp_sum = grid.total(grid.collect_second(mlp_parts, grid.collect_first(mlp_parts)))
     output = (x_mid + mlp_sum).astype(jnp.bfloat16)
     gain_sums = jnp.stack([gain_one_sum[0], gain_two_sum[0]], axis=0)
-    for swap in (grid.core, grid.x_swap, grid.y_swap):
-        gain_sums = gain_sums + swap(gain_sums)
+    gain_sums = grid.plane_sum(gain_sums)
     own_gains = lax.dynamic_slice(
         gain_sums.reshape(2, grid.dp, grid.depth, 2, shard_rows),
         (0, grid.dp_index, 0, grid.y, 0),

time: 602 us -> 556 us (0.924)
  waiting for transfers between devices: 248 us -> 193 us
  Pallas kernels: 228 us -> 236 us
  local copies, waits for them, and re-layouts: 25.6 us -> 32.9 us
    ppermute x25 -> x21, waiting for transfers between devices: 88.6 us -> 49.2 us  [x_swap(): return lax.ppermute(value, 'dp', [(i, i ^ 2) for i in range(self.dp)])]
    all_gather x4, waiting for transfers between devices: 27.1 us -> 3.94 us  [gather_outer(): lax.all_gather(value, 'fsdp', axis=0, tiled=True, axis_index_groups=self....]
    ppermute x25 -> x21, waiting for transfers between devices: 94.9 us -> 111 us  [y_swap(): return lax.ppermute(value, 'fsdp', [(i, i ^ 1) for i in range(self.fsdp)])]
    reduce_scatter x4, waiting for transfers between devices: 12.8 us -> 1.37 us  [scatter_outer(): lax.psum_scatter(value, 'fsdp', scatter_dimension=0, tiled=True, axis_ind...]
    pallas_call x23 -> x24, Pallas kernels: 228 us -> 236 us  [run(): pl.pallas_call(whole_body, out_shape=out_shapes, in_specs=in_specs + [any...]
    unnamed x119 -> x143, local copies, waits for them, and re-layouts: 13.2 us -> 19.5 us
    ppermute x25 -> x21, starting transfers between devices: 26.3 us -> 22.4 us  [y_swap(): return lax.ppermute(value, 'fsdp', [(i, i ^ 1) for i in range(self.fsdp)])]
    ppermute x25 -> x21, starting transfers between devices: 26.4 us -> 23.3 us  [x_swap(): return lax.ppermute(value, 'dp', [(i, i ^ 2) for i in range(self.dp)])]
  transfers between devices with their start and end apart: 85 -> 86, of which waited for: 43 -> 50; matrix products, arithmetic and copies ran while one was open for 5% -> 5% of each run, Pallas kernels for 33% -> 43%
where the time goes in v3:
time: 556 us; the launch traced here: 549 us
  Pallas kernels  236 us (42%)
  waiting for transfers between devices  193 us (35%)
  starting transfers between devices  54 us (10%)
  local copies, waits for them, and re-layouts  32.9 us (6%)
  other arithmetic  18 us (3%)
  between operations  16 us (3%)
    pallas_call x24, Pallas kernels, run(): pl.pallas_call(whole_body, out_shape=out_shapes, in_specs=in_specs + [any...  236 us
    ppermute x21, waiting for transfers between devices, y_swap(): return lax.ppermute(value, 'fsdp', [(i, i ^ 1) for i in range(self.fsdp)])  111 us
    ppermute x21, waiting for transfers between devices, x_swap(): return lax.ppermute(value, 'dp', [(i, i ^ 2) for i in range(self.dp)])  49.2 us
    ppermute x35, waiting for transfers between devices, core(): return lax.ppermute(value, 'dp', [(i, i ^ 1) for i in range(self.dp)])  26.4 us
    ppermute x21, starting transfers between devices, x_swap(): return lax.ppermute(value, 'dp', [(i, i ^ 2) for i in range(self.dp)])  23.3 us
    ppermute x21, starting transfers between devices, y_swap(): return lax.ppermute(value, 'fsdp', [(i, i ^ 1) for i in range(self.fsdp)])  22.4 us
    unnamed x143, local copies, waits for them, and re-layouts  19.5 us
  transfers between devices with their start and end apart: 86, of which 50 were waited for; matrix products, arithmetic and copies ran while one was open for 5% of the time, Pallas kernels for 43%

profile of v3, /device:TPU:0, one launch (start us, length us, event | category | flops | bytes accessed | tf_op | source)
XLA Modules:
  0.0 549.2 jit_solution(4934677974959952120)
XLA Ops:
  20.6 10.4 %collective-permute-done.1.refs_6_.refs_5_ = bf16[128,2048]{1,0:T(8,128)(2,1)S(1)} collective-permute-done((bf16[128,2048]{1,0:T(8,128)(2,1)S(1)}, bf16[128,2048]{1,0:T(8,128)(2,1)S(1)}, u32[]{:S(2)}, u32[]{:S(2)}) %collective-permute-start.1) | collective-permute-done | bytes 524320 | tf_op jit(solution)/shard_map/ppermute | solution.py:670
  34.5 10.6 %collective-permute-done.2.refs_7_.refs_6_ = bf16[128,2048]{1,0:T(8,128)(2,1)S(1)} collective-permute-done((bf16[128,2048]{1,0:T(8,128)(2,1)S(1)}, bf16[128,2048]{1,0:T(8,128)(2,1)S(1)}, u32[]{:S(2)}, u32[]{:S(2)}) %collective-permute-start.2) | collective-permute-done | bytes 524320 | tf_op jit(solution)/shard_map/ppermute | solution.py:670
  50.7 11.2 %collective-permute-done.4.refs_8_.refs_9_ = bf16[2,64,2432]{2,1,0:T(8,128)(2,1)} collective-permute-done((bf16[2,64,2432]{2,1,0:T(8,128)(2,1)S(1)}, bf16[2,64,2432]{2,1,0:T(8,128)(2,1)}, u32[]{:S(2)}, u32[]{:S(2)}) %collective-permute-start.4) | collective-permute-done | bytes 622624 | tf_op jit(solution)/shard_map/ppermute | solution.py:667
  67.5 12.8 %collective-permute-done.6.refs_6_.refs_7_ = bf16[2,64,2432]{2,1,0:T(8,128)(2,1)} collective-permute-done((bf16[2,64,2432]{2,1,0:T(8,128)(2,1)S(1)}, bf16[2,64,2432]{2,1,0:T(8,128)(2,1)}, u32[]{:S(2)}, u32[]{:S(2)}) %collective-permute-start.6) | collective-permute-done | bytes 622624 | tf_op jit(solution)/shard_map/ppermute | solution.py:670
  82.0 11.2 %collective-permute-done.8.refs_10_.refs_11_ = bf16[2,64,2432]{2,1,0:T(8,128)(2,1)} collective-permute-done((bf16[2,64,2432]{2,1,0:T(8,128)(2,1)}, bf16[2,64,2432]{2,1,0:T(8,128)(2,1)}, u32[]{:S(2)}, u32[]{:S(2)}) %collective-permute-start.8) | collective-permute-done | bytes 622624 | tf_op jit(solution)/shard_map/ppermute | solution.py:670
  100.5 13.1 %project.1 = (bf16[2048,256]{1,0:T(8,128)(2,1)}, bf16[256,2048]{1,0:T(8,128)(2,1)}, bf16[256,256]{1,0:T(8,128)(2,1)}, f32[8,2048]{1,0:T(8,128)}) custom-call(s32[2]{0:T(128)} %pad_add_fusion.refs_0_, bf16[256,2048]{1,0:T(8,128)(2,1)} %refs_1_.5, f32[256,128]{1,0:T(8,128)} %get-tuple-element.280.refs_2_.refs_7_, ...), custom_call_target="tpu_custom_call" | custom-call | flops 1 | bytes 1 | tf_op jit(solution)/shard_map/project/pallas_call | solution.py:68
  117.8 11.0 %attend.1 = (bf16[16,256,256]{2,1,0:T(8,128)(2,1)}, bf16[256,2048]{1,0:T(8,128)(2,1)}, bf16[2048,256]{1,0:T(8,128)(2,1)}) custom-call(s32[2]{0:T(128)} %pad_add_fusion.refs_0_, bf16[256,2048]{1,0:T(8,128)(2,1)} %get-tuple-element.135.refs_1_.refs_4_, bf16[256,256]{1,0:T(8,128)(2,1)} %get-tuple-element.258.refs_2_.refs_5_), custom_call_target="tpu_custom_call" | custom-call | flops 1 | bytes 1 | tf_op jit(solution)/shard_map/attend/pallas_call | solution.py:68
  130.1 9.5 %collective-permute-done.23.refs_11_.refs_16_ = bf16[2,64,2048]{2,1,0:T(8,128)(2,1)} collective-permute-done((bf16[2,64,2048]{2,1,0:T(8,128)(2,1)S(1)}, bf16[2,64,2048]{2,1,0:T(8,128)(2,1)}, u32[]{:S(2)}, u32[]{:S(2)}) %collective-permute-start.23) | collective-permute-done | bytes 524320 | tf_op jit(solution)/shard_map/ppermute | solution.py:667
  148.3 10.9 %mix.1 = (f32[256,2048]{1,0:T(8,128)}, bf16[128,2048]{1,0:T(8,128)(2,1)}, bf16[128,2048]{1,0:T(8,128)(2,1)}) custom-call(s32[2]{0:T(128)} %pad_add_fusion.refs_0_, bf16[256,2048]{1,0:T(8,128)(2,1)} %refs_1_.5, bf16[256,2048]{1,0:T(8,128)(2,1)} %get-tuple-element.137.refs_2_, f32[8,2048]{1,0:T(8,128)} %get-tuple-element.138.refs_3_.refs_2_, ...), custom_call_target="tpu_custom_call" | custom-call | flops 1 | bytes 1 | tf_op jit(solution)/shard_map/mix/pallas_call | solution.py:68
  161.4 12.1 %collective-permute-done.34.refs_2_.refs_4_ = bf16[128,2048]{1,0:T(8,128)(2,1)S(1)} collective-permute-done((bf16[128,2048]{1,0:T(8,128)(2,1)}, bf16[128,2048]{1,0:T(8,128)(2,1)S(1)}, u32[]{:S(2)}, u32[]{:S(2)}) %collective-permute-start.34) | collective-permute-done | bytes 524320 | tf_op jit(solution)/shard_map/ppermute | solution.py:667
  178.8 11.0 %collective-permute-done.37.refs_4_.refs_6_ = bf16[128,2048]{1,0:T(8,128)(2,1)S(1)} collective-permute-done((bf16[128,2048]{1,0:T(8,128)(2,1)}, bf16[128,2048]{1,0:T(8,128)(2,1)S(1)}, u32[]{:S(2)}, u32[]{:S(2)}) %collective-permute-start.37) | collective-permute-done | bytes 524320 | tf_op jit(solution)/shard_map/ppermute | solution.py:670
  202.0 14.0 %gate.2 = (bf16[1024,704]{1,0:T(8,128)(2,1)}, bf16[1024,704]{1,0:T(8,128)(2,1)}, bf16[1024,704]{1,0:T(8,128)(2,1)}) custom-call(bf16[128,2048]{1,0:T(8,128)(2,1)} %get-tuple-element.162.refs_0_.refs_2_, bf16[128,2048]{1,0:T(8,128)(2,1)} %get-tuple-element.163.refs_1_.refs_3_, bf16[128,2048]{1,0:T(8,128)(2,1)} %copy-done.10, bf16[128,2048]{1,0:T(8,128)(2,1)} %copy-done.13, ...), custom_call_target="tpu_custom_call" | custom-call | flops 1 | bytes 1 | tf_op jit(solution)/shard_map/gate/pallas_call | solution.py:68
  216.0 14.1 %gate.3 = (bf16[1024,704]{1,0:T(8,128)(2,1)}, bf16[1024,704]{1,0:T(8,128)(2,1)}, bf16[1024,704]{1,0:T(8,128)(2,1)}) custom-call(bf16[128,2048]{1,0:T(8,128)(2,1)} %get-tuple-element.162.refs_0_.refs_2_, bf16[128,2048]{1,0:T(8,128)(2,1)} %get-tuple-element.163.refs_1_.refs_3_, bf16[128,2048]{1,0:T(8,128)(2,1)} %copy-done.10, bf16[128,2048]{1,0:T(8,128)(2,1)} %copy-done.13, ...), custom_call_target="tpu_custom_call" | custom-call | flops 1 | bytes 1 | tf_op jit(solution)/shard_map/gate/pallas_call | solution.py:68
  260.6 10.7 %gate_back.2 = (bf16[1024,704]{1,0:T(8,128)(2,1)}, bf16[1024,704]{1,0:T(8,128)(2,1)}) custom-call(bf16[128,2048]{1,0:T(8,128)(2,1)} %copy-done.1, bf16[128,2048]{1,0:T(8,128)(2,1)} %copy-done, bf16[128,2048]{1,0:T(8,128)(2,1)} %copy-done.5, bf16[128,2048]{1,0:T(8,128)(2,1)} %copy-done.9, bf16[128,2048]{1,0:T(8,128)(2,1)} %copy-done.8, ...), custom_call_target="tpu_custom_call" | custom-call | flops 1 | bytes 1 | tf_op jit(solution)/shard_map/gate_back/pallas_call | solution.py:68
  271.4 11.1 %gate_back.3 = (bf16[1024,704]{1,0:T(8,128)(2,1)}, bf16[1024,704]{1,0:T(8,128)(2,1)}) custom-call(bf16[128,2048]{1,0:T(8,128)(2,1)} %copy-done.1, bf16[128,2048]{1,0:T(8,128)(2,1)} %copy-done, bf16[128,2048]{1,0:T(8,128)(2,1)} %copy-done.5, bf16[128,2048]{1,0:T(8,128)(2,1)} %copy-done.9, bf16[128,2048]{1,0:T(8,128)(2,1)} %copy-done.8, ...), custom_call_target="tpu_custom_call" | custom-call | flops 1 | bytes 1 | tf_op jit(solution)/shard_map/gate_back/pallas_call | solution.py:68
  282.5 21.6 %rows_back.1 = (bf16[128,2048]{1,0:T(8,128)(2,1)}, bf16[128,2048]{1,0:T(8,128)(2,1)}, bf16[128,2048]{1,0:T(8,128)(2,1)}, bf16[128,2048]{1,0:T(8,128)(2,1)}, bf16...) custom-call(bf16[1024,704]{1,0:T(8,128)(2,1)} %get-tuple-element.176.refs_11_.refs_0_, ...), custom_call_target="tpu_custom_call" | custom-call | flops 1 | bytes 1 | tf_op jit(solution)/shard_map/rows_back/pallas_call | solution.py:68
  307.2 12.3 %hidden_sums.6 = (bf16[176,2048]{1,0:T(8,128)(2,1)}, bf16[176,2048]{1,0:T(8,128)(2,1)}, bf16[176,2048]{1,0:T(8,128)(2,1)}, bf16[176,2048]{1,0:T(8,128)(2,1)}, bf...) custom-call(bf16[1024,704]{1,0:T(8,128)(2,1)} %get-tuple-element.180, ...), custom_call_target="tpu_custom_call" | custom-call | flops 1 | bytes 1 | tf_op jit(solution)/shard_map/hidden_sums/pallas_call | solution.py:68
  335.2 14.5 %hidden_sums.7.refs_10_ = bf16[1408,2048]{1,0:T(8,128)(2,1)} custom-call(bf16[1024,704]{1,0:T(8,128)(2,1)} %get-tuple-element.176.refs_11_.refs_0_, bf16[1024,704]{1,0:T(8,128)(2,1)} %get-tuple-element.177.refs_1_, bf16[128,2048]{1,0:T(8,128)(2,1)} %get-tuple-element.162.refs_0_.refs_2_, bf16[128,2048]{1,0:T(8,128)(2,1)} %get-tuple-element.163.refs_1_.refs_3_, ...), custom_call_target="tpu_custom_call" | custom-call | flops 1 | bytes 1 | tf_op jit(solution)/shard_map/hidden_sums/pallas_call | solution.py:68
  352.9 11.3 %collective-permute-done.49.refs_9_ = bf16[128,2048]{1,0:T(8,128)(2,1)S(1)} collective-permute-done((bf16[128,2048]{1,0:T(8,128)(2,1)S(1)}, bf16[128,2048]{1,0:T(8,128)(2,1)S(1)}, u32[]{:S(2)}, u32[]{:S(2)}) %collective-permute-start.49) | collective-permute-done | bytes 524320 | tf_op jit(solution)/shard_map/ppermute | solution.py:670
  394.1 20.8 %attend_back.1 = (bf16[256,2304]{1,0:T(8,128)(2,1)}, f32[256,256]{1,0:T(8,128)}) custom-call(s32[2]{0:T(128)} %pad_add_fusion.refs_0_, f32[1]{0:T(128)} %bitcast.9.refs_0_.refs_1_, bf16[256,2048]{1,0:T(8,128)(2,1)} %get-tuple-element.200.refs_1_.refs_2_, bf16[256,256]{1,0:T(8,128)(2,1)} %refs_3_.3, bf16[256,2048]{1,0:T(8,128)(2,1)} %get-tuple-element.135.refs_1_.refs_4_, ...), custom_call_target="tpu_custom_call" | custom-call | flops 1 | bytes 1 | tf_op jit(solution)/shard_map/attend_back/pallas_call | solution.py:68
  446.9 12.8 %finish.1 = (f32[256,2048]{1,0:T(8,128)}, f32[8,2048]{1,0:T(8,128)}) custom-call(s32[2]{0:T(128)} %pad_add_fusion.refs_0_, bf16[256,2048]{1,0:T(8,128)(2,1)} %refs_1_.5, f32[8,2048]{1,0:T(8,128)} %get-tuple-element.138.refs_3_.refs_2_, bf16[256,2304]{1,0:T(8,128)(2,1)} %get-tuple-element.206.refs_4_.refs_1_.refs_3_, f32[256,2048]{1,0:T(8,128)} %get-tuple-element.219.refs_4_, ...), custom_call_target="tpu_custom_call" | custom-call | flops 1 | bytes 1 | tf_op jit(solution)/shard_map/finish/pallas_call | solution.py:68
  460.6 9.7 %collective-permute-done.64.refs_3_ = bf16[256,2304]{1,0:T(8,128)(2,1)S(1)} collective-permute-done((bf16[256,2304]{1,0:T(8,128)(2,1)}, bf16[256,2304]{1,0:T(8,128)(2,1)S(1)}, u32[]{:S(2)}, u32[]{:S(2)}) %collective-permute-start.64) | collective-permute-done | bytes 1179680 | tf_op jit(solution)/shard_map/ppermute | solution.py:670
  481.9 11.3 %down.1 = (bf16[128,2048]{1,0:T(8,128)(2,1)}, bf16[128,2048]{1,0:T(8,128)(2,1)}, bf16[128,2048]{1,0:T(8,128)(2,1)}, bf16[128,2048]{1,0:T(8,128)(2,1)}, bf16[256,...) custom-call(bf16[1024,704]{1,0:T(8,128)(2,1)} %get-tuple-element.167.refs_9_.refs_0_, ...), custom_call_target="tpu_custom_call" | custom-call | flops 1 | bytes 1 | tf_op jit(solution)/shard_map/down/pallas_call | solution.py:68
  504.3 13.7 %collective-permute-done.68.refs_3_ = bf16[256,2048]{1,0:T(8,128)(2,1)S(1)} collective-permute-done((bf16[256,2048]{1,0:T(8,128)(2,1)}, bf16[256,2048]{1,0:T(8,128)(2,1)S(1)}, u32[]{:S(2)}, u32[]{:S(2)}) %collective-permute-start.68) | collective-permute-done | bytes 1048608 | tf_op jit(solution)/shard_map/ppermute | solution.py:670
  (360 shorter events, 231.4 us)
Async XLA Ops:
  7.2 38.3 %all-gather.5.cloned.1.call-start = ((), (), s32[]{:S(2)}) async-start(), calls=%async_computation.4 | async-start | bytes 1556480 | tf_op jit(solution)/shard_map/all_gather | solution.py:689
  9.8 83.5 %all-gather.7.cloned.1.call-start = ((), (), s32[]{:S(2)}) async-start(), calls=%async_computation.5 | async-start | bytes 1310720 | tf_op jit(solution)/shard_map/all_gather | solution.py:689
  10.5 189.4 %all-gather.9.cloned.1.call-start = ((), (), s32[]{:S(2)}) async-start(), calls=%async_computation.6 | async-start | bytes 7208960 | tf_op jit(solution)/shard_map/all_gather | solution.py:689
  13.7 245.1 %all-gather.11.cloned.1.call-start = ((), (), s32[]{:S(2)}) async-start(), calls=%async_computation.7 | async-start | bytes 3604480 | tf_op jit(solution)/shard_map/all_gather | solution.py:689
  65.4 27.9 %collective-permute-start.8 = (bf16[2,64,2432]{2,1,0:T(8,128)(2,1)}, bf16[2,64,2432]{2,1,0:T(8,128)(2,1)}, u32[]{:S(2)}, u32[]{:S(2)}) collective-permute-start(bf16[2,64,2432]{2,1,0:T(8,128)(2,1)} %collective-permute-done.4.refs_8_.refs_9_), channel_id=1, source_target_pairs={{0,1},{1,0},{2,3},{3,2},{4,5},{5,4},{6,7},{7,6},{8,9},{9,8},{10,11... | collective-permute-start | bytes 1867784 | tf_op jit(solution)/shard_map/ppermute | solution.py:670
  65.9 27.3 %collective-permute-start.11 = (bf16[2,64,2432]{2,1,0:T(8,128)(2,1)}, bf16[2,64,2432]{2,1,0:T(8,128)(2,1)}, u32[]{:S(2)}, u32[]{:S(2)}) collective-permute-start(bf16[2,64,2432]{2,1,0:T(8,128)(2,1)} %bitcast.6.refs_5_.refs_6_), channel_id=1, source_target_pairs={{0,8},{8,0},{16,24},{24,16},{1,9},{9,1},{17,25},{25,17},{2,10},{10... | collective-permute-start | bytes 1867784 | tf_op jit(solution)/shard_map/ppermute | solution.py:656
  65.9 28.7 %collective-permute-start.7 = (bf16[2,64,2432]{2,1,0:T(8,128)(2,1)}, bf16[2,64,2432]{2,1,0:T(8,128)(2,1)}, u32[]{:S(2)}, u32[]{:S(2)}) collective-permute-start(bf16[2,64,2432]{2,1,0:T(8,128)(2,1)} %bitcast.6.refs_5_.refs_6_), channel_id=1, source_target_pairs={{0,16},{8,24},{16,0},{24,8},{1,17},{9,25},{17,1},{25,9},{2,18},{10... | collective-permute-start | bytes 1867784 | tf_op jit(solution)/shard_map/ppermute | solution.py:667
  116.7 22.8 %collective-permute-start.23 = (bf16[2,64,2048]{2,1,0:T(8,128)(2,1)S(1)}, bf16[2,64,2048]{2,1,0:T(8,128)(2,1)}, u32[]{:S(2)}, u32[]{:S(2)}) collective-permute-start(bf16[2,64,2048]{2,1,0:T(8,128)(2,1)S(1)} %collective-permute-done.19.refs_7_.refs_12_), channel_id=1, source_target_pairs={{0,16},{8,24},{16,0},{24,8},{1,17},{9,25},{17,1},{25,9},{2,18},{10... | collective-permute-start | bytes 1572872 | tf_op jit(solution)/shard_map/ppermute | solution.py:667
  175.9 23.2 %collective-permute-start.38 = (bf16[128,2048]{1,0:T(8,128)(2,1)S(1)}, bf16[128,2048]{1,0:T(8,128)(2,1)S(1)}, u32[]{:S(2)}, u32[]{:S(2)}) collective-permute-start(bf16[128,2048]{1,0:T(8,128)(2,1)S(1)} %collective-permute-done.34.refs_2_.refs_4_), channel_id=1, source_target_pairs={{0,1},{1,0},{2,3},{3,2},{4,5},{5,4},{6,7},{7,6},{8,9},{9,8},{10,11... | collective-permute-start | bytes 1572872 | tf_op jit(solution)/shard_map/ppermute | solution.py:670
  177.3 22.6 %collective-permute-start.39 = (bf16[128,2048]{1,0:T(8,128)(2,1)S(1)}, bf16[128,2048]{1,0:T(8,128)(2,1)}, u32[]{:S(2)}, u32[]{:S(2)}) collective-permute-start(bf16[128,2048]{1,0:T(8,128)(2,1)S(1)} %collective-permute-done.35.refs_5_.refs_7_), channel_id=1, source_target_pairs={{0,16},{8,24},{16,0},{24,8},{1,17},{9,25},{17,1},{25,9},{2,18},{10... | collective-permute-start | bytes 1572872 | tf_op jit(solution)/shard_map/ppermute | solution.py:667
  199.9 149.8 %reduce-scatter.5.cloned.1.call-start = ((), (), s32[]{:S(2)}) async-start(), calls=%async_computation.8 | async-start | bytes 3604480 | tf_op jit(solution)/shard_map/reduce_scatter | solution.py:692
  200.2 29.9 %collective-permute-start.33 = (bf16[128,2048]{1,0:T(8,128)(2,1)S(1)}, bf16[128,2048]{1,0:T(8,128)(2,1)S(1)}, u32[]{:S(2)}, u32[]{:S(2)}) collective-permute-start(bf16[128,2048]{1,0:T(8,128)(2,1)S(1)} %get-tuple-element.158.refs_1_.refs_0_), channel_id=1, source_target_pairs={{0,1},{1,0},{2,3},{3,2},{4,5},{5,4},{6,7},{7,6},{8,9},{9,8},{10,11... | collective-permute-start | bytes 1572872 | tf_op jit(solution)/shard_map/ppermute | solution.py:670
  201.3 28.8 %collective-permute-start.32 = (bf16[128,2048]{1,0:T(8,128)(2,1)S(1)}, bf16[128,2048]{1,0:T(8,128)(2,1)S(1)}, u32[]{:S(2)}, u32[]{:S(2)}) collective-permute-start(bf16[128,2048]{1,0:T(8,128)(2,1)S(1)} %get-tuple-element.159.refs_2_.refs_1_), channel_id=1, source_target_pairs={{0,16},{8,24},{16,0},{24,8},{1,17},{9,25},{17,1},{25,9},{2,18},{10... | collective-permute-start | bytes 1572872 | tf_op jit(solution)/shard_map/ppermute | solution.py:667
  258.9 212.0 %reduce-scatter.7.cloned.1.call-start = ((), (), s32[]{:S(2)}) async-start(), calls=%async_computation.9 | async-start | bytes 7208960 | tf_op jit(solution)/shard_map/reduce_scatter | solution.py:692
  304.1 25.8 %collective-permute-start.46 = (bf16[256,2048]{1,0:T(8,128)(2,1)}, bf16[256,2048]{1,0:T(8,128)(2,1)S(1)}, u32[]{:S(2)}, u32[]{:S(2)}) collective-permute-start(bf16[256,2048]{1,0:T(8,128)(2,1)} %get-tuple-element.183), channel_id=1, source_target_pairs={{0,1},{1,0},{2,3},{3,2},{4,5},{5,4},{6,7},{7,6},{8,9},{9,8},{10,11... | collective-permute-start | bytes 3145736 | tf_op jit(solution)/shard_map/ppermute | solution.py:670
  305.7 25.5 %collective-permute-start.47 = (bf16[256,2048]{1,0:T(8,128)(2,1)}, bf16[256,2048]{1,0:T(8,128)(2,1)S(1)}, u32[]{:S(2)}, u32[]{:S(2)}) collective-permute-start(bf16[256,2048]{1,0:T(8,128)(2,1)} %get-tuple-element.186), channel_id=1, source_target_pairs={{0,16},{8,24},{16,0},{24,8},{1,17},{9,25},{17,1},{25,9},{2,18},{10... | collective-permute-start | bytes 3145736 | tf_op jit(solution)/shard_map/ppermute | solution.py:667
  349.8 152.7 %reduce-scatter.11.cloned.1.call-start = ((), (), s32[]{:S(2)}) async-start(), calls=%async_computation.11 | async-start | bytes 1310720 | tf_op jit(solution)/shard_map/reduce_scatter | solution.py:692
  391.8 25.4 %collective-permute-start.60 = (bf16[256,2048]{1,0:T(8,128)(2,1)}, bf16[256,2048]{1,0:T(8,128)(2,1)S(1)}, u32[]{:S(2)}, u32[]{:S(2)}) collective-permute-start(bf16[256,2048]{1,0:T(8,128)(2,1)} %get-tuple-element.209), channel_id=1, source_target_pairs={{0,16},{8,24},{16,0},{24,8},{1,17},{9,25},{17,1},{25,9},{2,18},{10... | collective-permute-start | bytes 3145736 | tf_op jit(solution)/shard_map/ppermute | solution.py:667
  393.3 25.1 %collective-permute-start.61 = (bf16[256,2048]{1,0:T(8,128)(2,1)}, bf16[256,2048]{1,0:T(8,128)(2,1)S(1)}, u32[]{:S(2)}, u32[]{:S(2)}) collective-permute-start(bf16[256,2048]{1,0:T(8,128)(2,1)} %get-tuple-element.210), channel_id=1, source_target_pairs={{0,1},{1,0},{2,3},{3,2},{4,5},{5,4},{6,7},{7,6},{8,9},{9,8},{10,11... | collective-permute-start | bytes 3145736 | tf_op jit(solution)/shard_map/ppermute | solution.py:670
  442.1 28.2 %collective-permute-start.64 = (bf16[256,2304]{1,0:T(8,128)(2,1)}, bf16[256,2304]{1,0:T(8,128)(2,1)S(1)}, u32[]{:S(2)}, u32[]{:S(2)}) collective-permute-start(bf16[256,2304]{1,0:T(8,128)(2,1)} %get-tuple-element.215), channel_id=1, source_target_pairs={{0,1},{1,0},{2,3},{3,2},{4,5},{5,4},{6,7},{7,6},{8,9},{9,8},{10,11... | collective-permute-start | bytes 3538952 | tf_op jit(solution)/shard_map/ppermute | solution.py:670
  442.9 27.9 %collective-permute-start.65 = (bf16[256,2304]{1,0:T(8,128)(2,1)}, bf16[256,2304]{1,0:T(8,128)(2,1)S(1)}, u32[]{:S(2)}, u32[]{:S(2)}) collective-permute-start(bf16[256,2304]{1,0:T(8,128)(2,1)} %get-tuple-element.218), channel_id=1, source_target_pairs={{0,16},{8,24},{16,0},{24,8},{1,17},{9,25},{17,1},{25,9},{2,18},{10... | collective-permute-start | bytes 3538952 | tf_op jit(solution)/shard_map/ppermute | solution.py:667
  476.8 60.2 %reduce-scatter.9.cloned.1.call-start = ((), (), s32[]{:S(2)}) async-start(), calls=%async_computation.10 | async-start | bytes 1556480 | tf_op jit(solution)/shard_map/reduce_scatter | solution.py:692
  494.9 23.1 %collective-permute-start.68 = (bf16[256,2048]{1,0:T(8,128)(2,1)}, bf16[256,2048]{1,0:T(8,128)(2,1)S(1)}, u32[]{:S(2)}, u32[]{:S(2)}) collective-permute-start(bf16[256,2048]{1,0:T(8,128)(2,1)} %get-tuple-element.231), channel_id=1, source_target_pairs={{0,1},{1,0},{2,3},{3,2},{4,5},{5,4},{6,7},{7,6},{8,9},{9,8},{10,11... | collective-permute-start | bytes 3145736 | tf_op jit(solution)/shard_map/ppermute | solution.py:670
  495.9 22.8 %collective-permute-start.69 = (bf16[256,2048]{1,0:T(8,128)(2,1)}, bf16[256,2048]{1,0:T(8,128)(2,1)S(1)}, u32[]{:S(2)}, u32[]{:S(2)}) collective-permute-start(bf16[256,2048]{1,0:T(8,128)(2,1)} %get-tuple-element.234), channel_id=1, source_target_pairs={{0,16},{8,24},{16,0},{24,8},{1,17},{9,25},{17,1},{25,9},{2,18},{10... | collective-permute-start | bytes 3145736 | tf_op jit(solution)/shard_map/ppermute | solution.py:667
  (132 other events, 1729.8 us)
Sparse Core Ops, SparseCore 0:
  10.2 34.2 all-gather.4
  46.0 26.9 all-gather.6
  75.2 106.1 all-gather.8
  200.1 58.7 all-gather.10
  261.5 54.8 reduce-scatter.4
  349.9 100.0 reduce-scatter.6
  476.9 25.5 reduce-scatter.10
  505.0 28.8 reduce-scatter.8

commit v4 on v3

--- a/solution.py
+++ b/solution.py
@@ -58,7 +58,7 @@
     return pl.BlockSpec(memory_space=pltpu.SMEM)
 
 
-def kernel_call(body, out_shapes, scratch, in_specs):
+def kernel_call(body, out_shapes, scratch, in_specs, out_spec=vmem_spec):
     def run(*operands):
         known, late = len(in_specs), len(operands) - len(in_specs)
 
@@ -69,7 +69,7 @@
             whole_body,
             out_shape=out_shapes,
             in_specs=in_specs + [any_spec()] * late,
-            out_specs=jax.tree.map(lambda _: vmem_spec(), out_shapes),
+            out_specs=jax.tree.map(lambda _: out_spec(), out_shapes),
             scratch_shapes=scratch,
             compiler_params=pltpu.CompilerParams(vmem_limit_bytes=vmem_limit),
             cost_estimate=pl.CostEstimate(flops=1, bytes_accessed=1, transcendentals=0),
@@ -102,10 +102,19 @@
     )
 
 
-def store_routed(way, outs, size, block):
+def send_blocks(way, outs, held, index, size, sem):
     for blocks, out in zip(way, outs):
         for spot, place in enumerate(blocks):
-            out[spot * size : (spot + 1) * size, :] = block(place).astype(bf16)
+
+            @pl.when(index == place // 2)
+            def _():
+                pltpu.make_async_copy(
+                    held.at[pl.ds(place * size, size)], out.at[pl.ds(spot * size, size)], sem
+                ).start()
+
+
+def wait_all(whole, sem):
+    pltpu.make_async_copy(whole, whole, sem).wait()
 
 
 class Pieces:
@@ -295,27 +304,29 @@
 def norm_back_body(factor, mid, gains, grad_out, *refs):
     sums = refs[:6]
     d_mid_out, d_mid_low, gain_out = refs[6:]
-    length = mid.shape[0]
-    half = length // 2
+    half = mid.shape[0] // 2
+    size = half // 4
+    gain = gains[1:2, :]
+    gain_out[...] = jnp.zeros_like(gain_out)
     for part in range(2):
-        rows = pl.ds(part * half, half)
-        terms = sums[3 * part : 3 * part + 3]
-        d_h = terms[0][...].astype(f32) + terms[1][half:, :].astype(f32) + terms[2][...].astype(f32)
-        x_mid = mid[rows, :]
-        inverse = lax.rsqrt(jnp.mean(x_mid * x_mid, axis=-1, keepdims=True) + epsilon)
-        normed = x_mid * inverse
-        product = d_h * normed
-        gain_sum = jnp.broadcast_to(jnp.sum(product, axis=0, keepdims=True), gain_out.shape)
-        if part == 0:
-            gain_out[...] = gain_sum
-        else:
-            gain_out[...] += gain_sum
-        gain = gains[1:2, :]
-        mean = jnp.mean(product * gain, axis=-1, keepdims=True)
-        grad_top = grad_out[rows, :].astype(f32) * factor[0]
-        d_mid = grad_top + inverse * (d_h * gain - normed * mean)
-        d_mid_out[rows, :] = d_mid
-        d_mid_low[rows, :] = d_mid.astype(bf16)
+        own, middle, last = sums[3 * part : 3 * part + 3]
+
+        @pl.loop(0, 4)
+        def _(block):
+            start = pl.multiple_of(block * size, size)
+            here, there = pl.ds(start, size), pl.ds(half + start, size)
+            rows = pl.ds(part * half + start, size)
+            d_h = own[here, :].astype(f32) + middle[there, :].astype(f32) + last[here, :].astype(f32)
+            x_mid = mid[rows, :]
+            inverse = lax.rsqrt(jnp.mean(x_mid * x_mid, axis=-1, keepdims=True) + epsilon)
+            normed = x_mid * inverse
+            product = d_h * normed
+            gain_out[0:1, :] += jnp.sum(product, axis=0, keepdims=True)
+            mean = jnp.mean(product * gain, axis=-1, keepdims=True)
+            grad_top = grad_out[rows, :].astype(f32) * factor[0]
+            d_mid = grad_top + inverse * (d_h * gain - normed * mean)
+            d_mid_out[rows, :] = d_mid
+            d_mid_low[rows, :] = d_mid.astype(bf16)
 
 
 def norm_back(factor, mid, gains, grad_out, sums, late=()):
@@ -442,18 +453,26 @@
     return waits
 
 
+def fetch_row_blocks(parts, whole, sems):
+    size = parts[0].shape[0]
+    for place, part in enumerate(parts):
+        sem = sems.at[place * size // step]
+        pltpu.make_async_copy(part, whole.at[pl.ds(place * size, size)], sem).start()
+
+
 def gate_body(shard, count, *refs):
     parts, both = refs[:count], refs[count]
     hid, by_gate, by_up = refs[count + 1 : count + 4]
-    rows, gate_w, up_w, row_sem, gate_sem, up_sem = refs[count + 4 :]
+    rows, gate_w, up_w, row_sems, gate_sem, up_sem = refs[count + 4 :]
     waits = fetch_gate_up(both, shard, gate_w, up_w, gate_sem, up_sem)
-    waits.append(fetch_rows(parts, rows, row_sem))
+    fetch_row_blocks(parts, rows, row_sems)
     for wait in waits:
         wait()
 
     @pl.loop(0, rows.shape[0] // step)
     def _(block):
         own = pl.ds(pl.multiple_of(block * step, step), step)
+        wait_all(rows.at[own], row_sems.at[block])
         gate = contract_last(rows[own, :], gate_w[...])
         up = contract_last(rows[own, :], up_w[...])
         sigma = 1.0 / (1.0 + jnp.exp(-gate))
@@ -472,25 +491,23 @@
         (out, out, out),
         [pltpu.VMEM((total, width), bf16)]
         + [pltpu.VMEM((hidden, width), bf16)] * 2
-        + [pltpu.SemaphoreType.DMA] * 3,
+        + [pltpu.SemaphoreType.DMA((total // step,)), pltpu.SemaphoreType.DMA, pltpu.SemaphoreType.DMA],
         [any_spec()] * (len(parts) + 1),
     )(*parts, both, *late)
 
 
-def d_hidden(rows, weight, scales, grads):
+def gate_back_body(count, *refs):
+    parts, weight, scales, grads = refs[:count], refs[count], refs[count + 1 : count + 3], refs[count + 3 : count + 5]
+    rows, row_sems = refs[count + 5 :]
+    fetch_row_blocks(parts, rows, row_sems)
+
     @pl.loop(0, rows.shape[0] // step)
     def _(block):
         own = pl.ds(pl.multiple_of(block * step, step), step)
+        wait_all(rows.at[own], row_sems.at[block])
         d_hid = contract_last(rows[own, :], weight[...])
         for scale, grad in zip(scales, grads):
             grad[own, :] = (d_hid * scale[own, :].astype(f32)).astype(bf16)
-
-
-def gate_back_body(count, *refs):
-    parts, weight, scales, grads = refs[:count], refs[count], refs[count + 1 : count + 3], refs[count + 3 : count + 5]
-    rows, sem = refs[count + 5 :]
-    fetch_rows(parts, rows, sem)()
-    d_hidden(rows, weight, scales, grads)
 
 
 def gate_back(parts, weight, scales, late=()):
@@ -500,14 +517,14 @@
     return kernel_call(
         functools.partial(gate_back_body, count),
         (grad, grad),
-        [pltpu.VMEM((total, width), bf16), pltpu.SemaphoreType.DMA],
+        [pltpu.VMEM((total, width), bf16), pltpu.SemaphoreType.DMA((total // step,))],
         [any_spec()] * count + [vmem_spec()] * 3,
     )(*parts, weight, *scales, *late)
 
 
-def rows_back_body(shard, size, *refs):
+def rows_back_body(shard, *refs):
     grads, boths, outs = refs[:4], refs[4:6], refs[6:12]
-    weights, sems = refs[12:16], refs[16]
+    weights, held, sems = refs[12:16], refs[16], refs[17]
     waits = []
     for place in range(2):
         waits += fetch_gate_up(
@@ -516,43 +533,61 @@
         )
     for wait in waits:
         wait()
-
-    def block(place):
-        own = pl.ds(place * size, size)
-        total = jnp.dot(grads[0][own, :], weights[0][...], preferred_element_type=f32)
-        for grad, piece in zip(grads[1:], weights[1:]):
-            total += jnp.dot(grad[own, :], piece[...], preferred_element_type=f32)
-        return total
-
-    store_routed(row_route, outs, size, block)
+    size = held.shape[0] // 8
+
+    @pl.loop(0, 4)
+    def _(index):
+        own = pl.ds(pl.multiple_of(index * 2 * size, 2 * size), 2 * size)
+
+        @pl.loop(0, held.shape[1] // (4 * step))
+        def _(block):
+            columns = pl.ds(pl.multiple_of(block * 4 * step, 4 * step), 4 * step)
+            total = jnp.dot(grads[0][own, :], weights[0][:, columns], preferred_element_type=f32)
+            for grad, piece in zip(grads[1:], weights[1:]):
+                total += jnp.dot(grad[own, :], piece[:, columns], preferred_element_type=f32)
+            held[own, columns] = total.astype(bf16)
+
+        send_blocks(row_route, outs, held, index, size, sems.at[4])
+
+    wait_all(held, sems.at[4])
 
 
 def rows_back(grads, boths, shard, late=()):
     total, hidden = grads[0].shape
     width = boths[0].shape[1]
     return kernel_call(
-        functools.partial(rows_back_body, shard, total // 8),
+        functools.partial(rows_back_body, shard),
         routed(total // 8, width),
-        [pltpu.VMEM((hidden, width), bf16)] * 4 + [pltpu.SemaphoreType.DMA((4,))],
+        [pltpu.VMEM((hidden, width), bf16)] * 4
+        + [pltpu.VMEM((total, width), bf16), pltpu.SemaphoreType.DMA((5,))],
         [vmem_spec()] * 4 + [any_spec()] * 2,
+        any_spec,
     )(*grads, *boths, *late)
 
 
-def down_body(size, *refs):
-    hids, downs, outs = refs[:2], refs[2:4], refs[4:]
-
-    def block(place):
-        own = pl.ds(place * size, size)
+def down_body(*refs):
+    hids, downs, outs, held, sem = refs[:2], refs[2:4], refs[4:10], refs[10], refs[11]
+    size = held.shape[0] // 8
+
+    @pl.loop(0, 4)
+    def _(index):
+        own = pl.ds(pl.multiple_of(index * 2 * size, 2 * size), 2 * size)
         total = jnp.dot(hids[0][own, :], downs[0][...], preferred_element_type=f32)
-        return total + jnp.dot(hids[1][own, :], downs[1][...], preferred_element_type=f32)
-
-    store_routed(row_route, outs, size, block)
+        total += jnp.dot(hids[1][own, :], downs[1][...], preferred_element_type=f32)
+        held[own, :] = total.astype(bf16)
+        send_blocks(row_route, outs, held, index, size, sem)
+
+    wait_all(held, sem)
 
 
 def down(hids, downs, late=()):
     total, width = hids[0].shape[0], downs[0].shape[1]
     return kernel_call(
-        functools.partial(down_body, total // 8), routed(total // 8, width), [], [vmem_spec()] * 4
+        down_body,
+        routed(total // 8, width),
+        [pltpu.VMEM((total, width), bf16), pltpu.SemaphoreType.DMA],
+        [vmem_spec()] * 4,
+        any_spec,
     )(*hids, *downs, *late)
 
 
@@ -560,21 +595,33 @@
     lefts, parts = refs[:pairs], refs[pairs : pairs + count]
     others = refs[pairs + count : pairs + count + pieces * received]
     refs = refs[pairs + count + pieces * received :]
-    outs, rows, sem = refs[:-2], refs[-2], refs[-1]
-    fetch_rows(parts, rows, sem)()
-    for place, left in enumerate(lefts):
-        product = contract_first(left[...], rows[...])
-        for outer in range(left.shape[1] // shard):
-            start = (pairs * outer + place) * shard
-            own = product[outer * shard : (outer + 1) * shard]
-            if received:
-                piece, row = start // others[0].shape[0], start % others[0].shape[0]
-                outs[0][start : start + shard, :] = (
-                    own + others[piece][row : row + shard, :].astype(f32)
-                ).astype(bf16)
-            else:
-                piece, row = start // outs[0].shape[0], start % outs[0].shape[0]
-                outs[piece][row : row + shard, :] = own.astype(bf16)
+    outs, turned, rows, sem = refs[: -pairs - 2], refs[-pairs - 2 : -2], refs[-2], refs[-1]
+    wait = fetch_rows(parts, rows, sem)
+
+    @pl.loop(0, rows.shape[0] // step)
+    def _(block):
+        own = pl.ds(pl.multiple_of(block * step, step), step)
+        for left, flat in zip(lefts, turned):
+            flat[:, own] = left[own, :].T
+
+    wait()
+
+    @pl.loop(0, rows.shape[1] // step)
+    def _(block):
+        columns = pl.ds(pl.multiple_of(block * step, step), step)
+        for place, flat in enumerate(turned):
+            product = jnp.dot(flat[...], rows[:, columns], preferred_element_type=f32)
+            for outer in range(flat.shape[0] // shard):
+                start = (pairs * outer + place) * shard
+                own = product[outer * shard : (outer + 1) * shard]
+                if received:
+                    piece, row = start // others[0].shape[0], start % others[0].shape[0]
+                    outs[0][start : start + shard, columns] = (
+                        own + others[piece][row : row + shard, columns].astype(f32)
+                    ).astype(bf16)
+                else:
+                    piece, row = start // outs[0].shape[0], start % outs[0].shape[0]
+                    outs[piece][row : row + shard, columns] = own.astype(bf16)
 
 
 def hidden_sums(lefts, parts, shard, pieces, others=None, late=()):
@@ -585,48 +632,83 @@
     outs = kernel_call(
         functools.partial(hidden_sums_body, len(parts), len(lefts), shard, pieces, received),
         (jax.ShapeDtypeStruct((hidden // count, width), bf16),) * count,
-        [pltpu.VMEM((total, width), bf16), pltpu.SemaphoreType.DMA],
+        [pltpu.VMEM((left.shape[1], total), bf16) for left in lefts]
+        + [pltpu.VMEM((total, width), bf16), pltpu.SemaphoreType.DMA],
         [vmem_spec()] * len(lefts) + [any_spec()] * len(parts) + [vmem_spec()] * (pieces * received),
     )(*lefts, *parts, *(others or ()), *late)
     return outs[0] if received else outs
 
 
-def send_sums_body(turned, right, *outs):
-    middle, size = turned.shape[0] // 2, outs[0].shape[0]
-    for place, out in enumerate(outs):
-        own = pl.ds(middle + place * size, size)
-        out[...] = jnp.dot(turned[own, :], right[...], preferred_element_type=f32).astype(bf16)
+def send_sums_body(turned, right, first, second, held, sem):
+    middle = turned.shape[0] // 2
+    size = middle // 4
+
+    @pl.loop(0, 4)
+    def _(index):
+        start = pl.multiple_of(index * size, size)
+        own = turned[pl.ds(middle + start, size), :]
+        held[pl.ds(start, size), :] = jnp.dot(own, right[...], preferred_element_type=f32).astype(bf16)
+        for place, out in enumerate((first, first, second, second)):
+
+            @pl.when(index == place)
+            def _():
+                target = out.at[pl.ds((place % 2) * size, size)]
+                pltpu.make_async_copy(held.at[pl.ds(place * size, size)], target, sem).start()
+
+    wait_all(held, sem)
 
 
 def send_sums(turned, right, late=()):
+    rows, columns = turned.shape[0] // 2, right.shape[1]
     return kernel_call(
         send_sums_body,
-        (jax.ShapeDtypeStruct((turned.shape[0] // 4, right.shape[1]), bf16),) * 2,
-        [],
+        (jax.ShapeDtypeStruct((rows // 2, columns), bf16),) * 2,
+        [pltpu.VMEM((rows, columns), bf16), pltpu.SemaphoreType.DMA],
         [vmem_spec()] * 2,
+        any_spec,
     )(turned, right, *late)
 
 
-def keep_sums_body(turned, right, *refs):
-    others, outs = refs[:2], refs[2:]
+def keep_sums_body(turned, right, first, second, *refs):
+    outs, arrived, held, in_sem, out_sem = refs[:6], refs[6], refs[7], refs[8], refs[9]
+    fetch_rows((first, second), arrived, in_sem)()
     size = turned.shape[0] // 16
 
-    def block(place):
-        own = pl.ds(place * size, size)
-        half = pl.ds((place % 4) * size, size)
+    @pl.loop(0, 4)
+    def _(index):
+        own = pl.ds(pl.multiple_of(index * 2 * size, 2 * size), 2 * size)
         product = jnp.dot(turned[own, :], right[...], preferred_element_type=f32)
-        return product + others[place // 4][half, :].astype(f32)
-
-    store_routed(column_route, outs, size, block)
+        held[own, :] = (product + arrived[own, :].astype(f32)).astype(bf16)
+        send_blocks(column_route, outs, held, index, size, out_sem)
+
+    wait_all(held, out_sem)
 
 
 def keep_sums(turned, right, others, late=()):
+    rows, columns = turned.shape[0] // 2, right.shape[1]
     return kernel_call(
         keep_sums_body,
-        routed(turned.shape[0] // 16, right.shape[1]),
-        [],
-        [vmem_spec()] * 4,
+        routed(rows // 8, columns),
+        [pltpu.VMEM((rows, columns), bf16)] * 2 + [pltpu.SemaphoreType.DMA] * 2,
+        [vmem_spec()] * 2 + [any_spec()] * 2,
+        any_spec,
     )(turned, right, *others, *late)
+
+
+def alternate_body(both, out):
+    rows = out.shape[0]
+
+    @pl.loop(0, rows // 8)
+    def _(block):
+        start = pl.multiple_of(block * 8, 8)
+        for place in range(2):
+            out[pl.ds(start, 8), place, :] = both[pl.ds(place * rows + start, 8), :].astype(f32)
+
+
+def alternate(both):
+    rows, columns = both.shape[0] // 2, both.shape[1]
+    out = jax.ShapeDtypeStruct((rows, 2, columns), f32)
+    return kernel_call(alternate_body, out, [], [vmem_spec()])(both)
 
 
 def pass_body(keep_x, keep_y, from_x, from_y, for_x, for_y):
@@ -844,7 +926,10 @@
     )
     in_passed = grid.collect_first(in_parts, [gain_one_sum, d_w_gu])
     d_w_in = grid.total(grid.collect_second(in_parts, in_passed)).astype(bf16)
-    d_w_gu = jnp.stack([d_w_gu[:hidden_rows], d_w_gu[hidden_rows:]], axis=1).astype(f32)
+    if by_shard:
+        d_w_gu = alternate(d_w_gu)
+    else:
+        d_w_gu = jnp.stack([d_w_gu[:hidden_rows], d_w_gu[hidden_rows:]], axis=1).astype(f32)
     d_w_down = d_w_down.astype(f32)
     mlp_parts = down((hid_mine, hid_other), (down_mine, down_other), [in_passed[0]])
     d_w_in, mlp_parts = lax.optimization_barrier((d_w_in, mlp_parts))
@@ -858,16 +943,16 @@
         (2, 1, grid.depth, 1, shard_rows),
     ).reshape(2, grid.depth * shard_rows)
     extra = jnp.pad(own_gains.T, ((0, 0), (0, lanes - 2))).astype(bf16)
-    d_w_in = grid.scatter_outer(jnp.concatenate([d_w_in, extra], axis=1)).astype(f32)
+    d_w_in = grid.scatter_outer(jnp.concatenate([d_w_in, extra], axis=1))
     return (
         output,
         d_tokens,
         kv_out,
         d_kv,
-        d_w_in[:, :q_width],
-        d_w_in[:, q_width : q_width + kv_width],
-        d_w_in[:, q_width + kv_width],
-        d_w_in[:, q_width + kv_width + 1],
+        d_w_in[:, :q_width].astype(f32),
+        d_w_in[:, q_width : q_width + kv_width].astype(f32),
+        d_w_in[:, q_width + kv_width].astype(f32),
+        d_w_in[:, q_width + kv_width + 1].astype(f32),
         d_w_o,
         d_w_gu,
         d_w_down,

time: 556 us -> 551 us (level); the launches traced: 549 us -> 550 us
  Pallas kernels: 236 us -> 246 us
  local copies, waits for them, and re-layouts: 32.9 us -> 23.4 us
    pallas_call x24 -> x25, Pallas kernels: 236 us -> 246 us  [run(): pl.pallas_call(whole_body, out_shape=out_shapes, in_specs=in_specs + [any...]
    unnamed x143 -> x138, local copies, waits for them, and re-layouts: 19.5 us -> 13.9 us
  transfers between devices with their start and end apart: 86 -> 86, of which waited for: 50 -> 49; matrix products, arithmetic and copies ran while one was open for 5% -> 4% of each run, Pallas kernels for 43% -> 45%
where the time goes in v4:
time: 551 us; the launch traced here: 550 us
  Pallas kernels  246 us (45%)
  waiting for transfers between devices  190 us (34%)
  starting transfers between devices  53.9 us (10%)
  local copies, waits for them, and re-layouts  23.4 us (4%)
  other arithmetic  21.3 us (4%)
  between operations  15.6 us (3%)
    pallas_call x25, Pallas kernels, run(): pl.pallas_call(whole_body, out_shape=out_shapes, in_specs=in_specs + [any...  246 us
    ppermute x21, waiting for transfers between devices, y_swap(): return lax.ppermute(value, 'fsdp', [(i, i ^ 1) for i in range(self.fsdp)])  114 us
    ppermute x21, waiting for transfers between devices, x_swap(): return lax.ppermute(value, 'dp', [(i, i ^ 2) for i in range(self.dp)])  46.7 us
    ppermute x35, waiting for transfers between devices, core(): return lax.ppermute(value, 'dp', [(i, i ^ 1) for i in range(self.dp)])  26.4 us
    ppermute x21, starting transfers between devices, x_swap(): return lax.ppermute(value, 'dp', [(i, i ^ 2) for i in range(self.dp)])  23.3 us
    ppermute x21, starting transfers between devices, y_swap(): return lax.ppermute(value, 'fsdp', [(i, i ^ 1) for i in range(self.fsdp)])  22.4 us
    unnamed x138, local copies, waits for them, and re-layouts  13.9 us
  transfers between devices with their start and end apart: 86, of which 49 were waited for; matrix products, arithmetic and copies ran while one was open for 4% of the time, Pallas kernels for 45%

profile of v4, /device:TPU:0, one launch (start us, length us, event | category | flops | bytes accessed | tf_op | source)
XLA Modules:
  0.0 550.0 jit_solution(6597930584498124649)
XLA Ops:
  20.6 10.4 %collective-permute-done.1.refs_6_.refs_5_ = bf16[128,2048]{1,0:T(8,128)(2,1)S(1)} collective-permute-done((bf16[128,2048]{1,0:T(8,128)(2,1)S(1)}, bf16[128,2048]{1,0:T(8,128)(2,1)S(1)}, u32[]{:S(2)}, u32[]{:S(2)}) %collective-permute-start.1) | collective-permute-done | bytes 524320 | tf_op jit(solution)/shard_map/ppermute | solution.py:752
  34.5 10.6 %collective-permute-done.2.refs_7_.refs_6_ = bf16[128,2048]{1,0:T(8,128)(2,1)S(1)} collective-permute-done((bf16[128,2048]{1,0:T(8,128)(2,1)S(1)}, bf16[128,2048]{1,0:T(8,128)(2,1)S(1)}, u32[]{:S(2)}, u32[]{:S(2)}) %collective-permute-start.2) | collective-permute-done | bytes 524320 | tf_op jit(solution)/shard_map/ppermute | solution.py:752
  50.7 11.2 %collective-permute-done.4.refs_8_.refs_9_ = bf16[2,64,2432]{2,1,0:T(8,128)(2,1)} collective-permute-done((bf16[2,64,2432]{2,1,0:T(8,128)(2,1)S(1)}, bf16[2,64,2432]{2,1,0:T(8,128)(2,1)}, u32[]{:S(2)}, u32[]{:S(2)}) %collective-permute-start.4) | collective-permute-done | bytes 622624 | tf_op jit(solution)/shard_map/ppermute | solution.py:749
  67.4 12.8 %collective-permute-done.6.refs_6_.refs_7_ = bf16[2,64,2432]{2,1,0:T(8,128)(2,1)} collective-permute-done((bf16[2,64,2432]{2,1,0:T(8,128)(2,1)S(1)}, bf16[2,64,2432]{2,1,0:T(8,128)(2,1)}, u32[]{:S(2)}, u32[]{:S(2)}) %collective-permute-start.6) | collective-permute-done | bytes 622624 | tf_op jit(solution)/shard_map/ppermute | solution.py:752
  82.0 11.2 %collective-permute-done.8.refs_10_.refs_11_ = bf16[2,64,2432]{2,1,0:T(8,128)(2,1)} collective-permute-done((bf16[2,64,2432]{2,1,0:T(8,128)(2,1)}, bf16[2,64,2432]{2,1,0:T(8,128)(2,1)}, u32[]{:S(2)}, u32[]{:S(2)}) %collective-permute-start.8) | collective-permute-done | bytes 622624 | tf_op jit(solution)/shard_map/ppermute | solution.py:752
  100.4 13.1 %project.1 = (bf16[2048,256]{1,0:T(8,128)(2,1)}, bf16[256,2048]{1,0:T(8,128)(2,1)}, bf16[256,256]{1,0:T(8,128)(2,1)}, f32[8,2048]{1,0:T(8,128)}) custom-call(s32[2]{0:T(128)} %pad_add_fusion.refs_0_, bf16[256,2048]{1,0:T(8,128)(2,1)} %refs_1_.5, f32[256,128]{1,0:T(8,128)} %get-tuple-element.256.refs_2_.refs_7_, ...), custom_call_target="tpu_custom_call" | custom-call | flops 1 | bytes 1 | tf_op jit(solution)/shard_map/project/pallas_call | solution.py:68
  117.7 11.0 %attend.1 = (bf16[16,256,256]{2,1,0:T(8,128)(2,1)}, bf16[256,2048]{1,0:T(8,128)(2,1)}, bf16[2048,256]{1,0:T(8,128)(2,1)}) custom-call(s32[2]{0:T(128)} %pad_add_fusion.refs_0_, bf16[256,2048]{1,0:T(8,128)(2,1)} %get-tuple-element.135.refs_1_.refs_4_, bf16[256,256]{1,0:T(8,128)(2,1)} %get-tuple-element.119.refs_2_.refs_5_), custom_call_target="tpu_custom_call" | custom-call | flops 1 | bytes 1 | tf_op jit(solution)/shard_map/attend/pallas_call | solution.py:68
  148.2 11.0 %mix.1 = (f32[256,2048]{1,0:T(8,128)}, bf16[128,2048]{1,0:T(8,128)(2,1)}, bf16[128,2048]{1,0:T(8,128)(2,1)}) custom-call(s32[2]{0:T(128)} %pad_add_fusion.refs_0_, bf16[256,2048]{1,0:T(8,128)(2,1)} %refs_1_.5, bf16[256,2048]{1,0:T(8,128)(2,1)} %get-tuple-element.137.refs_2_, f32[8,2048]{1,0:T(8,128)} %get-tuple-element.138.refs_3_.refs_2_, ...), custom_call_target="tpu_custom_call" | custom-call | flops 1 | bytes 1 | tf_op jit(solution)/shard_map/mix/pallas_call | solution.py:68
  161.4 12.1 %collective-permute-done.34.refs_2_.refs_4_ = bf16[128,2048]{1,0:T(8,128)(2,1)S(1)} collective-permute-done((bf16[128,2048]{1,0:T(8,128)(2,1)}, bf16[128,2048]{1,0:T(8,128)(2,1)S(1)}, u32[]{:S(2)}, u32[]{:S(2)}) %collective-permute-start.34) | collective-permute-done | bytes 524320 | tf_op jit(solution)/shard_map/ppermute | solution.py:749
  178.7 11.0 %collective-permute-done.37.refs_4_.refs_6_ = bf16[128,2048]{1,0:T(8,128)(2,1)S(1)} collective-permute-done((bf16[128,2048]{1,0:T(8,128)(2,1)}, bf16[128,2048]{1,0:T(8,128)(2,1)S(1)}, u32[]{:S(2)}, u32[]{:S(2)}) %collective-permute-start.37) | collective-permute-done | bytes 524320 | tf_op jit(solution)/shard_map/ppermute | solution.py:752
  201.9 13.9 %gate.2 = (bf16[1024,704]{1,0:T(8,128)(2,1)}, bf16[1024,704]{1,0:T(8,128)(2,1)}, bf16[1024,704]{1,0:T(8,128)(2,1)}) custom-call(bf16[128,2048]{1,0:T(8,128)(2,1)} %get-tuple-element.162.refs_0_.refs_2_, bf16[128,2048]{1,0:T(8,128)(2,1)} %get-tuple-element.163.refs_1_.refs_3_, bf16[128,2048]{1,0:T(8,128)(2,1)} %copy-done.10, bf16[128,2048]{1,0:T(8,128)(2,1)} %copy-done.13, ...), custom_call_target="tpu_custom_call" | custom-call | flops 1 | bytes 1 | tf_op jit(solution)/shard_map/gate/pallas_call | solution.py:68
  215.8 14.0 %gate.3 = (bf16[1024,704]{1,0:T(8,128)(2,1)}, bf16[1024,704]{1,0:T(8,128)(2,1)}, bf16[1024,704]{1,0:T(8,128)(2,1)}) custom-call(bf16[128,2048]{1,0:T(8,128)(2,1)} %get-tuple-element.162.refs_0_.refs_2_, bf16[128,2048]{1,0:T(8,128)(2,1)} %get-tuple-element.163.refs_1_.refs_3_, bf16[128,2048]{1,0:T(8,128)(2,1)} %copy-done.10, bf16[128,2048]{1,0:T(8,128)(2,1)} %copy-done.13, ...), custom_call_target="tpu_custom_call" | custom-call | flops 1 | bytes 1 | tf_op jit(solution)/shard_map/gate/pallas_call | solution.py:68
  246.7 10.4 %hidden_sums.5 = bf16[704,2048]{1,0:T(8,128)(2,1)} custom-call(bf16[1024,704]{1,0:T(8,128)(2,1)} %get-tuple-element.167.refs_9_.refs_0_, bf16[128,2048]{1,0:T(8,128)(2,1)} %copy-done.1, bf16[128,2048]{1,0:T(8,128)(2,1)} %copy-done, bf16[128,2048]{1,0:T(8,128)(2,1)} %copy-done.5, bf16[128,2048]{1,0:T(8,128)(2,1)} %copy-done.9, bf16[128,2048]{1,0:T(8,128)(2,1)} %copy-done.8, ...), custom_call_target="tpu_custom_call" | custom-call | flops 1 | bytes 1 | tf_op jit(solution)/shard_map/hidden_sums/pallas_call | solution.py:68
  260.5 9.8 %gate_back.2 = (bf16[1024,704]{1,0:T(8,128)(2,1)}, bf16[1024,704]{1,0:T(8,128)(2,1)}) custom-call(bf16[128,2048]{1,0:T(8,128)(2,1)} %copy-done.1, bf16[128,2048]{1,0:T(8,128)(2,1)} %copy-done, bf16[128,2048]{1,0:T(8,128)(2,1)} %copy-done.5, bf16[128,2048]{1,0:T(8,128)(2,1)} %copy-done.9, bf16[128,2048]{1,0:T(8,128)(2,1)} %copy-done.8, ...), custom_call_target="tpu_custom_call" | custom-call | flops 1 | bytes 1 | tf_op jit(solution)/shard_map/gate_back/pallas_call | solution.py:68
  270.3 9.8 %gate_back.3 = (bf16[1024,704]{1,0:T(8,128)(2,1)}, bf16[1024,704]{1,0:T(8,128)(2,1)}) custom-call(bf16[128,2048]{1,0:T(8,128)(2,1)} %copy-done.1, bf16[128,2048]{1,0:T(8,128)(2,1)} %copy-done, bf16[128,2048]{1,0:T(8,128)(2,1)} %copy-done.5, bf16[128,2048]{1,0:T(8,128)(2,1)} %copy-done.9, bf16[128,2048]{1,0:T(8,128)(2,1)} %copy-done.8, ...), custom_call_target="tpu_custom_call" | custom-call | flops 1 | bytes 1 | tf_op jit(solution)/shard_map/gate_back/pallas_call | solution.py:68
  280.1 22.6 %rows_back.1 = (bf16[128,2048]{1,0:T(8,128)(2,1)}, bf16[128,2048]{1,0:T(8,128)(2,1)}, bf16[128,2048]{1,0:T(8,128)(2,1)}, bf16[128,2048]{1,0:T(8,128)(2,1)}, bf16...) custom-call(bf16[1024,704]{1,0:T(8,128)(2,1)} %get-tuple-element.176.refs_11_.refs_0_, ...), custom_call_target="tpu_custom_call" | custom-call | flops 1 | bytes 1 | tf_op jit(solution)/shard_map/rows_back/pallas_call | solution.py:68
  305.7 13.9 %hidden_sums.6 = (bf16[176,2048]{1,0:T(8,128)(2,1)}, bf16[176,2048]{1,0:T(8,128)(2,1)}, bf16[176,2048]{1,0:T(8,128)(2,1)}, bf16[176,2048]{1,0:T(8,128)(2,1)}, bf...) custom-call(bf16[1024,704]{1,0:T(8,128)(2,1)} %get-tuple-element.180, ...), custom_call_target="tpu_custom_call" | custom-call | flops 1 | bytes 1 | tf_op jit(solution)/shard_map/hidden_sums/pallas_call | solution.py:68
  333.8 15.8 %hidden_sums.7.refs_10_ = bf16[1408,2048]{1,0:T(8,128)(2,1)} custom-call(bf16[1024,704]{1,0:T(8,128)(2,1)} %get-tuple-element.176.refs_11_.refs_0_, bf16[1024,704]{1,0:T(8,128)(2,1)} %get-tuple-element.177.refs_1_, bf16[128,2048]{1,0:T(8,128)(2,1)} %get-tuple-element.162.refs_0_.refs_2_, bf16[128,2048]{1,0:T(8,128)(2,1)} %get-tuple-element.163.refs_1_.refs_3_, ...), custom_call_target="tpu_custom_call" | custom-call | flops 1 | bytes 1 | tf_op jit(solution)/shard_map/hidden_sums/pallas_call | solution.py:68
  352.7 11.3 %collective-permute-done.49.refs_9_ = bf16[128,2048]{1,0:T(8,128)(2,1)S(1)} collective-permute-done((bf16[128,2048]{1,0:T(8,128)(2,1)S(1)}, bf16[128,2048]{1,0:T(8,128)(2,1)S(1)}, u32[]{:S(2)}, u32[]{:S(2)}) %collective-permute-start.49) | collective-permute-done | bytes 524320 | tf_op jit(solution)/shard_map/ppermute | solution.py:752
  394.7 20.8 %attend_back.1 = (bf16[256,2304]{1,0:T(8,128)(2,1)}, f32[256,256]{1,0:T(8,128)}) custom-call(s32[2]{0:T(128)} %pad_add_fusion.refs_0_, f32[1]{0:T(128)} %bitcast.9.refs_0_.refs_1_, bf16[256,2048]{1,0:T(8,128)(2,1)} %get-tuple-element.200.refs_1_.refs_2_, bf16[256,256]{1,0:T(8,128)(2,1)} %refs_3_.3, bf16[256,2048]{1,0:T(8,128)(2,1)} %get-tuple-element.135.refs_1_.refs_4_, ...), custom_call_target="tpu_custom_call" | custom-call | flops 1 | bytes 1 | tf_op jit(solution)/shard_map/attend_back/pallas_call | solution.py:68
  448.1 12.8 %finish.1 = (f32[256,2048]{1,0:T(8,128)}, f32[8,2048]{1,0:T(8,128)}) custom-call(s32[2]{0:T(128)} %pad_add_fusion.refs_0_, bf16[256,2048]{1,0:T(8,128)(2,1)} %refs_1_.5, f32[8,2048]{1,0:T(8,128)} %get-tuple-element.138.refs_3_.refs_2_, bf16[256,2304]{1,0:T(8,128)(2,1)} %get-tuple-element.206.refs_4_.refs_1_.refs_3_, f32[256,2048]{1,0:T(8,128)} %get-tuple-element.219.refs_4_, ...), custom_call_target="tpu_custom_call" | custom-call | flops 1 | bytes 1 | tf_op jit(solution)/shard_map/finish/pallas_call | solution.py:68
  461.9 9.6 %collective-permute-done.64.refs_3_ = bf16[256,2304]{1,0:T(8,128)(2,1)S(1)} collective-permute-done((bf16[256,2304]{1,0:T(8,128)(2,1)}, bf16[256,2304]{1,0:T(8,128)(2,1)S(1)}, u32[]{:S(2)}, u32[]{:S(2)}) %collective-permute-start.64) | collective-permute-done | bytes 1179680 | tf_op jit(solution)/shard_map/ppermute | solution.py:752
  482.9 11.8 %down.1 = (bf16[128,2048]{1,0:T(8,128)(2,1)}, bf16[128,2048]{1,0:T(8,128)(2,1)}, bf16[128,2048]{1,0:T(8,128)(2,1)}, bf16[128,2048]{1,0:T(8,128)(2,1)}, bf16[256,...) custom-call(bf16[1024,704]{1,0:T(8,128)(2,1)} %get-tuple-element.167.refs_9_.refs_0_, ...), custom_call_target="tpu_custom_call" | custom-call | flops 1 | bytes 1 | tf_op jit(solution)/shard_map/down/pallas_call | solution.py:68
  500.3 19.2 %collective-permute-done.68.refs_3_ = bf16[256,2048]{1,0:T(8,128)(2,1)S(1)} collective-permute-done((bf16[256,2048]{1,0:T(8,128)(2,1)}, bf16[256,2048]{1,0:T(8,128)(2,1)S(1)}, u32[]{:S(2)}, u32[]{:S(2)}) %collective-permute-start.68) | collective-permute-done | bytes 1048608 | tf_op jit(solution)/shard_map/ppermute | solution.py:752
  (353 shorter events, 224.4 us)
Async XLA Ops:
  7.2 38.3 %all-gather.5.cloned.1.call-start = ((), (), s32[]{:S(2)}) async-start(), calls=%async_computation.4 | async-start | bytes 1556480 | tf_op jit(solution)/shard_map/all_gather | solution.py:771
  9.8 83.4 %all-gather.7.cloned.1.call-start = ((), (), s32[]{:S(2)}) async-start(), calls=%async_computation.5 | async-start | bytes 1310720 | tf_op jit(solution)/shard_map/all_gather | solution.py:771
  10.5 189.3 %all-gather.9.cloned.1.call-start = ((), (), s32[]{:S(2)}) async-start(), calls=%async_computation.6 | async-start | bytes 7208960 | tf_op jit(solution)/shard_map/all_gather | solution.py:771
  13.7 245.0 %all-gather.11.cloned.1.call-start = ((), (), s32[]{:S(2)}) async-start(), calls=%async_computation.7 | async-start | bytes 3604480 | tf_op jit(solution)/shard_map/all_gather | solution.py:771
  65.3 27.9 %collective-permute-start.8 = (bf16[2,64,2432]{2,1,0:T(8,128)(2,1)}, bf16[2,64,2432]{2,1,0:T(8,128)(2,1)}, u32[]{:S(2)}, u32[]{:S(2)}) collective-permute-start(bf16[2,64,2432]{2,1,0:T(8,128)(2,1)} %collective-permute-done.4.refs_8_.refs_9_), channel_id=1, source_target_pairs={{0,1},{1,0},{2,3},{3,2},{4,5},{5,4},{6,7},{7,6},{8,9},{9,8},{10,11... | collective-permute-start | bytes 1867784 | tf_op jit(solution)/shard_map/ppermute | solution.py:752
  65.9 27.3 %collective-permute-start.11 = (bf16[2,64,2432]{2,1,0:T(8,128)(2,1)}, bf16[2,64,2432]{2,1,0:T(8,128)(2,1)}, u32[]{:S(2)}, u32[]{:S(2)}) collective-permute-start(bf16[2,64,2432]{2,1,0:T(8,128)(2,1)} %bitcast.6.refs_5_.refs_6_), channel_id=1, source_target_pairs={{0,8},{8,0},{16,24},{24,16},{1,9},{9,1},{17,25},{25,17},{2,10},{10... | collective-permute-start | bytes 1867784 | tf_op jit(solution)/shard_map/ppermute | solution.py:738
  65.9 28.7 %collective-permute-start.7 = (bf16[2,64,2432]{2,1,0:T(8,128)(2,1)}, bf16[2,64,2432]{2,1,0:T(8,128)(2,1)}, u32[]{:S(2)}, u32[]{:S(2)}) collective-permute-start(bf16[2,64,2432]{2,1,0:T(8,128)(2,1)} %bitcast.6.refs_5_.refs_6_), channel_id=1, source_target_pairs={{0,16},{8,24},{16,0},{24,8},{1,17},{9,25},{17,1},{25,9},{2,18},{10... | collective-permute-start | bytes 1867784 | tf_op jit(solution)/shard_map/ppermute | solution.py:749
  116.6 22.9 %collective-permute-start.23 = (bf16[2,64,2048]{2,1,0:T(8,128)(2,1)S(1)}, bf16[2,64,2048]{2,1,0:T(8,128)(2,1)}, u32[]{:S(2)}, u32[]{:S(2)}) collective-permute-start(bf16[2,64,2048]{2,1,0:T(8,128)(2,1)S(1)} %collective-permute-done.19.refs_7_.refs_12_), channel_id=1, source_target_pairs={{0,16},{8,24},{16,0},{24,8},{1,17},{9,25},{17,1},{25,9},{2,18},{10... | collective-permute-start | bytes 1572872 | tf_op jit(solution)/shard_map/ppermute | solution.py:749
  175.8 23.2 %collective-permute-start.38 = (bf16[128,2048]{1,0:T(8,128)(2,1)S(1)}, bf16[128,2048]{1,0:T(8,128)(2,1)S(1)}, u32[]{:S(2)}, u32[]{:S(2)}) collective-permute-start(bf16[128,2048]{1,0:T(8,128)(2,1)S(1)} %collective-permute-done.34.refs_2_.refs_4_), channel_id=1, source_target_pairs={{0,1},{1,0},{2,3},{3,2},{4,5},{5,4},{6,7},{7,6},{8,9},{9,8},{10,11... | collective-permute-start | bytes 1572872 | tf_op jit(solution)/shard_map/ppermute | solution.py:752
  177.3 22.6 %collective-permute-start.39 = (bf16[128,2048]{1,0:T(8,128)(2,1)S(1)}, bf16[128,2048]{1,0:T(8,128)(2,1)}, u32[]{:S(2)}, u32[]{:S(2)}) collective-permute-start(bf16[128,2048]{1,0:T(8,128)(2,1)S(1)} %collective-permute-done.35.refs_5_.refs_7_), channel_id=1, source_target_pairs={{0,16},{8,24},{16,0},{24,8},{1,17},{9,25},{17,1},{25,9},{2,18},{10... | collective-permute-start | bytes 1572872 | tf_op jit(solution)/shard_map/ppermute | solution.py:749
  199.8 149.7 %reduce-scatter.5.cloned.1.call-start = ((), (), s32[]{:S(2)}) async-start(), calls=%async_computation.8 | async-start | bytes 3604480 | tf_op jit(solution)/shard_map/reduce_scatter | solution.py:774
  200.1 29.7 %collective-permute-start.33 = (bf16[128,2048]{1,0:T(8,128)(2,1)S(1)}, bf16[128,2048]{1,0:T(8,128)(2,1)S(1)}, u32[]{:S(2)}, u32[]{:S(2)}) collective-permute-start(bf16[128,2048]{1,0:T(8,128)(2,1)S(1)} %get-tuple-element.158.refs_1_.refs_0_), channel_id=1, source_target_pairs={{0,1},{1,0},{2,3},{3,2},{4,5},{5,4},{6,7},{7,6},{8,9},{9,8},{10,11... | collective-permute-start | bytes 1572872 | tf_op jit(solution)/shard_map/ppermute | solution.py:752
  201.2 28.6 %collective-permute-start.32 = (bf16[128,2048]{1,0:T(8,128)(2,1)S(1)}, bf16[128,2048]{1,0:T(8,128)(2,1)S(1)}, u32[]{:S(2)}, u32[]{:S(2)}) collective-permute-start(bf16[128,2048]{1,0:T(8,128)(2,1)S(1)} %get-tuple-element.159.refs_2_.refs_1_), channel_id=1, source_target_pairs={{0,16},{8,24},{16,0},{24,8},{1,17},{9,25},{17,1},{25,9},{2,18},{10... | collective-permute-start | bytes 1572872 | tf_op jit(solution)/shard_map/ppermute | solution.py:749
  258.7 213.4 %reduce-scatter.7.cloned.1.call-start = ((), (), s32[]{:S(2)}) async-start(), calls=%async_computation.9 | async-start | bytes 7208960 | tf_op jit(solution)/shard_map/reduce_scatter | solution.py:774
  302.7 25.8 %collective-permute-start.46 = (bf16[256,2048]{1,0:T(8,128)(2,1)}, bf16[256,2048]{1,0:T(8,128)(2,1)S(1)}, u32[]{:S(2)}, u32[]{:S(2)}) collective-permute-start(bf16[256,2048]{1,0:T(8,128)(2,1)} %get-tuple-element.183), channel_id=1, source_target_pairs={{0,1},{1,0},{2,3},{3,2},{4,5},{5,4},{6,7},{7,6},{8,9},{9,8},{10,11... | collective-permute-start | bytes 3145736 | tf_op jit(solution)/shard_map/ppermute | solution.py:752
  304.2 25.5 %collective-permute-start.47 = (bf16[256,2048]{1,0:T(8,128)(2,1)}, bf16[256,2048]{1,0:T(8,128)(2,1)S(1)}, u32[]{:S(2)}, u32[]{:S(2)}) collective-permute-start(bf16[256,2048]{1,0:T(8,128)(2,1)} %get-tuple-element.186), channel_id=1, source_target_pairs={{0,16},{8,24},{16,0},{24,8},{1,17},{9,25},{17,1},{25,9},{2,18},{10... | collective-permute-start | bytes 3145736 | tf_op jit(solution)/shard_map/ppermute | solution.py:749
  349.6 178.5 %reduce-scatter.11.cloned.1.call-start = ((), (), s32[]{:S(2)}) async-start(), calls=%async_computation.11 | async-start | bytes 1310720 | tf_op jit(solution)/shard_map/reduce_scatter | solution.py:774
  392.3 25.5 %collective-permute-start.60 = (bf16[256,2048]{1,0:T(8,128)(2,1)}, bf16[256,2048]{1,0:T(8,128)(2,1)S(1)}, u32[]{:S(2)}, u32[]{:S(2)}) collective-permute-start(bf16[256,2048]{1,0:T(8,128)(2,1)} %get-tuple-element.209), channel_id=1, source_target_pairs={{0,16},{8,24},{16,0},{24,8},{1,17},{9,25},{17,1},{25,9},{2,18},{10... | collective-permute-start | bytes 3145736 | tf_op jit(solution)/shard_map/ppermute | solution.py:749
  393.8 25.1 %collective-permute-start.61 = (bf16[256,2048]{1,0:T(8,128)(2,1)}, bf16[256,2048]{1,0:T(8,128)(2,1)S(1)}, u32[]{:S(2)}, u32[]{:S(2)}) collective-permute-start(bf16[256,2048]{1,0:T(8,128)(2,1)} %get-tuple-element.210), channel_id=1, source_target_pairs={{0,1},{1,0},{2,3},{3,2},{4,5},{5,4},{6,7},{7,6},{8,9},{9,8},{10,11... | collective-permute-start | bytes 3145736 | tf_op jit(solution)/shard_map/ppermute | solution.py:752
  443.2 28.3 %collective-permute-start.64 = (bf16[256,2304]{1,0:T(8,128)(2,1)}, bf16[256,2304]{1,0:T(8,128)(2,1)S(1)}, u32[]{:S(2)}, u32[]{:S(2)}) collective-permute-start(bf16[256,2304]{1,0:T(8,128)(2,1)} %get-tuple-element.215), channel_id=1, source_target_pairs={{0,1},{1,0},{2,3},{3,2},{4,5},{5,4},{6,7},{7,6},{8,9},{9,8},{10,11... | collective-permute-start | bytes 3538952 | tf_op jit(solution)/shard_map/ppermute | solution.py:752
  444.1 27.9 %collective-permute-start.65 = (bf16[256,2304]{1,0:T(8,128)(2,1)}, bf16[256,2304]{1,0:T(8,128)(2,1)S(1)}, u32[]{:S(2)}, u32[]{:S(2)}) collective-permute-start(bf16[256,2304]{1,0:T(8,128)(2,1)} %get-tuple-element.218), channel_id=1, source_target_pairs={{0,16},{8,24},{16,0},{24,8},{1,17},{9,25},{17,1},{25,9},{2,18},{10... | collective-permute-start | bytes 3538952 | tf_op jit(solution)/shard_map/ppermute | solution.py:749
  478.0 60.5 %reduce-scatter.9.cloned.1.call-start = ((), (), s32[]{:S(2)}) async-start(), calls=%async_computation.10 | async-start | bytes 1556480 | tf_op jit(solution)/shard_map/reduce_scatter | solution.py:774
  496.4 23.1 %collective-permute-start.68 = (bf16[256,2048]{1,0:T(8,128)(2,1)}, bf16[256,2048]{1,0:T(8,128)(2,1)S(1)}, u32[]{:S(2)}, u32[]{:S(2)}) collective-permute-start(bf16[256,2048]{1,0:T(8,128)(2,1)} %get-tuple-element.231), channel_id=1, source_target_pairs={{0,1},{1,0},{2,3},{3,2},{4,5},{5,4},{6,7},{7,6},{8,9},{9,8},{10,11... | collective-permute-start | bytes 3145736 | tf_op jit(solution)/shard_map/ppermute | solution.py:752
  497.4 22.8 %collective-permute-start.69 = (bf16[256,2048]{1,0:T(8,128)(2,1)}, bf16[256,2048]{1,0:T(8,128)(2,1)S(1)}, u32[]{:S(2)}, u32[]{:S(2)}) collective-permute-start(bf16[256,2048]{1,0:T(8,128)(2,1)} %get-tuple-element.234), channel_id=1, source_target_pairs={{0,16},{8,24},{16,0},{24,8},{1,17},{9,25},{17,1},{25,9},{2,18},{10... | collective-permute-start | bytes 3145736 | tf_op jit(solution)/shard_map/ppermute | solution.py:749
  (130 other events, 1717.1 us)
Sparse Core Ops, SparseCore 0:
  10.2 34.2 all-gather.4
  46.0 26.9 all-gather.6
  75.2 106.1 all-gather.8
  200.0 58.6 all-gather.10
  261.4 54.8 reduce-scatter.4
  349.7 100.2 reduce-scatter.6
  478.2 25.5 reduce-scatter.10
  506.2 28.8 reduce-scatter.8

commit v5 on v4

--- a/solution.py
+++ b/solution.py
@@ -121,7 +121,7 @@
     def __init__(self, depth, rows, columns, arrays):
         self.depth, self.rows, self.columns, self.arrays = depth, rows, columns, arrays
 
-    def start(self, refs, spot, whole, sem):
+    def start(self, refs, spot, whole, sem, apart=False):
         cut = self.depth // 2
         place = 0
         for flip in range(2):
@@ -134,12 +134,19 @@
                             ) * 2 + (spot[1] ^ dy)
                             row = pl.multiple_of(block * self.rows, self.rows)
                             pltpu.make_async_copy(
-                                refs[place].at[outer - low], whole.at[pl.ds(row, self.rows)], sem
+                                refs[place].at[outer - low],
+                                whole.at[pl.ds(row, self.rows)],
+                                sem.at[2 * dx + flip] if apart else sem,
                             ).start()
                         place += 1
 
     def wait(self, whole, sem):
         pltpu.make_async_copy(whole, whole, sem).wait()
+
+    def group(self, whole, spot, index):
+        flip = (index % 2) * 2 + index // 2
+        size = whole.shape[0] // 4
+        return pl.multiple_of((spot[0] ^ flip) * size, size), size, flip
 
 
 def swap_halves(value):
@@ -270,20 +277,26 @@
     shards = refs[4 : 4 + count]
     mid_out, first_out, second_out = refs[4 + count : 7 + count]
     whole, sem = refs[7 + count :]
-    pieces.start(shards, spot, whole, sem)
+    pieces.start(shards, spot, whole, sem, True)
     length, width = tokens.shape
-    pieces.wait(whole, sem)
-
-    def add(block, total):
-        start = pl.multiple_of(block * step, step)
-        branch = jnp.dot(attended[...], whole[:, pl.ds(start, step)], preferred_element_type=f32)
-        x_mid = tokens[:, pl.ds(start, step)].astype(f32) + branch
-        mid_out[:, pl.ds(start, step)] = x_mid
-        return total + jnp.sum(x_mid * x_mid, axis=-1, keepdims=True)
-
-    total = lax.fori_loop(0, width // step, add, jnp.zeros((length, 1), f32))
-    inverse = lax.rsqrt(total / width + epsilon)
-    h_two = (mid_out[...] * inverse * gains[1:2, :]).astype(bf16)
+    mid_out[...] = tokens[...].astype(f32)
+
+    @pl.loop(0, 4)
+    def _(index):
+        row, size, flip = pieces.group(whole, spot, index)
+        rows = pl.ds(row, size)
+        wait_all(whole.at[rows], sem.at[flip])
+
+        @pl.loop(0, width // (2 * step))
+        def _(block):
+            columns = pl.ds(pl.multiple_of(block * 2 * step, 2 * step), 2 * step)
+            mid_out[:, columns] += jnp.dot(
+                attended[:, rows], whole[rows, columns], preferred_element_type=f32
+            )
+
+    x_mid = mid_out[...]
+    inverse = lax.rsqrt(jnp.mean(x_mid * x_mid, axis=-1, keepdims=True) + epsilon)
+    h_two = (x_mid * inverse * gains[1:2, :]).astype(bf16)
     first_out[...] = h_two[: length // 2]
     second_out[...] = h_two[length // 2 :]
 
@@ -296,7 +309,7 @@
     return kernel_call(
         functools.partial(mix_body, pieces),
         (shape((length, width), f32), half, half),
-        [pltpu.VMEM((rows, width), bf16), pltpu.SemaphoreType.DMA],
+        [pltpu.VMEM((rows, width), bf16), pltpu.SemaphoreType.DMA((4,))],
         [smem_spec(), vmem_spec(), vmem_spec(), vmem_spec()] + [any_spec()] * len(pieces.arrays),
     )(spot, tokens, attended, gains, *pieces.arrays, *late)
 
@@ -346,26 +359,32 @@
     shards = refs[9 : 9 + count]
     joined, d_kv_out = refs[9 + count : 11 + count]
     whole, sem = refs[11 + count :]
-    pieces.start(shards, spot, whole, sem)
+    pieces.start(shards, spot, whole, sem, True)
     length = d_mid_low.shape[0]
     q_width = q_low.shape[1]
     scale = head_dim ** (-0.5)
     cos, sin = cosines[...], sines[...]
     keys, values = kv_low[:, :head_dim], kv_low[:, head_dim:]
     d_kv_out[...] = grad_kv[...].astype(f32) * factor[0]
-    pieces.wait(whole, sem)
     heads = step // head_dim
 
     @pl.loop(0, q_width // step)
     def _(block):
-        start = pl.multiple_of(block * step, step)
+        row, size, flip = pieces.group(whole, spot, block // (whole.shape[0] // 4 // step))
+        inside = block % (size // step)
+
+        @pl.when(inside == 0)
+        def _():
+            wait_all(whole.at[pl.ds(row, size)], sem.at[flip])
+
+        start = pl.multiple_of(row + inside * step, step)
         d_att = contract_last(d_mid_low[...], whole[pl.ds(start, step), :]).astype(bf16)
         d_k = jnp.zeros((length, head_dim), f32)
         d_v = jnp.zeros((length, head_dim), f32)
         for head in range(heads):
             own = d_att[:, head * head_dim : (head + 1) * head_dim]
             column = pl.multiple_of(start + head * head_dim, head_dim)
-            low = prob_ref[block * heads + head]
+            low = prob_ref[start // head_dim + head]
             prob = low.astype(f32)
             d_prob = contract_last(values, own)
             centre = jnp.sum(prob * d_prob, axis=0, keepdims=True)
@@ -390,7 +409,7 @@
     return kernel_call(
         functools.partial(attend_back_body, pieces, head_dim),
         (shape((length, q_width + kv_width), bf16), shape((length, kv_width), f32)),
-        [pltpu.VMEM((q_width, width), bf16), pltpu.SemaphoreType.DMA],
+        [pltpu.VMEM((q_width, width), bf16), pltpu.SemaphoreType.DMA((4,))],
         [smem_spec()] * 2 + [vmem_spec()] * 7 + [any_spec()] * len(pieces.arrays),
     )(spot, factor, d_mid_low, grad_kv, q_low, kv_low, prob, cosines, sines, *pieces.arrays, *late)
 
@@ -461,9 +480,9 @@
 
 
 def gate_body(shard, count, *refs):
-    parts, both = refs[:count], refs[count]
-    hid, by_gate, by_up = refs[count + 1 : count + 4]
-    rows, gate_w, up_w, row_sems, gate_sem, up_sem = refs[count + 4 :]
+    parts, both, outs = refs[:count], refs[count], refs[count + 1 : count + 4]
+    held, refs = refs[count + 4 : count + 7], refs[count + 7 :]
+    rows, gate_w, up_w, row_sems, gate_sem, up_sem, out_sem = refs
     waits = fetch_gate_up(both, shard, gate_w, up_w, gate_sem, up_sem)
     fetch_row_blocks(parts, rows, row_sems)
     for wait in waits:
@@ -477,9 +496,14 @@
         up = contract_last(rows[own, :], up_w[...])
         sigma = 1.0 / (1.0 + jnp.exp(-gate))
         silu = gate * sigma
-        hid[own, :] = (silu * up).astype(bf16)
-        by_gate[own, :] = (up * sigma * (1.0 + gate * (1.0 - sigma))).astype(bf16)
-        by_up[own, :] = silu.astype(bf16)
+        held[0][own, :] = (silu * up).astype(bf16)
+        held[1][own, :] = (up * sigma * (1.0 + gate * (1.0 - sigma))).astype(bf16)
+        held[2][own, :] = silu.astype(bf16)
+        for source, out in zip(held, outs):
+            pltpu.make_async_copy(source.at[own], out.at[own], out_sem).start()
+
+    for source in held:
+        wait_all(source, out_sem)
 
 
 def gate(parts, both, shard, late=()):
@@ -489,67 +513,95 @@
     return kernel_call(
         functools.partial(gate_body, shard, len(parts)),
         (out, out, out),
-        [pltpu.VMEM((total, width), bf16)]
+        [pltpu.VMEM((total, hidden), bf16)] * 3
+        + [pltpu.VMEM((total, width), bf16)]
         + [pltpu.VMEM((hidden, width), bf16)] * 2
-        + [pltpu.SemaphoreType.DMA((total // step,)), pltpu.SemaphoreType.DMA, pltpu.SemaphoreType.DMA],
+        + [pltpu.SemaphoreType.DMA((total // step,))]
+        + [pltpu.SemaphoreType.DMA] * 3,
         [any_spec()] * (len(parts) + 1),
+        any_spec,
     )(*parts, both, *late)
 
 
 def gate_back_body(count, *refs):
     parts, weight, scales, grads = refs[:count], refs[count], refs[count + 1 : count + 3], refs[count + 3 : count + 5]
-    rows, row_sems = refs[count + 5 :]
+    rows, weight_in, first, second, row_sems, weight_sem, out_sem = refs[count + 5 :]
+    wait = fetch_rows([weight], weight_in, weight_sem)
+    scaled = (first, second)
+    for source, held in zip(scales, scaled):
+        for block in range(rows.shape[0] // step):
+            own = pl.ds(block * step, step)
+            pltpu.make_async_copy(source.at[own], held.at[own], row_sems.at[block]).start()
     fetch_row_blocks(parts, rows, row_sems)
+    wait()
 
     @pl.loop(0, rows.shape[0] // step)
     def _(block):
         own = pl.ds(pl.multiple_of(block * step, step), step)
-        wait_all(rows.at[own], row_sems.at[block])
-        d_hid = contract_last(rows[own, :], weight[...])
-        for scale, grad in zip(scales, grads):
-            grad[own, :] = (d_hid * scale[own, :].astype(f32)).astype(bf16)
+        for whole in (rows, first, second):
+            wait_all(whole.at[own], row_sems.at[block])
+        d_hid = contract_last(rows[own, :], weight_in[...])
+        for held, grad in zip(scaled, grads):
+            held[own, :] = (d_hid * held[own, :].astype(f32)).astype(bf16)
+            pltpu.make_async_copy(held.at[own], grad.at[own], out_sem).start()
+
+    for held in scaled:
+        wait_all(held, out_sem)
 
 
 def gate_back(parts, weight, scales, late=()):
     count = len(parts)
     total, width = sum(part.shape[0] for part in parts), parts[0].shape[1]
-    grad = jax.ShapeDtypeStruct((total, weight.shape[0]), bf16)
+    hidden = weight.shape[0]
+    grad = jax.ShapeDtypeStruct((total, hidden), bf16)
     return kernel_call(
         functools.partial(gate_back_body, count),
         (grad, grad),
-        [pltpu.VMEM((total, width), bf16), pltpu.SemaphoreType.DMA((total // step,))],
-        [any_spec()] * count + [vmem_spec()] * 3,
+        [pltpu.VMEM((total, width), bf16), pltpu.VMEM((hidden, width), bf16)]
+        + [pltpu.VMEM((total, hidden), bf16)] * 2
+        + [pltpu.SemaphoreType.DMA((total // step,))]
+        + [pltpu.SemaphoreType.DMA] * 2,
+        [any_spec()] * (count + 3),
+        any_spec,
     )(*parts, weight, *scales, *late)
 
 
 def rows_back_body(shard, *refs):
     grads, boths, outs = refs[:4], refs[4:6], refs[6:12]
-    weights, held, sems = refs[12:16], refs[16], refs[17]
-    waits = []
-    for place in range(2):
-        waits += fetch_gate_up(
-            boths[place], shard, weights[2 * place], weights[2 * place + 1],
-            sems.at[2 * place], sems.at[2 * place + 1],
-        )
-    for wait in waits:
-        wait()
-    size = held.shape[0] // 8
-
-    @pl.loop(0, 4)
-    def _(index):
-        own = pl.ds(pl.multiple_of(index * 2 * size, 2 * size), 2 * size)
-
-        @pl.loop(0, held.shape[1] // (4 * step))
-        def _(block):
-            columns = pl.ds(pl.multiple_of(block * 4 * step, 4 * step), 4 * step)
+    weights, held, sems, out_sem = refs[12:16], refs[16], refs[17], refs[18]
+    size, chunk = held.shape[0] // 8, 2 * step
+    chunks = held.shape[1] // chunk
+
+    @pl.loop(0, chunks)
+    def _(block):
+        columns = pl.ds(pl.multiple_of(block * chunk, chunk), chunk)
+        for place, weight in enumerate(weights):
+            for outer in range(weight.shape[0] // shard):
+                source = boths[place // 2].at[pl.ds((2 * outer + place % 2) * shard, shard), columns]
+                target = weight.at[pl.ds(outer * shard, shard), columns]
+                pltpu.make_async_copy(source, target, sems.at[block]).start()
+
+    @pl.loop(0, chunks)
+    def _(block):
+        columns = pl.ds(pl.multiple_of(block * chunk, chunk), chunk)
+        for weight in weights:
+            wait_all(weight.at[:, columns], sems.at[block])
+
+        @pl.loop(0, 4)
+        def _(index):
+            own = pl.ds(pl.multiple_of(index * 2 * size, 2 * size), 2 * size)
             total = jnp.dot(grads[0][own, :], weights[0][:, columns], preferred_element_type=f32)
             for grad, piece in zip(grads[1:], weights[1:]):
                 total += jnp.dot(grad[own, :], piece[:, columns], preferred_element_type=f32)
             held[own, columns] = total.astype(bf16)
 
-        send_blocks(row_route, outs, held, index, size, sems.at[4])
-
-    wait_all(held, sems.at[4])
+        for blocks, out in zip(row_route, outs):
+            for spot, place in enumerate(blocks):
+                source = held.at[pl.ds(place * size, size), columns]
+                target = out.at[pl.ds(spot * size, size), columns]
+                pltpu.make_async_copy(source, target, out_sem).start()
+
+    wait_all(held, out_sem)
 
 
 def rows_back(grads, boths, shard, late=()):
@@ -559,7 +611,11 @@
         functools.partial(rows_back_body, shard),
         routed(total // 8, width),
         [pltpu.VMEM((hidden, width), bf16)] * 4
-        + [pltpu.VMEM((total, width), bf16), pltpu.SemaphoreType.DMA((5,))],
+        + [
+            pltpu.VMEM((total, width), bf16),
+            pltpu.SemaphoreType.DMA((width // (2 * step),)),
+            pltpu.SemaphoreType.DMA,
+        ],
         [vmem_spec()] * 4 + [any_spec()] * 2,
         any_spec,
     )(*grads, *boths, *late)
@@ -595,8 +651,12 @@
     lefts, parts = refs[:pairs], refs[pairs : pairs + count]
     others = refs[pairs + count : pairs + count + pieces * received]
     refs = refs[pairs + count + pieces * received :]
+    if received:
+        refs, arrived, other_sem, out_sem = refs[:-3], refs[-3], refs[-2], refs[-1]
     outs, turned, rows, sem = refs[: -pairs - 2], refs[-pairs - 2 : -2], refs[-2], refs[-1]
-    wait = fetch_rows(parts, rows, sem)
+    waits = [fetch_rows(parts, rows, sem)]
+    if received:
+        waits.append(fetch_rows(others, arrived, other_sem))
 
     @pl.loop(0, rows.shape[0] // step)
     def _(block):
@@ -604,7 +664,8 @@
         for left, flat in zip(lefts, turned):
             flat[:, own] = left[own, :].T
 
-    wait()
+    for wait in waits:
+        wait()
 
     @pl.loop(0, rows.shape[1] // step)
     def _(block):
@@ -615,13 +676,18 @@
                 start = (pairs * outer + place) * shard
                 own = product[outer * shard : (outer + 1) * shard]
                 if received:
-                    piece, row = start // others[0].shape[0], start % others[0].shape[0]
-                    outs[0][start : start + shard, columns] = (
-                        own + others[piece][row : row + shard, columns].astype(f32)
-                    ).astype(bf16)
+                    here = pl.ds(start, shard)
+                    arrived[here, columns] = (own + arrived[here, columns].astype(f32)).astype(bf16)
                 else:
                     piece, row = start // outs[0].shape[0], start % outs[0].shape[0]
                     outs[piece][row : row + shard, columns] = own.astype(bf16)
+        if received:
+            pltpu.make_async_copy(
+                arrived.at[:, columns], outs[0].at[:, columns], out_sem
+            ).start()
+
+    if received:
+        wait_all(arrived, out_sem)
 
 
 def hidden_sums(lefts, parts, shard, pieces, others=None, late=()):
@@ -629,12 +695,16 @@
     hidden = lefts[0].shape[1] * len(lefts)
     received = others is not None
     count = 1 if received else pieces
+    scratch = [pltpu.VMEM((left.shape[1], total), bf16) for left in lefts]
+    scratch += [pltpu.VMEM((total, width), bf16), pltpu.SemaphoreType.DMA]
+    if received:
+        scratch += [pltpu.VMEM((hidden, width), bf16)] + [pltpu.SemaphoreType.DMA] * 2
     outs = kernel_call(
         functools.partial(hidden_sums_body, len(parts), len(lefts), shard, pieces, received),
         (jax.ShapeDtypeStruct((hidden // count, width), bf16),) * count,
-        [pltpu.VMEM((left.shape[1], total), bf16) for left in lefts]
-        + [pltpu.VMEM((total, width), bf16), pltpu.SemaphoreType.DMA],
-        [vmem_spec()] * len(lefts) + [any_spec()] * len(parts) + [vmem_spec()] * (pieces * received),
+        scratch,
+        [vmem_spec()] * len(lefts) + [any_spec()] * (len(parts) + pieces * received),
+        any_spec if received else vmem_spec,
     )(*lefts, *parts, *(others or ()), *late)
     return outs[0] if received else outs
 
@@ -670,14 +740,18 @@
 
 
 def keep_sums_body(turned, right, first, second, *refs):
-    outs, arrived, held, in_sem, out_sem = refs[:6], refs[6], refs[7], refs[8], refs[9]
-    fetch_rows((first, second), arrived, in_sem)()
+    outs, arrived, held, in_sems, out_sem = refs[:6], refs[6], refs[7], refs[8], refs[9]
     size = turned.shape[0] // 16
+    for place, part in enumerate((first, first, second, second)):
+        source = part.at[pl.ds((place % 2) * 2 * size, 2 * size)]
+        target = arrived.at[pl.ds(place * 2 * size, 2 * size)]
+        pltpu.make_async_copy(source, target, in_sems.at[place]).start()
 
     @pl.loop(0, 4)
     def _(index):
         own = pl.ds(pl.multiple_of(index * 2 * size, 2 * size), 2 * size)
         product = jnp.dot(turned[own, :], right[...], preferred_element_type=f32)
+        wait_all(arrived.at[own], in_sems.at[index])
         held[own, :] = (product + arrived[own, :].astype(f32)).astype(bf16)
         send_blocks(column_route, outs, held, index, size, out_sem)
 
@@ -689,7 +763,8 @@
     return kernel_call(
         keep_sums_body,
         routed(rows // 8, columns),
-        [pltpu.VMEM((rows, columns), bf16)] * 2 + [pltpu.SemaphoreType.DMA] * 2,
+        [pltpu.VMEM((rows, columns), bf16)] * 2
+        + [pltpu.SemaphoreType.DMA((4,)), pltpu.SemaphoreType.DMA],
         [vmem_spec()] * 2 + [any_spec()] * 2,
         any_spec,
     )(turned, right, *others, *late)

time: 551 us -> 545 us (0.989)
  Pallas kernels: 246 us -> 234 us
    pallas_call x25, Pallas kernels: 246 us -> 234 us  [run(): pl.pallas_call(whole_body, out_shape=out_shapes, in_specs=in_specs + [any...]
  transfers between devices with their start and end apart: 86 -> 86, of which waited for: 49 -> 49; matrix products, arithmetic and copies ran while one was open for 4% -> 4% of each run, Pallas kernels for 45% -> 43%
where the time goes in v5:
time: 545 us; the launch traced here: 543 us
  Pallas kernels  234 us (43%)
  waiting for transfers between devices  195 us (36%)
  starting transfers between devices  53.8 us (10%)
  local copies, waits for them, and re-layouts  23.4 us (4%)
  other arithmetic  21.3 us (4%)
  between operations  15.6 us (3%)
    pallas_call x25, Pallas kernels, run(): pl.pallas_call(whole_body, out_shape=out_shapes, in_specs=in_specs + [any...  234 us
    ppermute x21, waiting for transfers between devices, y_swap(): return lax.ppermute(value, 'fsdp', [(i, i ^ 1) for i in range(self.fsdp)])  114 us
    ppermute x21, waiting for transfers between devices, x_swap(): return lax.ppermute(value, 'dp', [(i, i ^ 2) for i in range(self.dp)])  48.5 us
    ppermute x35, waiting for transfers between devices, core(): return lax.ppermute(value, 'dp', [(i, i ^ 1) for i in range(self.dp)])  26.4 us
    ppermute x21, starting transfers between devices, x_swap(): return lax.ppermute(value, 'dp', [(i, i ^ 2) for i in range(self.dp)])  23.4 us
    ppermute x21, starting transfers between devices, y_swap(): return lax.ppermute(value, 'fsdp', [(i, i ^ 1) for i in range(self.fsdp)])  22.3 us
    unnamed x138, local copies, waits for them, and re-layouts  13.9 us
  transfers between devices with their start and end apart: 86, of which 49 were waited for; matrix products, arithmetic and copies ran while one was open for 4% of the time, Pallas kernels for 43%

profile of v5, /device:TPU:0, one launch (start us, length us, event | category | flops | bytes accessed | tf_op | source)
XLA Modules:
  0.0 543.4 jit_solution(4762321982045866745)
XLA Ops:
  20.6 10.4 %collective-permute-done.1.refs_6_.refs_5_ = bf16[128,2048]{1,0:T(8,128)(2,1)S(1)} collective-permute-done((bf16[128,2048]{1,0:T(8,128)(2,1)S(1)}, bf16[128,2048]{1,0:T(8,128)(2,1)S(1)}, u32[]{:S(2)}, u32[]{:S(2)}) %collective-permute-start.1) | collective-permute-done | bytes 524320 | tf_op jit(solution)/shard_map/ppermute | solution.py:827
  34.5 10.6 %collective-permute-done.2.refs_7_.refs_6_ = bf16[128,2048]{1,0:T(8,128)(2,1)S(1)} collective-permute-done((bf16[128,2048]{1,0:T(8,128)(2,1)S(1)}, bf16[128,2048]{1,0:T(8,128)(2,1)S(1)}, u32[]{:S(2)}, u32[]{:S(2)}) %collective-permute-start.2) | collective-permute-done | bytes 524320 | tf_op jit(solution)/shard_map/ppermute | solution.py:827
  50.7 11.2 %collective-permute-done.4.refs_8_.refs_9_ = bf16[2,64,2432]{2,1,0:T(8,128)(2,1)} collective-permute-done((bf16[2,64,2432]{2,1,0:T(8,128)(2,1)S(1)}, bf16[2,64,2432]{2,1,0:T(8,128)(2,1)}, u32[]{:S(2)}, u32[]{:S(2)}) %collective-permute-start.4) | collective-permute-done | bytes 622624 | tf_op jit(solution)/shard_map/ppermute | solution.py:824
  67.4 12.8 %collective-permute-done.6.refs_6_.refs_7_ = bf16[2,64,2432]{2,1,0:T(8,128)(2,1)} collective-permute-done((bf16[2,64,2432]{2,1,0:T(8,128)(2,1)S(1)}, bf16[2,64,2432]{2,1,0:T(8,128)(2,1)}, u32[]{:S(2)}, u32[]{:S(2)}) %collective-permute-start.6) | collective-permute-done | bytes 622624 | tf_op jit(solution)/shard_map/ppermute | solution.py:827
  82.0 11.2 %collective-permute-done.8.refs_10_.refs_11_ = bf16[2,64,2432]{2,1,0:T(8,128)(2,1)} collective-permute-done((bf16[2,64,2432]{2,1,0:T(8,128)(2,1)}, bf16[2,64,2432]{2,1,0:T(8,128)(2,1)}, u32[]{:S(2)}, u32[]{:S(2)}) %collective-permute-start.8) | collective-permute-done | bytes 622624 | tf_op jit(solution)/shard_map/ppermute | solution.py:827
  100.4 13.1 %project.1 = (bf16[2048,256]{1,0:T(8,128)(2,1)}, bf16[256,2048]{1,0:T(8,128)(2,1)}, bf16[256,256]{1,0:T(8,128)(2,1)}, f32[8,2048]{1,0:T(8,128)}) custom-call(s32[2]{0:T(128)} %pad_add_fusion.refs_0_, bf16[256,2048]{1,0:T(8,128)(2,1)} %refs_1_.5, f32[256,128]{1,0:T(8,128)} %get-tuple-element.256.refs_2_.refs_7_, ...), custom_call_target="tpu_custom_call" | custom-call | flops 1 | bytes 1 | tf_op jit(solution)/shard_map/project/pallas_call | solution.py:68
  117.7 11.0 %attend.1 = (bf16[16,256,256]{2,1,0:T(8,128)(2,1)}, bf16[256,2048]{1,0:T(8,128)(2,1)}, bf16[2048,256]{1,0:T(8,128)(2,1)}) custom-call(s32[2]{0:T(128)} %pad_add_fusion.refs_0_, bf16[256,2048]{1,0:T(8,128)(2,1)} %get-tuple-element.135.refs_1_.refs_4_, bf16[256,256]{1,0:T(8,128)(2,1)} %get-tuple-element.119.refs_2_.refs_5_), custom_call_target="tpu_custom_call" | custom-call | flops 1 | bytes 1 | tf_op jit(solution)/shard_map/attend/pallas_call | solution.py:68
  130.0 9.5 %collective-permute-done.23.refs_11_.refs_16_ = bf16[2,64,2048]{2,1,0:T(8,128)(2,1)} collective-permute-done((bf16[2,64,2048]{2,1,0:T(8,128)(2,1)S(1)}, bf16[2,64,2048]{2,1,0:T(8,128)(2,1)}, u32[]{:S(2)}, u32[]{:S(2)}) %collective-permute-start.23) | collective-permute-done | bytes 524320 | tf_op jit(solution)/shard_map/ppermute | solution.py:824
  148.2 9.8 %mix.1 = (f32[256,2048]{1,0:T(8,128)}, bf16[128,2048]{1,0:T(8,128)(2,1)}, bf16[128,2048]{1,0:T(8,128)(2,1)}) custom-call(s32[2]{0:T(128)} %pad_add_fusion.refs_0_, bf16[256,2048]{1,0:T(8,128)(2,1)} %refs_1_.5, bf16[256,2048]{1,0:T(8,128)(2,1)} %get-tuple-element.137.refs_2_, f32[8,2048]{1,0:T(8,128)} %get-tuple-element.138.refs_3_.refs_2_, ...), custom_call_target="tpu_custom_call" | custom-call | flops 1 | bytes 1 | tf_op jit(solution)/shard_map/mix/pallas_call | solution.py:68
  160.2 12.0 %collective-permute-done.34.refs_2_.refs_4_ = bf16[128,2048]{1,0:T(8,128)(2,1)S(1)} collective-permute-done((bf16[128,2048]{1,0:T(8,128)(2,1)}, bf16[128,2048]{1,0:T(8,128)(2,1)S(1)}, u32[]{:S(2)}, u32[]{:S(2)}) %collective-permute-start.34) | collective-permute-done | bytes 524320 | tf_op jit(solution)/shard_map/ppermute | solution.py:824
  177.5 11.0 %collective-permute-done.37.refs_4_.refs_6_ = bf16[128,2048]{1,0:T(8,128)(2,1)S(1)} collective-permute-done((bf16[128,2048]{1,0:T(8,128)(2,1)}, bf16[128,2048]{1,0:T(8,128)(2,1)S(1)}, u32[]{:S(2)}, u32[]{:S(2)}) %collective-permute-start.37) | collective-permute-done | bytes 524320 | tf_op jit(solution)/shard_map/ppermute | solution.py:827
  200.6 12.7 %gate.2 = (bf16[1024,704]{1,0:T(8,128)(2,1)}, bf16[1024,704]{1,0:T(8,128)(2,1)}, bf16[1024,704]{1,0:T(8,128)(2,1)}) custom-call(bf16[128,2048]{1,0:T(8,128)(2,1)} %get-tuple-element.162.refs_0_.refs_2_, bf16[128,2048]{1,0:T(8,128)(2,1)} %get-tuple-element.163.refs_1_.refs_3_, bf16[128,2048]{1,0:T(8,128)(2,1)} %copy-done.10, bf16[128,2048]{1,0:T(8,128)(2,1)} %copy-done.13, ...), custom_call_target="tpu_custom_call" | custom-call | flops 1 | bytes 1 | tf_op jit(solution)/shard_map/gate/pallas_call | solution.py:68
  213.4 12.8 %gate.3 = (bf16[1024,704]{1,0:T(8,128)(2,1)}, bf16[1024,704]{1,0:T(8,128)(2,1)}, bf16[1024,704]{1,0:T(8,128)(2,1)}) custom-call(bf16[128,2048]{1,0:T(8,128)(2,1)} %get-tuple-element.162.refs_0_.refs_2_, bf16[128,2048]{1,0:T(8,128)(2,1)} %get-tuple-element.163.refs_1_.refs_3_, bf16[128,2048]{1,0:T(8,128)(2,1)} %copy-done.10, bf16[128,2048]{1,0:T(8,128)(2,1)} %copy-done.13, ...), custom_call_target="tpu_custom_call" | custom-call | flops 1 | bytes 1 | tf_op jit(solution)/shard_map/gate/pallas_call | solution.py:68
  227.2 9.5 %hidden_sums.4 = (bf16[176,2048]{1,0:T(8,128)(2,1)}, bf16[176,2048]{1,0:T(8,128)(2,1)}, bf16[176,2048]{1,0:T(8,128)(2,1)}, bf16[176,2048]{1,0:T(8,128)(2,1)}) custom-call(bf16[1024,704]{1,0:T(8,128)(2,1)} %get-tuple-element.168.refs_0_.refs_1_, bf16[128,2048]{1,0:T(8,128)(2,1)} %copy-done.1, bf16[128,2048]{1,0:T(8,128)(2,1)} %copy-done, ...), custom_call_target="tpu_custom_call" | custom-call | flops 1 | bytes 1 | tf_op jit(solution)/shard_map/hidden_sums/pallas_call | solution.py:68
  243.1 9.7 %hidden_sums.5 = bf16[704,2048]{1,0:T(8,128)(2,1)} custom-call(bf16[1024,704]{1,0:T(8,128)(2,1)} %get-tuple-element.167.refs_9_.refs_0_, bf16[128,2048]{1,0:T(8,128)(2,1)} %copy-done.1, bf16[128,2048]{1,0:T(8,128)(2,1)} %copy-done, bf16[128,2048]{1,0:T(8,128)(2,1)} %copy-done.5, bf16[128,2048]{1,0:T(8,128)(2,1)} %copy-done.9, bf16[128,2048]{1,0:T(8,128)(2,1)} %copy-done.8, ...), custom_call_target="tpu_custom_call" | custom-call | flops 1 | bytes 1 | tf_op jit(solution)/shard_map/hidden_sums/pallas_call | solution.py:68
  277.2 21.7 %rows_back.1 = (bf16[128,2048]{1,0:T(8,128)(2,1)}, bf16[128,2048]{1,0:T(8,128)(2,1)}, bf16[128,2048]{1,0:T(8,128)(2,1)}, bf16[128,2048]{1,0:T(8,128)(2,1)}, bf16...) custom-call(bf16[1024,704]{1,0:T(8,128)(2,1)} %get-tuple-element.176.refs_11_.refs_0_, ...), custom_call_target="tpu_custom_call" | custom-call | flops 1 | bytes 1 | tf_op jit(solution)/shard_map/rows_back/pallas_call | solution.py:68
  301.9 13.8 %hidden_sums.6 = (bf16[176,2048]{1,0:T(8,128)(2,1)}, bf16[176,2048]{1,0:T(8,128)(2,1)}, bf16[176,2048]{1,0:T(8,128)(2,1)}, bf16[176,2048]{1,0:T(8,128)(2,1)}, bf...) custom-call(bf16[1024,704]{1,0:T(8,128)(2,1)} %get-tuple-element.180, ...), custom_call_target="tpu_custom_call" | custom-call | flops 1 | bytes 1 | tf_op jit(solution)/shard_map/hidden_sums/pallas_call | solution.py:68
  330.1 14.4 %hidden_sums.7.refs_10_ = bf16[1408,2048]{1,0:T(8,128)(2,1)} custom-call(bf16[1024,704]{1,0:T(8,128)(2,1)} %get-tuple-element.176.refs_11_.refs_0_, bf16[1024,704]{1,0:T(8,128)(2,1)} %get-tuple-element.177.refs_1_, bf16[128,2048]{1,0:T(8,128)(2,1)} %get-tuple-element.162.refs_0_.refs_2_, bf16[128,2048]{1,0:T(8,128)(2,1)} %get-tuple-element.163.refs_1_.refs_3_, ...), custom_call_target="tpu_custom_call" | custom-call | flops 1 | bytes 1 | tf_op jit(solution)/shard_map/hidden_sums/pallas_call | solution.py:68
  347.7 11.3 %collective-permute-done.49.refs_9_ = bf16[128,2048]{1,0:T(8,128)(2,1)S(1)} collective-permute-done((bf16[128,2048]{1,0:T(8,128)(2,1)S(1)}, bf16[128,2048]{1,0:T(8,128)(2,1)S(1)}, u32[]{:S(2)}, u32[]{:S(2)}) %collective-permute-start.49) | collective-permute-done | bytes 524320 | tf_op jit(solution)/shard_map/ppermute | solution.py:827
  388.8 19.0 %attend_back.1 = (bf16[256,2304]{1,0:T(8,128)(2,1)}, f32[256,256]{1,0:T(8,128)}) custom-call(s32[2]{0:T(128)} %pad_add_fusion.refs_0_, f32[1]{0:T(128)} %bitcast.9.refs_0_.refs_1_, bf16[256,2048]{1,0:T(8,128)(2,1)} %get-tuple-element.200.refs_1_.refs_2_, bf16[256,256]{1,0:T(8,128)(2,1)} %refs_3_.3, bf16[256,2048]{1,0:T(8,128)(2,1)} %get-tuple-element.135.refs_1_.refs_4_, ...), custom_call_target="tpu_custom_call" | custom-call | flops 1 | bytes 1 | tf_op jit(solution)/shard_map/attend_back/pallas_call | solution.py:68
  441.5 12.8 %finish.1 = (f32[256,2048]{1,0:T(8,128)}, f32[8,2048]{1,0:T(8,128)}) custom-call(s32[2]{0:T(128)} %pad_add_fusion.refs_0_, bf16[256,2048]{1,0:T(8,128)(2,1)} %refs_1_.5, f32[8,2048]{1,0:T(8,128)} %get-tuple-element.138.refs_3_.refs_2_, bf16[256,2304]{1,0:T(8,128)(2,1)} %get-tuple-element.206.refs_4_.refs_1_.refs_3_, f32[256,2048]{1,0:T(8,128)} %get-tuple-element.219.refs_4_, ...), custom_call_target="tpu_custom_call" | custom-call | flops 1 | bytes 1 | tf_op jit(solution)/shard_map/finish/pallas_call | solution.py:68
  455.3 9.7 %collective-permute-done.64.refs_3_ = bf16[256,2304]{1,0:T(8,128)(2,1)S(1)} collective-permute-done((bf16[256,2304]{1,0:T(8,128)(2,1)}, bf16[256,2304]{1,0:T(8,128)(2,1)S(1)}, u32[]{:S(2)}, u32[]{:S(2)}) %collective-permute-start.64) | collective-permute-done | bytes 1179680 | tf_op jit(solution)/shard_map/ppermute | solution.py:827
  476.3 11.8 %down.1 = (bf16[128,2048]{1,0:T(8,128)(2,1)}, bf16[128,2048]{1,0:T(8,128)(2,1)}, bf16[128,2048]{1,0:T(8,128)(2,1)}, bf16[128,2048]{1,0:T(8,128)(2,1)}, bf16[256,...) custom-call(bf16[1024,704]{1,0:T(8,128)(2,1)} %get-tuple-element.167.refs_9_.refs_0_, ...), custom_call_target="tpu_custom_call" | custom-call | flops 1 | bytes 1 | tf_op jit(solution)/shard_map/down/pallas_call | solution.py:68
  493.6 19.3 %collective-permute-done.68.refs_3_ = bf16[256,2048]{1,0:T(8,128)(2,1)S(1)} collective-permute-done((bf16[256,2048]{1,0:T(8,128)(2,1)}, bf16[256,2048]{1,0:T(8,128)(2,1)S(1)}, u32[]{:S(2)}, u32[]{:S(2)}) %collective-permute-start.68) | collective-permute-done | bytes 1048608 | tf_op jit(solution)/shard_map/ppermute | solution.py:827
  (353 shorter events, 226.7 us)
Async XLA Ops:
  7.2 38.3 %all-gather.5.cloned.1.call-start = ((), (), s32[]{:S(2)}) async-start(), calls=%async_computation.4 | async-start | bytes 1556480 | tf_op jit(solution)/shard_map/all_gather | solution.py:846
  9.8 83.4 %all-gather.7.cloned.1.call-start = ((), (), s32[]{:S(2)}) async-start(), calls=%async_computation.5 | async-start | bytes 1310720 | tf_op jit(solution)/shard_map/all_gather | solution.py:846
  10.5 188.1 %all-gather.9.cloned.1.call-start = ((), (), s32[]{:S(2)}) async-start(), calls=%async_computation.6 | async-start | bytes 7208960 | tf_op jit(solution)/shard_map/all_gather | solution.py:846
  13.7 243.8 %all-gather.11.cloned.1.call-start = ((), (), s32[]{:S(2)}) async-start(), calls=%async_computation.7 | async-start | bytes 3604480 | tf_op jit(solution)/shard_map/all_gather | solution.py:846
  65.3 27.9 %collective-permute-start.8 = (bf16[2,64,2432]{2,1,0:T(8,128)(2,1)}, bf16[2,64,2432]{2,1,0:T(8,128)(2,1)}, u32[]{:S(2)}, u32[]{:S(2)}) collective-permute-start(bf16[2,64,2432]{2,1,0:T(8,128)(2,1)} %collective-permute-done.4.refs_8_.refs_9_), channel_id=1, source_target_pairs={{0,1},{1,0},{2,3},{3,2},{4,5},{5,4},{6,7},{7,6},{8,9},{9,8},{10,11... | collective-permute-start | bytes 1867784 | tf_op jit(solution)/shard_map/ppermute | solution.py:827
  65.9 27.3 %collective-permute-start.11 = (bf16[2,64,2432]{2,1,0:T(8,128)(2,1)}, bf16[2,64,2432]{2,1,0:T(8,128)(2,1)}, u32[]{:S(2)}, u32[]{:S(2)}) collective-permute-start(bf16[2,64,2432]{2,1,0:T(8,128)(2,1)} %bitcast.6.refs_5_.refs_6_), channel_id=1, source_target_pairs={{0,8},{8,0},{16,24},{24,16},{1,9},{9,1},{17,25},{25,17},{2,10},{10... | collective-permute-start | bytes 1867784 | tf_op jit(solution)/shard_map/ppermute | solution.py:813
  65.9 28.7 %collective-permute-start.7 = (bf16[2,64,2432]{2,1,0:T(8,128)(2,1)}, bf16[2,64,2432]{2,1,0:T(8,128)(2,1)}, u32[]{:S(2)}, u32[]{:S(2)}) collective-permute-start(bf16[2,64,2432]{2,1,0:T(8,128)(2,1)} %bitcast.6.refs_5_.refs_6_), channel_id=1, source_target_pairs={{0,16},{8,24},{16,0},{24,8},{1,17},{9,25},{17,1},{25,9},{2,18},{10... | collective-permute-start | bytes 1867784 | tf_op jit(solution)/shard_map/ppermute | solution.py:824
  116.6 22.9 %collective-permute-start.23 = (bf16[2,64,2048]{2,1,0:T(8,128)(2,1)S(1)}, bf16[2,64,2048]{2,1,0:T(8,128)(2,1)}, u32[]{:S(2)}, u32[]{:S(2)}) collective-permute-start(bf16[2,64,2048]{2,1,0:T(8,128)(2,1)S(1)} %collective-permute-done.19.refs_7_.refs_12_), channel_id=1, source_target_pairs={{0,16},{8,24},{16,0},{24,8},{1,17},{9,25},{17,1},{25,9},{2,18},{10... | collective-permute-start | bytes 1572872 | tf_op jit(solution)/shard_map/ppermute | solution.py:824
  174.7 23.1 %collective-permute-start.38 = (bf16[128,2048]{1,0:T(8,128)(2,1)S(1)}, bf16[128,2048]{1,0:T(8,128)(2,1)S(1)}, u32[]{:S(2)}, u32[]{:S(2)}) collective-permute-start(bf16[128,2048]{1,0:T(8,128)(2,1)S(1)} %collective-permute-done.34.refs_2_.refs_4_), channel_id=1, source_target_pairs={{0,1},{1,0},{2,3},{3,2},{4,5},{5,4},{6,7},{7,6},{8,9},{9,8},{10,11... | collective-permute-start | bytes 1572872 | tf_op jit(solution)/shard_map/ppermute | solution.py:827
  176.0 22.6 %collective-permute-start.39 = (bf16[128,2048]{1,0:T(8,128)(2,1)S(1)}, bf16[128,2048]{1,0:T(8,128)(2,1)}, u32[]{:S(2)}, u32[]{:S(2)}) collective-permute-start(bf16[128,2048]{1,0:T(8,128)(2,1)S(1)} %collective-permute-done.35.refs_5_.refs_7_), channel_id=1, source_target_pairs={{0,16},{8,24},{16,0},{24,8},{1,17},{9,25},{17,1},{25,9},{2,18},{10... | collective-permute-start | bytes 1572872 | tf_op jit(solution)/shard_map/ppermute | solution.py:824
  198.6 145.9 %reduce-scatter.5.cloned.1.call-start = ((), (), s32[]{:S(2)}) async-start(), calls=%async_computation.8 | async-start | bytes 3604480 | tf_op jit(solution)/shard_map/reduce_scatter | solution.py:849
  198.8 27.3 %collective-permute-start.33 = (bf16[128,2048]{1,0:T(8,128)(2,1)S(1)}, bf16[128,2048]{1,0:T(8,128)(2,1)S(1)}, u32[]{:S(2)}, u32[]{:S(2)}) collective-permute-start(bf16[128,2048]{1,0:T(8,128)(2,1)S(1)} %get-tuple-element.158.refs_1_.refs_0_), channel_id=1, source_target_pairs={{0,1},{1,0},{2,3},{3,2},{4,5},{5,4},{6,7},{7,6},{8,9},{9,8},{10,11... | collective-permute-start | bytes 1572872 | tf_op jit(solution)/shard_map/ppermute | solution.py:827
  200.0 26.3 %collective-permute-start.32 = (bf16[128,2048]{1,0:T(8,128)(2,1)S(1)}, bf16[128,2048]{1,0:T(8,128)(2,1)S(1)}, u32[]{:S(2)}, u32[]{:S(2)}) collective-permute-start(bf16[128,2048]{1,0:T(8,128)(2,1)S(1)} %get-tuple-element.159.refs_2_.refs_1_), channel_id=1, source_target_pairs={{0,16},{8,24},{16,0},{24,8},{1,17},{9,25},{17,1},{25,9},{2,18},{10... | collective-permute-start | bytes 1572872 | tf_op jit(solution)/shard_map/ppermute | solution.py:824
  257.5 207.8 %reduce-scatter.7.cloned.1.call-start = ((), (), s32[]{:S(2)}) async-start(), calls=%async_computation.9 | async-start | bytes 7208960 | tf_op jit(solution)/shard_map/reduce_scatter | solution.py:849
  298.9 26.0 %collective-permute-start.46 = (bf16[256,2048]{1,0:T(8,128)(2,1)}, bf16[256,2048]{1,0:T(8,128)(2,1)S(1)}, u32[]{:S(2)}, u32[]{:S(2)}) collective-permute-start(bf16[256,2048]{1,0:T(8,128)(2,1)} %get-tuple-element.183), channel_id=1, source_target_pairs={{0,1},{1,0},{2,3},{3,2},{4,5},{5,4},{6,7},{7,6},{8,9},{9,8},{10,11... | collective-permute-start | bytes 3145736 | tf_op jit(solution)/shard_map/ppermute | solution.py:827
  300.4 25.6 %collective-permute-start.47 = (bf16[256,2048]{1,0:T(8,128)(2,1)}, bf16[256,2048]{1,0:T(8,128)(2,1)S(1)}, u32[]{:S(2)}, u32[]{:S(2)}) collective-permute-start(bf16[256,2048]{1,0:T(8,128)(2,1)} %get-tuple-element.186), channel_id=1, source_target_pairs={{0,16},{8,24},{16,0},{24,8},{1,17},{9,25},{17,1},{25,9},{2,18},{10... | collective-permute-start | bytes 3145736 | tf_op jit(solution)/shard_map/ppermute | solution.py:824
  344.6 176.9 %reduce-scatter.11.cloned.1.call-start = ((), (), s32[]{:S(2)}) async-start(), calls=%async_computation.11 | async-start | bytes 1310720 | tf_op jit(solution)/shard_map/reduce_scatter | solution.py:849
  386.5 25.5 %collective-permute-start.60 = (bf16[256,2048]{1,0:T(8,128)(2,1)}, bf16[256,2048]{1,0:T(8,128)(2,1)S(1)}, u32[]{:S(2)}, u32[]{:S(2)}) collective-permute-start(bf16[256,2048]{1,0:T(8,128)(2,1)} %get-tuple-element.209), channel_id=1, source_target_pairs={{0,16},{8,24},{16,0},{24,8},{1,17},{9,25},{17,1},{25,9},{2,18},{10... | collective-permute-start | bytes 3145736 | tf_op jit(solution)/shard_map/ppermute | solution.py:824
  388.1 25.1 %collective-permute-start.61 = (bf16[256,2048]{1,0:T(8,128)(2,1)}, bf16[256,2048]{1,0:T(8,128)(2,1)S(1)}, u32[]{:S(2)}, u32[]{:S(2)}) collective-permute-start(bf16[256,2048]{1,0:T(8,128)(2,1)} %get-tuple-element.210), channel_id=1, source_target_pairs={{0,1},{1,0},{2,3},{3,2},{4,5},{5,4},{6,7},{7,6},{8,9},{9,8},{10,11... | collective-permute-start | bytes 3145736 | tf_op jit(solution)/shard_map/ppermute | solution.py:827
  436.6 28.3 %collective-permute-start.64 = (bf16[256,2304]{1,0:T(8,128)(2,1)}, bf16[256,2304]{1,0:T(8,128)(2,1)S(1)}, u32[]{:S(2)}, u32[]{:S(2)}) collective-permute-start(bf16[256,2304]{1,0:T(8,128)(2,1)} %get-tuple-element.215), channel_id=1, source_target_pairs={{0,1},{1,0},{2,3},{3,2},{4,5},{5,4},{6,7},{7,6},{8,9},{9,8},{10,11... | collective-permute-start | bytes 3538952 | tf_op jit(solution)/shard_map/ppermute | solution.py:827
  437.4 27.9 %collective-permute-start.65 = (bf16[256,2304]{1,0:T(8,128)(2,1)}, bf16[256,2304]{1,0:T(8,128)(2,1)S(1)}, u32[]{:S(2)}, u32[]{:S(2)}) collective-permute-start(bf16[256,2304]{1,0:T(8,128)(2,1)} %get-tuple-element.218), channel_id=1, source_target_pairs={{0,16},{8,24},{16,0},{24,8},{1,17},{9,25},{17,1},{25,9},{2,18},{10... | collective-permute-start | bytes 3538952 | tf_op jit(solution)/shard_map/ppermute | solution.py:824
  471.3 60.5 %reduce-scatter.9.cloned.1.call-start = ((), (), s32[]{:S(2)}) async-start(), calls=%async_computation.10 | async-start | bytes 1556480 | tf_op jit(solution)/shard_map/reduce_scatter | solution.py:849
  489.8 23.1 %collective-permute-start.68 = (bf16[256,2048]{1,0:T(8,128)(2,1)}, bf16[256,2048]{1,0:T(8,128)(2,1)S(1)}, u32[]{:S(2)}, u32[]{:S(2)}) collective-permute-start(bf16[256,2048]{1,0:T(8,128)(2,1)} %get-tuple-element.231), channel_id=1, source_target_pairs={{0,1},{1,0},{2,3},{3,2},{4,5},{5,4},{6,7},{7,6},{8,9},{9,8},{10,11... | collective-permute-start | bytes 3145736 | tf_op jit(solution)/shard_map/ppermute | solution.py:827
  490.7 22.9 %collective-permute-start.69 = (bf16[256,2048]{1,0:T(8,128)(2,1)}, bf16[256,2048]{1,0:T(8,128)(2,1)S(1)}, u32[]{:S(2)}, u32[]{:S(2)}) collective-permute-start(bf16[256,2048]{1,0:T(8,128)(2,1)} %get-tuple-element.234), channel_id=1, source_target_pairs={{0,16},{8,24},{16,0},{24,8},{1,17},{9,25},{17,1},{25,9},{2,18},{10... | collective-permute-start | bytes 3145736 | tf_op jit(solution)/shard_map/ppermute | solution.py:824
  (130 other events, 1710.1 us)
Sparse Core Ops, SparseCore 0:
  10.2 34.2 all-gather.4
  46.0 26.9 all-gather.6
  75.2 106.1 all-gather.8
  198.7 58.7 all-gather.10
  260.2 54.8 reduce-scatter.4
  344.7 100.0 reduce-scatter.6
  471.5 25.5 reduce-scatter.10
  499.5 28.8 reduce-scatter.8

commit v6 on v5

--- a/solution.py
+++ b/solution.py
@@ -314,43 +314,70 @@
     )(spot, tokens, attended, gains, *pieces.arrays, *late)
 
 
-def norm_back_body(factor, mid, gains, grad_out, *refs):
-    sums = refs[:6]
-    d_mid_out, d_mid_low, gain_out = refs[6:]
-    half = mid.shape[0] // 2
-    size = half // 4
+def norm_back_body(factor, gains, mid, grad_out, *refs):
+    sums, outs = refs[:6], refs[6:9]
+    mid_in, grad_in, own, middle, last, d_mid_held, low_held, gain_held = refs[9:17]
+    in_sems, out_sem = refs[17], refs[18]
+    length = mid.shape[0]
+    half = length // 2
+    blocks = in_sems.shape[0]
+    size = length // blocks
+
+    @pl.loop(0, blocks)
+    def _(block):
+        rows = pl.ds(pl.multiple_of(block * size, size), size)
+        for source, target in ((mid, mid_in), (grad_out, grad_in)):
+            pltpu.make_async_copy(source.at[rows], target.at[rows], in_sems.at[block]).start()
+        for part in range(2):
+
+            @pl.when(block // (blocks // 2) == part)
+            def _():
+                start = pl.multiple_of((block - part * (blocks // 2)) * size, size)
+                for source, target, skip in zip(sums[3 * part :], (own, middle, last), (0, half, 0)):
+                    pltpu.make_async_copy(
+                        source.at[pl.ds(skip + start, size)], target.at[rows], in_sems.at[block]
+                    ).start()
+
     gain = gains[1:2, :]
-    gain_out[...] = jnp.zeros_like(gain_out)
-    for part in range(2):
-        own, middle, last = sums[3 * part : 3 * part + 3]
-
-        @pl.loop(0, 4)
-        def _(block):
-            start = pl.multiple_of(block * size, size)
-            here, there = pl.ds(start, size), pl.ds(half + start, size)
-            rows = pl.ds(part * half + start, size)
-            d_h = own[here, :].astype(f32) + middle[there, :].astype(f32) + last[here, :].astype(f32)
-            x_mid = mid[rows, :]
-            inverse = lax.rsqrt(jnp.mean(x_mid * x_mid, axis=-1, keepdims=True) + epsilon)
-            normed = x_mid * inverse
-            product = d_h * normed
-            gain_out[0:1, :] += jnp.sum(product, axis=0, keepdims=True)
-            mean = jnp.mean(product * gain, axis=-1, keepdims=True)
-            grad_top = grad_out[rows, :].astype(f32) * factor[0]
-            d_mid = grad_top + inverse * (d_h * gain - normed * mean)
-            d_mid_out[rows, :] = d_mid
-            d_mid_low[rows, :] = d_mid.astype(bf16)
+    gain_held[...] = jnp.zeros_like(gain_held)
+
+    @pl.loop(0, blocks)
+    def _(block):
+        rows = pl.ds(pl.multiple_of(block * size, size), size)
+        for held in (mid_in, grad_in, own, middle, last):
+            wait_all(held.at[rows], in_sems.at[block])
+        d_h = own[rows, :].astype(f32) + middle[rows, :].astype(f32) + last[rows, :].astype(f32)
+        x_mid = mid_in[rows, :]
+        inverse = lax.rsqrt(jnp.mean(x_mid * x_mid, axis=-1, keepdims=True) + epsilon)
+        normed = x_mid * inverse
+        product = d_h * normed
+        gain_held[0:1, :] += jnp.sum(product, axis=0, keepdims=True)
+        mean = jnp.mean(product * gain, axis=-1, keepdims=True)
+        grad_top = grad_in[rows, :].astype(f32) * factor[0]
+        d_mid = grad_top + inverse * (d_h * gain - normed * mean)
+        d_mid_held[rows, :] = d_mid
+        low_held[rows, :] = d_mid.astype(bf16)
+        for held, target in zip((d_mid_held, low_held), outs):
+            pltpu.make_async_copy(held.at[rows], target.at[rows], out_sem).start()
+
+    pltpu.make_async_copy(gain_held, outs[2], out_sem).start()
+    for held in (d_mid_held, low_held, gain_held):
+        wait_all(held, out_sem)
 
 
 def norm_back(factor, mid, gains, grad_out, sums, late=()):
     length, width = mid.shape
     shape = jax.ShapeDtypeStruct
+    whole = pltpu.VMEM((length, width), bf16)
+    wide = pltpu.VMEM((length, width), f32)
     return kernel_call(
         norm_back_body,
         (shape((length, width), f32), shape((length, width), bf16), shape((8, width), f32)),
-        [],
-        [smem_spec()] + [vmem_spec()] * 9,
-    )(factor, mid, gains, grad_out, *sums, *late)
+        [wide, whole, whole, whole, whole, wide, whole, pltpu.VMEM((8, width), f32)]
+        + [pltpu.SemaphoreType.DMA((8,)), pltpu.SemaphoreType.DMA],
+        [smem_spec(), vmem_spec()] + [any_spec()] * 8,
+        any_spec,
+    )(factor, gains, mid, grad_out, *sums, *late)
 
 
 def attend_back_body(pieces, head_dim, *refs):
@@ -786,17 +813,62 @@
     return kernel_call(alternate_body, out, [], [vmem_spec()])(both)
 
 
-def pass_body(keep_x, keep_y, from_x, from_y, for_x, for_y):
-    size = keep_x.shape[0]
-    for_x[...] = (keep_x[...].astype(f32) + from_y[:size, :].astype(f32)).astype(bf16)
-    for_y[...] = (keep_y[...].astype(f32) + from_x[:size, :].astype(f32)).astype(bf16)
+def widen_body(rows, first, second, gain_one, gain_two):
+    columns, more = first.shape[1], second.shape[1]
+    first[...] = rows[:, :columns].astype(f32)
+    second[...] = rows[:, columns : columns + more].astype(f32)
+    turned = rows[:, columns + more :].astype(f32).T
+    gain_one[...] = turned[0:1, :]
+    gain_two[...] = turned[1:2, :]
+
+
+def widen(rows, first, second):
+    shape = jax.ShapeDtypeStruct
+    size = rows.shape[0]
+    outs = (
+        shape((size, first), f32),
+        shape((size, second), f32),
+        shape((1, size), f32),
+        shape((1, size), f32),
+    )
+    *wide, gain_one, gain_two = kernel_call(widen_body, outs, [], [vmem_spec()])(rows)
+    return *wide, gain_one.reshape(size), gain_two.reshape(size)
+
+
+def pass_body(keep_x, keep_y, from_x, from_y, for_x, for_y, *refs):
+    held, in_sems, out_sem = refs[:4], refs[4], refs[5]
+    blocks = in_sems.shape[0]
+    size = keep_x.shape[0] // blocks
+
+    @pl.loop(0, blocks)
+    def _(block):
+        rows = pl.ds(pl.multiple_of(block * size, size), size)
+        for source, target in zip((keep_x, from_y, keep_y, from_x), held):
+            pltpu.make_async_copy(source.at[rows], target.at[rows], in_sems.at[block]).start()
+
+    @pl.loop(0, blocks)
+    def _(block):
+        rows = pl.ds(pl.multiple_of(block * size, size), size)
+        for target in held:
+            wait_all(target.at[rows], in_sems.at[block])
+        for keep, come, out in ((held[0], held[1], for_x), (held[2], held[3], for_y)):
+            keep[rows, :] = (keep[rows, :].astype(f32) + come[rows, :].astype(f32)).astype(bf16)
+            pltpu.make_async_copy(keep.at[rows], out.at[rows], out_sem).start()
+
+    wait_all(held[0], out_sem)
+    wait_all(held[2], out_sem)
 
 
 def pass_on(keep_x, keep_y, from_x, from_y, late=()):
     out = jax.ShapeDtypeStruct(keep_x.shape, bf16)
-    return kernel_call(pass_body, (out, out), [], [vmem_spec()] * 4)(
-        keep_x, keep_y, from_x, from_y, *late
-    )
+    return kernel_call(
+        pass_body,
+        (out, out),
+        [pltpu.VMEM(keep_x.shape, bf16)] * 4
+        + [pltpu.SemaphoreType.DMA((4,)), pltpu.SemaphoreType.DMA],
+        [any_spec()] * 4,
+        any_spec,
+    )(keep_x, keep_y, from_x, from_y, *late)
 
 
 class Grid:
@@ -1024,10 +1096,7 @@
         d_tokens,
         kv_out,
         d_kv,
-        d_w_in[:, :q_width].astype(f32),
-        d_w_in[:, q_width : q_width + kv_width].astype(f32),
-        d_w_in[:, q_width + kv_width].astype(f32),
-        d_w_in[:, q_width + kv_width + 1].astype(f32),
+        *widen(d_w_in, q_width, kv_width),
         d_w_o,
         d_w_gu,
         d_w_down,

time: 545 us -> 537 us (0.985)
    pallas_call x25 -> x26, Pallas kernels: 234 us -> 232 us  [run(): pl.pallas_call(whole_body, out_shape=out_shapes, in_specs=in_specs + [any...]
where the time goes in v6:
time: 537 us; the launch traced here: 536 us
  Pallas kernels  232 us (43%)
  waiting for transfers between devices  195 us (36%)
  starting transfers between devices  54.1 us (10%)
  local copies, waits for them, and re-layouts  23.1 us (4%)
  other arithmetic  16.6 us (3%)
  between operations  15.6 us (3%)
    pallas_call x26, Pallas kernels, run(): pl.pallas_call(whole_body, out_shape=out_shapes, in_specs=in_specs + [any...  232 us
    ppermute x21, waiting for transfers between devices, y_swap(): return lax.ppermute(value, 'fsdp', [(i, i ^ 1) for i in range(self.fsdp)])  115 us
    ppermute x21, waiting for transfers between devices, x_swap(): return lax.ppermute(value, 'dp', [(i, i ^ 2) for i in range(self.dp)])  48.1 us
    ppermute x35, waiting for transfers between devices, core(): return lax.ppermute(value, 'dp', [(i, i ^ 1) for i in range(self.dp)])  26.3 us
    ppermute x21, starting transfers between devices, x_swap(): return lax.ppermute(value, 'dp', [(i, i ^ 2) for i in range(self.dp)])  23.9 us
    ppermute x21, starting transfers between devices, y_swap(): return lax.ppermute(value, 'fsdp', [(i, i ^ 1) for i in range(self.fsdp)])  22.1 us
    unnamed x138, local copies, waits for them, and re-layouts  13.6 us
  transfers between devices with their start and end apart: 86, of which 49 were waited for; matrix products, arithmetic and copies ran while one was open for 4% of the time, Pallas kernels for 43%

profile of v6, /device:TPU:0, one launch (start us, length us, event | category | flops | bytes accessed | tf_op | source)
XLA Modules:
  0.0 536.2 jit_solution(12353843197837978923)
XLA Ops:
  20.5 10.4 %collective-permute-done.1.refs_6_.refs_5_ = bf16[128,2048]{1,0:T(8,128)(2,1)S(1)} collective-permute-done((bf16[128,2048]{1,0:T(8,128)(2,1)S(1)}, bf16[128,2048]{1,0:T(8,128)(2,1)S(1)}, u32[]{:S(2)}, u32[]{:S(2)}) %collective-permute-start.1) | collective-permute-done | bytes 524320 | tf_op jit(solution)/shard_map/ppermute | solution.py:899
  34.4 10.7 %collective-permute-done.2.refs_7_.refs_6_ = bf16[128,2048]{1,0:T(8,128)(2,1)S(1)} collective-permute-done((bf16[128,2048]{1,0:T(8,128)(2,1)S(1)}, bf16[128,2048]{1,0:T(8,128)(2,1)S(1)}, u32[]{:S(2)}, u32[]{:S(2)}) %collective-permute-start.2) | collective-permute-done | bytes 524320 | tf_op jit(solution)/shard_map/ppermute | solution.py:899
  50.6 11.3 %collective-permute-done.4.refs_8_.refs_9_ = bf16[2,64,2432]{2,1,0:T(8,128)(2,1)} collective-permute-done((bf16[2,64,2432]{2,1,0:T(8,128)(2,1)S(1)}, bf16[2,64,2432]{2,1,0:T(8,128)(2,1)}, u32[]{:S(2)}, u32[]{:S(2)}) %collective-permute-start.4) | collective-permute-done | bytes 622624 | tf_op jit(solution)/shard_map/ppermute | solution.py:896
  67.5 12.8 %collective-permute-done.6.refs_6_.refs_7_ = bf16[2,64,2432]{2,1,0:T(8,128)(2,1)} collective-permute-done((bf16[2,64,2432]{2,1,0:T(8,128)(2,1)S(1)}, bf16[2,64,2432]{2,1,0:T(8,128)(2,1)}, u32[]{:S(2)}, u32[]{:S(2)}) %collective-permute-start.6) | collective-permute-done | bytes 622624 | tf_op jit(solution)/shard_map/ppermute | solution.py:899
  82.0 11.2 %collective-permute-done.8.refs_10_.refs_11_ = bf16[2,64,2432]{2,1,0:T(8,128)(2,1)} collective-permute-done((bf16[2,64,2432]{2,1,0:T(8,128)(2,1)}, bf16[2,64,2432]{2,1,0:T(8,128)(2,1)}, u32[]{:S(2)}, u32[]{:S(2)}) %collective-permute-start.8) | collective-permute-done | bytes 622624 | tf_op jit(solution)/shard_map/ppermute | solution.py:899
  100.5 13.1 %project.1 = (bf16[2048,256]{1,0:T(8,128)(2,1)}, bf16[256,2048]{1,0:T(8,128)(2,1)}, bf16[256,256]{1,0:T(8,128)(2,1)}, f32[8,2048]{1,0:T(8,128)}) custom-call(s32[2]{0:T(128)} %pad_add_fusion.refs_0_, bf16[256,2048]{1,0:T(8,128)(2,1)} %refs_1_.5, f32[256,128]{1,0:T(8,128)} %get-tuple-element.262.refs_2_.refs_7_, ...), custom_call_target="tpu_custom_call" | custom-call | flops 1 | bytes 1 | tf_op jit(solution)/shard_map/project/pallas_call | solution.py:68
  117.8 11.0 %attend.1 = (bf16[16,256,256]{2,1,0:T(8,128)(2,1)}, bf16[256,2048]{1,0:T(8,128)(2,1)}, bf16[2048,256]{1,0:T(8,128)(2,1)}) custom-call(s32[2]{0:T(128)} %pad_add_fusion.refs_0_, bf16[256,2048]{1,0:T(8,128)(2,1)} %get-tuple-element.139.refs_1_.refs_4_, bf16[256,256]{1,0:T(8,128)(2,1)} %get-tuple-element.123.refs_2_.refs_5_), custom_call_target="tpu_custom_call" | custom-call | flops 1 | bytes 1 | tf_op jit(solution)/shard_map/attend/pallas_call | solution.py:68
  130.1 9.5 %collective-permute-done.23.refs_11_.refs_16_ = bf16[2,64,2048]{2,1,0:T(8,128)(2,1)} collective-permute-done((bf16[2,64,2048]{2,1,0:T(8,128)(2,1)S(1)}, bf16[2,64,2048]{2,1,0:T(8,128)(2,1)}, u32[]{:S(2)}, u32[]{:S(2)}) %collective-permute-start.23) | collective-permute-done | bytes 524320 | tf_op jit(solution)/shard_map/ppermute | solution.py:896
  148.3 9.7 %mix.1 = (f32[256,2048]{1,0:T(8,128)}, bf16[128,2048]{1,0:T(8,128)(2,1)}, bf16[128,2048]{1,0:T(8,128)(2,1)}) custom-call(s32[2]{0:T(128)} %pad_add_fusion.refs_0_, bf16[256,2048]{1,0:T(8,128)(2,1)} %refs_1_.5, bf16[256,2048]{1,0:T(8,128)(2,1)} %get-tuple-element.141.refs_2_, f32[8,2048]{1,0:T(8,128)} %get-tuple-element.142.refs_3_.refs_1_.refs_2_, ...), custom_call_target="tpu_custom_call" | custom-call | flops 1 | bytes 1 | tf_op jit(solution)/shard_map/mix/pallas_call | solution.py:68
  160.3 12.0 %collective-permute-done.34.refs_2_.refs_4_ = bf16[128,2048]{1,0:T(8,128)(2,1)S(1)} collective-permute-done((bf16[128,2048]{1,0:T(8,128)(2,1)}, bf16[128,2048]{1,0:T(8,128)(2,1)S(1)}, u32[]{:S(2)}, u32[]{:S(2)}) %collective-permute-start.34) | collective-permute-done | bytes 524320 | tf_op jit(solution)/shard_map/ppermute | solution.py:896
  177.5 11.0 %collective-permute-done.37.refs_4_.refs_6_ = bf16[128,2048]{1,0:T(8,128)(2,1)S(1)} collective-permute-done((bf16[128,2048]{1,0:T(8,128)(2,1)}, bf16[128,2048]{1,0:T(8,128)(2,1)S(1)}, u32[]{:S(2)}, u32[]{:S(2)}) %collective-permute-start.37) | collective-permute-done | bytes 524320 | tf_op jit(solution)/shard_map/ppermute | solution.py:899
  200.7 12.7 %gate.2 = (bf16[1024,704]{1,0:T(8,128)(2,1)}, bf16[1024,704]{1,0:T(8,128)(2,1)}, bf16[1024,704]{1,0:T(8,128)(2,1)}) custom-call(bf16[128,2048]{1,0:T(8,128)(2,1)} %get-tuple-element.166.refs_0_.refs_2_, bf16[128,2048]{1,0:T(8,128)(2,1)} %get-tuple-element.167.refs_1_.refs_3_, bf16[128,2048]{1,0:T(8,128)(2,1)} %copy-done.10, bf16[128,2048]{1,0:T(8,128)(2,1)} %copy-done.13, ...), custom_call_target="tpu_custom_call" | custom-call | flops 1 | bytes 1 | tf_op jit(solution)/shard_map/gate/pallas_call | solution.py:68
  213.4 12.8 %gate.3 = (bf16[1024,704]{1,0:T(8,128)(2,1)}, bf16[1024,704]{1,0:T(8,128)(2,1)}, bf16[1024,704]{1,0:T(8,128)(2,1)}) custom-call(bf16[128,2048]{1,0:T(8,128)(2,1)} %get-tuple-element.166.refs_0_.refs_2_, bf16[128,2048]{1,0:T(8,128)(2,1)} %get-tuple-element.167.refs_1_.refs_3_, bf16[128,2048]{1,0:T(8,128)(2,1)} %copy-done.10, bf16[128,2048]{1,0:T(8,128)(2,1)} %copy-done.13, ...), custom_call_target="tpu_custom_call" | custom-call | flops 1 | bytes 1 | tf_op jit(solution)/shard_map/gate/pallas_call | solution.py:68
  227.3 9.4 %hidden_sums.4 = (bf16[176,2048]{1,0:T(8,128)(2,1)}, bf16[176,2048]{1,0:T(8,128)(2,1)}, bf16[176,2048]{1,0:T(8,128)(2,1)}, bf16[176,2048]{1,0:T(8,128)(2,1)}) custom-call(bf16[1024,704]{1,0:T(8,128)(2,1)} %get-tuple-element.172.refs_0_.refs_1_, bf16[128,2048]{1,0:T(8,128)(2,1)} %copy-done.1, bf16[128,2048]{1,0:T(8,128)(2,1)} %copy-done, ...), custom_call_target="tpu_custom_call" | custom-call | flops 1 | bytes 1 | tf_op jit(solution)/shard_map/hidden_sums/pallas_call | solution.py:68
  243.1 9.7 %hidden_sums.5 = bf16[704,2048]{1,0:T(8,128)(2,1)} custom-call(bf16[1024,704]{1,0:T(8,128)(2,1)} %get-tuple-element.171.refs_9_.refs_0_, bf16[128,2048]{1,0:T(8,128)(2,1)} %copy-done.1, bf16[128,2048]{1,0:T(8,128)(2,1)} %copy-done, bf16[128,2048]{1,0:T(8,128)(2,1)} %copy-done.5, bf16[128,2048]{1,0:T(8,128)(2,1)} %copy-done.9, bf16[128,2048]{1,0:T(8,128)(2,1)} %copy-done.8, ...), custom_call_target="tpu_custom_call" | custom-call | flops 1 | bytes 1 | tf_op jit(solution)/shard_map/hidden_sums/pallas_call | solution.py:68
  277.2 21.7 %rows_back.1 = (bf16[128,2048]{1,0:T(8,128)(2,1)}, bf16[128,2048]{1,0:T(8,128)(2,1)}, bf16[128,2048]{1,0:T(8,128)(2,1)}, bf16[128,2048]{1,0:T(8,128)(2,1)}, bf16...) custom-call(bf16[1024,704]{1,0:T(8,128)(2,1)} %get-tuple-element.180.refs_11_.refs_0_, ...), custom_call_target="tpu_custom_call" | custom-call | flops 1 | bytes 1 | tf_op jit(solution)/shard_map/rows_back/pallas_call | solution.py:68
  301.9 13.8 %hidden_sums.6 = (bf16[176,2048]{1,0:T(8,128)(2,1)}, bf16[176,2048]{1,0:T(8,128)(2,1)}, bf16[176,2048]{1,0:T(8,128)(2,1)}, bf16[176,2048]{1,0:T(8,128)(2,1)}, bf...) custom-call(bf16[1024,704]{1,0:T(8,128)(2,1)} %get-tuple-element.184, ...), custom_call_target="tpu_custom_call" | custom-call | flops 1 | bytes 1 | tf_op jit(solution)/shard_map/hidden_sums/pallas_call | solution.py:68
  329.4 14.5 %hidden_sums.7.refs_10_ = bf16[1408,2048]{1,0:T(8,128)(2,1)} custom-call(bf16[1024,704]{1,0:T(8,128)(2,1)} %get-tuple-element.180.refs_11_.refs_0_, bf16[1024,704]{1,0:T(8,128)(2,1)} %get-tuple-element.181.refs_1_, bf16[128,2048]{1,0:T(8,128)(2,1)} %get-tuple-element.166.refs_0_.refs_2_, bf16[128,2048]{1,0:T(8,128)(2,1)} %get-tuple-element.167.refs_1_.refs_3_, ...), custom_call_target="tpu_custom_call" | custom-call | flops 1 | bytes 1 | tf_op jit(solution)/shard_map/hidden_sums/pallas_call | solution.py:68
  347.0 11.3 %collective-permute-done.49.refs_9_ = bf16[128,2048]{1,0:T(8,128)(2,1)S(1)} collective-permute-done((bf16[128,2048]{1,0:T(8,128)(2,1)S(1)}, bf16[128,2048]{1,0:T(8,128)(2,1)S(1)}, u32[]{:S(2)}, u32[]{:S(2)}) %collective-permute-start.49) | collective-permute-done | bytes 524320 | tf_op jit(solution)/shard_map/ppermute | solution.py:899
  386.3 19.0 %attend_back.1 = (bf16[256,2304]{1,0:T(8,128)(2,1)}, f32[256,256]{1,0:T(8,128)}) custom-call(s32[2]{0:T(128)} %pad_add_fusion.refs_0_, f32[1]{0:T(128)} %bitcast.9.refs_0_.refs_1_, bf16[256,2048]{1,0:T(8,128)(2,1)} %get-tuple-element.204.refs_1_.refs_2_, bf16[256,256]{1,0:T(8,128)(2,1)} %refs_3_.3, bf16[256,2048]{1,0:T(8,128)(2,1)} %get-tuple-element.139.refs_1_.refs_4_, ...), custom_call_target="tpu_custom_call" | custom-call | flops 1 | bytes 1 | tf_op jit(solution)/shard_map/attend_back/pallas_call | solution.py:68
  438.5 12.8 %finish.1 = (f32[256,2048]{1,0:T(8,128)}, f32[8,2048]{1,0:T(8,128)}) custom-call(s32[2]{0:T(128)} %pad_add_fusion.refs_0_, bf16[256,2048]{1,0:T(8,128)(2,1)} %refs_1_.5, f32[8,2048]{1,0:T(8,128)} %get-tuple-element.142.refs_3_.refs_1_.refs_2_, bf16[256,2304]{1,0:T(8,128)(2,1)} %get-tuple-element.210.refs_4_.refs_1_.refs_3_, ...), custom_call_target="tpu_custom_call" | custom-call | flops 1 | bytes 1 | tf_op jit(solution)/shard_map/finish/pallas_call | solution.py:68
  452.3 9.7 %collective-permute-done.64.refs_3_ = bf16[256,2304]{1,0:T(8,128)(2,1)S(1)} collective-permute-done((bf16[256,2304]{1,0:T(8,128)(2,1)}, bf16[256,2304]{1,0:T(8,128)(2,1)S(1)}, u32[]{:S(2)}, u32[]{:S(2)}) %collective-permute-start.64) | collective-permute-done | bytes 1179680 | tf_op jit(solution)/shard_map/ppermute | solution.py:899
  472.6 11.8 %down.1 = (bf16[128,2048]{1,0:T(8,128)(2,1)}, bf16[128,2048]{1,0:T(8,128)(2,1)}, bf16[128,2048]{1,0:T(8,128)(2,1)}, bf16[128,2048]{1,0:T(8,128)(2,1)}, bf16[256,...) custom-call(bf16[1024,704]{1,0:T(8,128)(2,1)} %get-tuple-element.171.refs_9_.refs_0_, ...), custom_call_target="tpu_custom_call" | custom-call | flops 1 | bytes 1 | tf_op jit(solution)/shard_map/down/pallas_call | solution.py:68
  489.9 19.3 %collective-permute-done.68.refs_3_ = bf16[256,2048]{1,0:T(8,128)(2,1)S(1)} collective-permute-done((bf16[256,2048]{1,0:T(8,128)(2,1)}, bf16[256,2048]{1,0:T(8,128)(2,1)S(1)}, u32[]{:S(2)}, u32[]{:S(2)}) %collective-permute-start.68) | collective-permute-done | bytes 1048608 | tf_op jit(solution)/shard_map/ppermute | solution.py:899
  (351 shorter events, 219.3 us)
Async XLA Ops:
  7.2 38.2 %all-gather.5.cloned.1.call-start = ((), (), s32[]{:S(2)}) async-start(), calls=%async_computation.4 | async-start | bytes 1556480 | tf_op jit(solution)/shard_map/all_gather | solution.py:918
  9.8 83.5 %all-gather.7.cloned.1.call-start = ((), (), s32[]{:S(2)}) async-start(), calls=%async_computation.5 | async-start | bytes 1310720 | tf_op jit(solution)/shard_map/all_gather | solution.py:918
  10.5 188.1 %all-gather.9.cloned.1.call-start = ((), (), s32[]{:S(2)}) async-start(), calls=%async_computation.6 | async-start | bytes 7208960 | tf_op jit(solution)/shard_map/all_gather | solution.py:918
  13.7 243.8 %all-gather.11.cloned.1.call-start = ((), (), s32[]{:S(2)}) async-start(), calls=%async_computation.7 | async-start | bytes 3604480 | tf_op jit(solution)/shard_map/all_gather | solution.py:918
  65.4 27.9 %collective-permute-start.8 = (bf16[2,64,2432]{2,1,0:T(8,128)(2,1)}, bf16[2,64,2432]{2,1,0:T(8,128)(2,1)}, u32[]{:S(2)}, u32[]{:S(2)}) collective-permute-start(bf16[2,64,2432]{2,1,0:T(8,128)(2,1)} %collective-permute-done.4.refs_8_.refs_9_), channel_id=1, source_target_pairs={{0,1},{1,0},{2,3},{3,2},{4,5},{5,4},{6,7},{7,6},{8,9},{9,8},{10,11... | collective-permute-start | bytes 1867784 | tf_op jit(solution)/shard_map/ppermute | solution.py:899
  65.9 27.3 %collective-permute-start.11 = (bf16[2,64,2432]{2,1,0:T(8,128)(2,1)}, bf16[2,64,2432]{2,1,0:T(8,128)(2,1)}, u32[]{:S(2)}, u32[]{:S(2)}) collective-permute-start(bf16[2,64,2432]{2,1,0:T(8,128)(2,1)} %bitcast.6.refs_5_.refs_6_), channel_id=1, source_target_pairs={{0,8},{8,0},{16,24},{24,16},{1,9},{9,1},{17,25},{25,17},{2,10},{10... | collective-permute-start | bytes 1867784 | tf_op jit(solution)/shard_map/ppermute | solution.py:885
  65.9 28.7 %collective-permute-start.7 = (bf16[2,64,2432]{2,1,0:T(8,128)(2,1)}, bf16[2,64,2432]{2,1,0:T(8,128)(2,1)}, u32[]{:S(2)}, u32[]{:S(2)}) collective-permute-start(bf16[2,64,2432]{2,1,0:T(8,128)(2,1)} %bitcast.6.refs_5_.refs_6_), channel_id=1, source_target_pairs={{0,16},{8,24},{16,0},{24,8},{1,17},{9,25},{17,1},{25,9},{2,18},{10... | collective-permute-start | bytes 1867784 | tf_op jit(solution)/shard_map/ppermute | solution.py:896
  116.7 22.8 %collective-permute-start.23 = (bf16[2,64,2048]{2,1,0:T(8,128)(2,1)S(1)}, bf16[2,64,2048]{2,1,0:T(8,128)(2,1)}, u32[]{:S(2)}, u32[]{:S(2)}) collective-permute-start(bf16[2,64,2048]{2,1,0:T(8,128)(2,1)S(1)} %collective-permute-done.19.refs_7_.refs_12_), channel_id=1, source_target_pairs={{0,16},{8,24},{16,0},{24,8},{1,17},{9,25},{17,1},{25,9},{2,18},{10... | collective-permute-start | bytes 1572872 | tf_op jit(solution)/shard_map/ppermute | solution.py:896
  174.7 23.1 %collective-permute-start.38 = (bf16[128,2048]{1,0:T(8,128)(2,1)S(1)}, bf16[128,2048]{1,0:T(8,128)(2,1)S(1)}, u32[]{:S(2)}, u32[]{:S(2)}) collective-permute-start(bf16[128,2048]{1,0:T(8,128)(2,1)S(1)} %collective-permute-done.34.refs_2_.refs_4_), channel_id=1, source_target_pairs={{0,1},{1,0},{2,3},{3,2},{4,5},{5,4},{6,7},{7,6},{8,9},{9,8},{10,11... | collective-permute-start | bytes 1572872 | tf_op jit(solution)/shard_map/ppermute | solution.py:899
  176.1 22.6 %collective-permute-start.39 = (bf16[128,2048]{1,0:T(8,128)(2,1)S(1)}, bf16[128,2048]{1,0:T(8,128)(2,1)}, u32[]{:S(2)}, u32[]{:S(2)}) collective-permute-start(bf16[128,2048]{1,0:T(8,128)(2,1)S(1)} %collective-permute-done.35.refs_5_.refs_7_), channel_id=1, source_target_pairs={{0,16},{8,24},{16,0},{24,8},{1,17},{9,25},{17,1},{25,9},{2,18},{10... | collective-permute-start | bytes 1572872 | tf_op jit(solution)/shard_map/ppermute | solution.py:896
  198.7 145.3 %reduce-scatter.5.cloned.1.call-start = ((), (), s32[]{:S(2)}) async-start(), calls=%async_computation.8 | async-start | bytes 3604480 | tf_op jit(solution)/shard_map/reduce_scatter | solution.py:921
  198.9 27.4 %collective-permute-start.33 = (bf16[128,2048]{1,0:T(8,128)(2,1)S(1)}, bf16[128,2048]{1,0:T(8,128)(2,1)S(1)}, u32[]{:S(2)}, u32[]{:S(2)}) collective-permute-start(bf16[128,2048]{1,0:T(8,128)(2,1)S(1)} %get-tuple-element.162.refs_1_.refs_0_), channel_id=1, source_target_pairs={{0,1},{1,0},{2,3},{3,2},{4,5},{5,4},{6,7},{7,6},{8,9},{9,8},{10,11... | collective-permute-start | bytes 1572872 | tf_op jit(solution)/shard_map/ppermute | solution.py:899
  200.0 26.3 %collective-permute-start.32 = (bf16[128,2048]{1,0:T(8,128)(2,1)S(1)}, bf16[128,2048]{1,0:T(8,128)(2,1)S(1)}, u32[]{:S(2)}, u32[]{:S(2)}) collective-permute-start(bf16[128,2048]{1,0:T(8,128)(2,1)S(1)} %get-tuple-element.163.refs_2_.refs_1_), channel_id=1, source_target_pairs={{0,16},{8,24},{16,0},{24,8},{1,17},{9,25},{17,1},{25,9},{2,18},{10... | collective-permute-start | bytes 1572872 | tf_op jit(solution)/shard_map/ppermute | solution.py:896
  257.6 204.8 %reduce-scatter.7.cloned.1.call-start = ((), (), s32[]{:S(2)}) async-start(), calls=%async_computation.9 | async-start | bytes 7208960 | tf_op jit(solution)/shard_map/reduce_scatter | solution.py:921
  298.9 25.9 %collective-permute-start.46 = (bf16[256,2048]{1,0:T(8,128)(2,1)}, bf16[256,2048]{1,0:T(8,128)(2,1)S(1)}, u32[]{:S(2)}, u32[]{:S(2)}) collective-permute-start(bf16[256,2048]{1,0:T(8,128)(2,1)} %get-tuple-element.187), channel_id=1, source_target_pairs={{0,1},{1,0},{2,3},{3,2},{4,5},{5,4},{6,7},{7,6},{8,9},{9,8},{10,11... | collective-permute-start | bytes 3145736 | tf_op jit(solution)/shard_map/ppermute | solution.py:899
  300.4 25.6 %collective-permute-start.47 = (bf16[256,2048]{1,0:T(8,128)(2,1)}, bf16[256,2048]{1,0:T(8,128)(2,1)S(1)}, u32[]{:S(2)}, u32[]{:S(2)}) collective-permute-start(bf16[256,2048]{1,0:T(8,128)(2,1)} %get-tuple-element.190), channel_id=1, source_target_pairs={{0,16},{8,24},{16,0},{24,8},{1,17},{9,25},{17,1},{25,9},{2,18},{10... | collective-permute-start | bytes 3145736 | tf_op jit(solution)/shard_map/ppermute | solution.py:896
  344.0 173.4 %reduce-scatter.11.cloned.1.call-start = ((), (), s32[]{:S(2)}) async-start(), calls=%async_computation.11 | async-start | bytes 1310720 | tf_op jit(solution)/shard_map/reduce_scatter | solution.py:921
  384.0 25.5 %collective-permute-start.60 = (bf16[256,2048]{1,0:T(8,128)(2,1)}, bf16[256,2048]{1,0:T(8,128)(2,1)S(1)}, u32[]{:S(2)}, u32[]{:S(2)}) collective-permute-start(bf16[256,2048]{1,0:T(8,128)(2,1)} %get-tuple-element.213), channel_id=1, source_target_pairs={{0,16},{8,24},{16,0},{24,8},{1,17},{9,25},{17,1},{25,9},{2,18},{10... | collective-permute-start | bytes 3145736 | tf_op jit(solution)/shard_map/ppermute | solution.py:896
  385.5 25.1 %collective-permute-start.61 = (bf16[256,2048]{1,0:T(8,128)(2,1)}, bf16[256,2048]{1,0:T(8,128)(2,1)S(1)}, u32[]{:S(2)}, u32[]{:S(2)}) collective-permute-start(bf16[256,2048]{1,0:T(8,128)(2,1)} %get-tuple-element.214), channel_id=1, source_target_pairs={{0,1},{1,0},{2,3},{3,2},{4,5},{5,4},{6,7},{7,6},{8,9},{9,8},{10,11... | collective-permute-start | bytes 3145736 | tf_op jit(solution)/shard_map/ppermute | solution.py:899
  433.6 28.3 %collective-permute-start.64 = (bf16[256,2304]{1,0:T(8,128)(2,1)}, bf16[256,2304]{1,0:T(8,128)(2,1)S(1)}, u32[]{:S(2)}, u32[]{:S(2)}) collective-permute-start(bf16[256,2304]{1,0:T(8,128)(2,1)} %get-tuple-element.219), channel_id=1, source_target_pairs={{0,1},{1,0},{2,3},{3,2},{4,5},{5,4},{6,7},{7,6},{8,9},{9,8},{10,11... | collective-permute-start | bytes 3538952 | tf_op jit(solution)/shard_map/ppermute | solution.py:899
  434.5 27.9 %collective-permute-start.65 = (bf16[256,2304]{1,0:T(8,128)(2,1)}, bf16[256,2304]{1,0:T(8,128)(2,1)S(1)}, u32[]{:S(2)}, u32[]{:S(2)}) collective-permute-start(bf16[256,2304]{1,0:T(8,128)(2,1)} %get-tuple-element.222), channel_id=1, source_target_pairs={{0,16},{8,24},{16,0},{24,8},{1,17},{9,25},{17,1},{25,9},{2,18},{10... | collective-permute-start | bytes 3538952 | tf_op jit(solution)/shard_map/ppermute | solution.py:896
  467.8 59.8 %reduce-scatter.9.cloned.1.call-start = ((), (), s32[]{:S(2)}) async-start(), calls=%async_computation.10 | async-start | bytes 1556480 | tf_op jit(solution)/shard_map/reduce_scatter | solution.py:921
  486.1 23.1 %collective-permute-start.68 = (bf16[256,2048]{1,0:T(8,128)(2,1)}, bf16[256,2048]{1,0:T(8,128)(2,1)S(1)}, u32[]{:S(2)}, u32[]{:S(2)}) collective-permute-start(bf16[256,2048]{1,0:T(8,128)(2,1)} %get-tuple-element.235), channel_id=1, source_target_pairs={{0,1},{1,0},{2,3},{3,2},{4,5},{5,4},{6,7},{7,6},{8,9},{9,8},{10,11... | collective-permute-start | bytes 3145736 | tf_op jit(solution)/shard_map/ppermute | solution.py:899
  487.1 22.8 %collective-permute-start.69 = (bf16[256,2048]{1,0:T(8,128)(2,1)}, bf16[256,2048]{1,0:T(8,128)(2,1)S(1)}, u32[]{:S(2)}, u32[]{:S(2)}) collective-permute-start(bf16[256,2048]{1,0:T(8,128)(2,1)} %get-tuple-element.238), channel_id=1, source_target_pairs={{0,16},{8,24},{16,0},{24,8},{1,17},{9,25},{17,1},{25,9},{2,18},{10... | collective-permute-start | bytes 3145736 | tf_op jit(solution)/shard_map/ppermute | solution.py:896
  (130 other events, 1704.6 us)
Sparse Core Ops, SparseCore 0:
  10.2 34.2 all-gather.4
  46.0 26.9 all-gather.6
  75.2 106.1 all-gather.8
  198.8 58.6 all-gather.10
  260.3 54.8 reduce-scatter.4
  344.1 99.9 reduce-scatter.6
  467.9 25.4 reduce-scatter.10
  495.8 28.8 reduce-scatter.8

commit v7 on v6

--- a/solution.py
+++ b/solution.py
@@ -171,8 +171,8 @@
     count = len(pieces.arrays)
     spot, tokens, cosines, sines = refs[:4]
     shards = refs[4 : 4 + count]
-    h_turned, q_out, kv_out, gain_out = refs[4 + count : 8 + count]
-    whole, h_low, flat, sem = refs[8 + count :]
+    h_low, q_out, kv_out, gain_out = refs[4 + count : 8 + count]
+    whole, sem = refs[8 + count :]
     pieces.start(shards, spot, whole, sem)
     width = tokens.shape[1]
     x_full = tokens[...].astype(f32)
@@ -199,13 +199,6 @@
             column = pl.multiple_of(start + head * head_dim, head_dim)
             q_out[:, pl.ds(column, head_dim)] = (own * cos + swap_halves(own) * sin).astype(bf16)
 
-    @pl.loop(0, width // step)
-    def _(block):
-        start = pl.multiple_of(block * step, step)
-        flat[pl.ds(start, step), :] = h_low[:, pl.ds(start, step)].T
-
-    put_in_order(flat, h_turned, spot, pieces.depth, pieces.rows)
-
 
 def project(spot, tokens, cosines, sines, pieces, q_width, kv_width, head_dim, late=()):
     length, width = tokens.shape
@@ -214,22 +207,21 @@
     return kernel_call(
         functools.partial(project_body, pieces, q_width, kv_width, head_dim),
         (
-            shape((width, length), bf16),
+            shape((length, width), bf16),
             shape((length, q_width), bf16),
             shape((length, kv_width), bf16),
             shape((8, width), f32),
         ),
         [
             pltpu.VMEM((width, pieces.columns), bf16),
-            pltpu.VMEM((length, width), bf16),
-            pltpu.VMEM((width, length), bf16),
             pltpu.SemaphoreType.DMA,
         ],
         [smem_spec(), vmem_spec(), vmem_spec(), vmem_spec()] + [any_spec()] * count,
     )(spot, tokens, cosines, sines, *pieces.arrays, *late)
 
 
-def attend_body(depth, rows, head_dim, spot, q_low, kv_low, prob_out, attended_out, turned, flat):
+def attend_body(depth, rows, head_dim, *refs):
+    spot, q_low, kv_low, h_low, prob_out, attended_out, turned, h_turned, flat = refs
     length, q_width = q_low.shape
     scale = head_dim ** (-0.5)
     keys = kv_low[:, :head_dim]
@@ -252,10 +244,17 @@
             flat[pl.ds(column, head_dim), :] = mixed.astype(bf16)
             attended_out[:, pl.ds(column, head_dim)] = mixed.T.astype(bf16)
 
-    put_in_order(flat, turned, spot, depth, rows)
-
-
-def attend(spot, q_low, kv_low, depth, rows, late=()):
+    put_in_order(flat.at[pl.ds(0, q_width)], turned, spot, depth, rows)
+
+    @pl.loop(0, h_low.shape[1] // step)
+    def _(block):
+        start = pl.multiple_of(block * step, step)
+        flat[pl.ds(start, step), :] = h_low[:, pl.ds(start, step)].T
+
+    put_in_order(flat.at[pl.ds(0, h_turned.shape[0])], h_turned, spot, depth, rows)
+
+
+def attend(spot, q_low, kv_low, h_low, depth, rows, late=()):
     length, q_width = q_low.shape
     head_dim = kv_low.shape[1] // 2
     shape = jax.ShapeDtypeStruct
@@ -265,10 +264,11 @@
             shape((q_width // head_dim, length, length), bf16),
             shape((length, q_width), bf16),
             shape((q_width, length), bf16),
+            shape((h_low.shape[1], length), bf16),
         ),
-        [pltpu.VMEM((q_width, length), bf16)],
-        [smem_spec(), vmem_spec(), vmem_spec()],
-    )(spot, q_low, kv_low, *late)
+        [pltpu.VMEM((max(q_width, h_low.shape[1]), length), bf16)],
+        [smem_spec(), vmem_spec(), vmem_spec(), vmem_spec()],
+    )(spot, q_low, kv_low, h_low, *late)
 
 
 def mix_body(pieces, *refs):
@@ -1014,11 +1014,13 @@
     down_mine = grid.gather_outer(w_down)
     w_o_column = after(w_o_column, in_planes[1, 1]).reshape(grid.depth, shard_rows, -1)
     o_first = grid.spread_first(w_o_column[:cut], w_o_column[cut:])
-    h_turned, q_low, kv_out, gain_rows = project(
+    h_one, q_low, kv_out, gain_rows = project(
         grid.spot, tokens, cosines, sines, in_pieces, q_width, kv_width, head_dim
     )
     o_planes = grid.spread_second(*after(o_first, q_low))
-    prob, attended, turned = attend(grid.spot, q_low, kv_out, grid.depth, shard_rows)
+    prob, attended, turned, h_turned = attend(
+        grid.spot, q_low, kv_out, h_one, grid.depth, shard_rows
+    )
     o_pieces = grid.pieces(o_planes, shard_rows, attended)
     x_mid, h_first, h_second = mix(grid.spot, tokens, attended, gain_rows, o_pieces)
 

time: 537 us -> 535 us (level)
  transfers between devices with their start and end apart: 86 -> 86, of which waited for: 49 -> 48; matrix products, arithmetic and copies ran while one was open for 4% -> 4% of each run, Pallas kernels for 43% -> 43%
where the time goes in v7:
time: 535 us; the launch traced here: 534 us
  Pallas kernels  232 us (43%)
  waiting for transfers between devices  193 us (36%)
  starting transfers between devices  54 us (10%)
  local copies, waits for them, and re-layouts  23.2 us (4%)
  other arithmetic  16.6 us (3%)
  between operations  15.6 us (3%)
    pallas_call x26, Pallas kernels, run(): pl.pallas_call(whole_body, out_shape=out_shapes, in_specs=in_specs + [any...  232 us
    ppermute x21, waiting for transfers between devices, y_swap(): return lax.ppermute(value, 'fsdp', [(i, i ^ 1) for i in range(self.fsdp)])  115 us
    ppermute x21, waiting for transfers between devices, x_swap(): return lax.ppermute(value, 'dp', [(i, i ^ 2) for i in range(self.dp)])  45.9 us
    ppermute x35, waiting for transfers between devices, core(): return lax.ppermute(value, 'dp', [(i, i ^ 1) for i in range(self.dp)])  26.4 us
    ppermute x21, starting transfers between devices, x_swap(): return lax.ppermute(value, 'dp', [(i, i ^ 2) for i in range(self.dp)])  23.8 us
    ppermute x21, starting transfers between devices, y_swap(): return lax.ppermute(value, 'fsdp', [(i, i ^ 1) for i in range(self.fsdp)])  22 us
    unnamed x138, local copies, waits for them, and re-layouts  13.7 us
  transfers between devices with their start and end apart: 86, of which 48 were waited for; matrix products, arithmetic and copies ran while one was open for 4% of the time, Pallas kernels for 43%

profile of v7, /device:TPU:0, one launch (start us, length us, event | category | flops | bytes accessed | tf_op | source)
XLA Modules:
  0.0 534.2 jit_solution(7190689468803687953)
XLA Ops:
  20.6 10.4 %collective-permute-done.1.refs_6_.refs_5_ = bf16[128,2048]{1,0:T(8,128)(2,1)S(1)} collective-permute-done((bf16[128,2048]{1,0:T(8,128)(2,1)S(1)}, bf16[128,2048]{1,0:T(8,128)(2,1)S(1)}, u32[]{:S(2)}, u32[]{:S(2)}) %collective-permute-start.1) | collective-permute-done | bytes 524320 | tf_op jit(solution)/shard_map/ppermute | solution.py:899
  34.4 10.6 %collective-permute-done.2.refs_7_.refs_6_ = bf16[128,2048]{1,0:T(8,128)(2,1)S(1)} collective-permute-done((bf16[128,2048]{1,0:T(8,128)(2,1)S(1)}, bf16[128,2048]{1,0:T(8,128)(2,1)S(1)}, u32[]{:S(2)}, u32[]{:S(2)}) %collective-permute-start.2) | collective-permute-done | bytes 524320 | tf_op jit(solution)/shard_map/ppermute | solution.py:899
  50.6 11.3 %collective-permute-done.4.refs_8_.refs_9_ = bf16[2,64,2432]{2,1,0:T(8,128)(2,1)} collective-permute-done((bf16[2,64,2432]{2,1,0:T(8,128)(2,1)S(1)}, bf16[2,64,2432]{2,1,0:T(8,128)(2,1)}, u32[]{:S(2)}, u32[]{:S(2)}) %collective-permute-start.4) | collective-permute-done | bytes 622624 | tf_op jit(solution)/shard_map/ppermute | solution.py:896
  67.4 12.8 %collective-permute-done.6.refs_6_.refs_7_ = bf16[2,64,2432]{2,1,0:T(8,128)(2,1)} collective-permute-done((bf16[2,64,2432]{2,1,0:T(8,128)(2,1)S(1)}, bf16[2,64,2432]{2,1,0:T(8,128)(2,1)}, u32[]{:S(2)}, u32[]{:S(2)}) %collective-permute-start.6) | collective-permute-done | bytes 622624 | tf_op jit(solution)/shard_map/ppermute | solution.py:899
  81.9 11.2 %collective-permute-done.8.refs_10_.refs_11_ = bf16[2,64,2432]{2,1,0:T(8,128)(2,1)} collective-permute-done((bf16[2,64,2432]{2,1,0:T(8,128)(2,1)}, bf16[2,64,2432]{2,1,0:T(8,128)(2,1)}, u32[]{:S(2)}, u32[]{:S(2)}) %collective-permute-start.8) | collective-permute-done | bytes 622624 | tf_op jit(solution)/shard_map/ppermute | solution.py:899
  100.4 11.4 %project.1 = (bf16[256,2048]{1,0:T(8,128)(2,1)}, bf16[256,2048]{1,0:T(8,128)(2,1)}, bf16[256,256]{1,0:T(8,128)(2,1)}, f32[8,2048]{1,0:T(8,128)}) custom-call(s32[2]{0:T(128)} %pad_add_fusion.refs_0_, bf16[256,2048]{1,0:T(8,128)(2,1)} %refs_1_.5, f32[256,128]{1,0:T(8,128)} %get-tuple-element.264.refs_2_.refs_7_, ...), custom_call_target="tpu_custom_call" | custom-call | flops 1 | bytes 1 | tf_op jit(solution)/shard_map/project/pallas_call | solution.py:68
  115.9 13.2 %attend.1 = (bf16[16,256,256]{2,1,0:T(8,128)(2,1)}, bf16[256,2048]{1,0:T(8,128)(2,1)}, bf16[2048,256]{1,0:T(8,128)(2,1)}, bf16[2048,256]{1,0:T(8,128)(2,1)}) custom-call(s32[2]{0:T(128)} %pad_add_fusion.refs_0_, bf16[256,2048]{1,0:T(8,128)(2,1)} %get-tuple-element.140.refs_1_.refs_4_, bf16[256,256]{1,0:T(8,128)(2,1)} %get-tuple-element.124.refs_2_.refs_5_, ...), custom_call_target="tpu_custom_call" | custom-call | flops 1 | bytes 1 | tf_op jit(solution)/shard_map/attend/pallas_call | solution.py:68
  146.4 9.7 %mix.1 = (f32[256,2048]{1,0:T(8,128)}, bf16[128,2048]{1,0:T(8,128)(2,1)}, bf16[128,2048]{1,0:T(8,128)(2,1)}) custom-call(s32[2]{0:T(128)} %pad_add_fusion.refs_0_, bf16[256,2048]{1,0:T(8,128)(2,1)} %refs_1_.5, bf16[256,2048]{1,0:T(8,128)(2,1)} %get-tuple-element.143.refs_2_, f32[8,2048]{1,0:T(8,128)} %get-tuple-element.144.refs_3_.refs_1_.refs_2_, ...), custom_call_target="tpu_custom_call" | custom-call | flops 1 | bytes 1 | tf_op jit(solution)/shard_map/mix/pallas_call | solution.py:68
  158.4 12.0 %collective-permute-done.34.refs_2_.refs_4_ = bf16[128,2048]{1,0:T(8,128)(2,1)S(1)} collective-permute-done((bf16[128,2048]{1,0:T(8,128)(2,1)}, bf16[128,2048]{1,0:T(8,128)(2,1)S(1)}, u32[]{:S(2)}, u32[]{:S(2)}) %collective-permute-start.34) | collective-permute-done | bytes 524320 | tf_op jit(solution)/shard_map/ppermute | solution.py:896
  175.6 11.0 %collective-permute-done.37.refs_4_.refs_6_ = bf16[128,2048]{1,0:T(8,128)(2,1)S(1)} collective-permute-done((bf16[128,2048]{1,0:T(8,128)(2,1)}, bf16[128,2048]{1,0:T(8,128)(2,1)S(1)}, u32[]{:S(2)}, u32[]{:S(2)}) %collective-permute-start.37) | collective-permute-done | bytes 524320 | tf_op jit(solution)/shard_map/ppermute | solution.py:899
  198.8 12.7 %gate.2 = (bf16[1024,704]{1,0:T(8,128)(2,1)}, bf16[1024,704]{1,0:T(8,128)(2,1)}, bf16[1024,704]{1,0:T(8,128)(2,1)}) custom-call(bf16[128,2048]{1,0:T(8,128)(2,1)} %get-tuple-element.168.refs_0_.refs_2_, bf16[128,2048]{1,0:T(8,128)(2,1)} %get-tuple-element.169.refs_1_.refs_3_, bf16[128,2048]{1,0:T(8,128)(2,1)} %copy-done.10, bf16[128,2048]{1,0:T(8,128)(2,1)} %copy-done.13, ...), custom_call_target="tpu_custom_call" | custom-call | flops 1 | bytes 1 | tf_op jit(solution)/shard_map/gate/pallas_call | solution.py:68
  211.5 12.8 %gate.3 = (bf16[1024,704]{1,0:T(8,128)(2,1)}, bf16[1024,704]{1,0:T(8,128)(2,1)}, bf16[1024,704]{1,0:T(8,128)(2,1)}) custom-call(bf16[128,2048]{1,0:T(8,128)(2,1)} %get-tuple-element.168.refs_0_.refs_2_, bf16[128,2048]{1,0:T(8,128)(2,1)} %get-tuple-element.169.refs_1_.refs_3_, bf16[128,2048]{1,0:T(8,128)(2,1)} %copy-done.10, bf16[128,2048]{1,0:T(8,128)(2,1)} %copy-done.13, ...), custom_call_target="tpu_custom_call" | custom-call | flops 1 | bytes 1 | tf_op jit(solution)/shard_map/gate/pallas_call | solution.py:68
  225.4 9.4 %hidden_sums.4 = (bf16[176,2048]{1,0:T(8,128)(2,1)}, bf16[176,2048]{1,0:T(8,128)(2,1)}, bf16[176,2048]{1,0:T(8,128)(2,1)}, bf16[176,2048]{1,0:T(8,128)(2,1)}) custom-call(bf16[1024,704]{1,0:T(8,128)(2,1)} %get-tuple-element.174.refs_0_.refs_1_, bf16[128,2048]{1,0:T(8,128)(2,1)} %copy-done.1, bf16[128,2048]{1,0:T(8,128)(2,1)} %copy-done, ...), custom_call_target="tpu_custom_call" | custom-call | flops 1 | bytes 1 | tf_op jit(solution)/shard_map/hidden_sums/pallas_call | solution.py:68
  241.3 9.6 %hidden_sums.5 = bf16[704,2048]{1,0:T(8,128)(2,1)} custom-call(bf16[1024,704]{1,0:T(8,128)(2,1)} %get-tuple-element.173.refs_9_.refs_0_, bf16[128,2048]{1,0:T(8,128)(2,1)} %copy-done.1, bf16[128,2048]{1,0:T(8,128)(2,1)} %copy-done, bf16[128,2048]{1,0:T(8,128)(2,1)} %copy-done.5, bf16[128,2048]{1,0:T(8,128)(2,1)} %copy-done.9, bf16[128,2048]{1,0:T(8,128)(2,1)} %copy-done.8, ...), custom_call_target="tpu_custom_call" | custom-call | flops 1 | bytes 1 | tf_op jit(solution)/shard_map/hidden_sums/pallas_call | solution.py:68
  266.4 8.9 %gate_back.3 = (bf16[1024,704]{1,0:T(8,128)(2,1)}, bf16[1024,704]{1,0:T(8,128)(2,1)}) custom-call(bf16[128,2048]{1,0:T(8,128)(2,1)} %copy-done.1, bf16[128,2048]{1,0:T(8,128)(2,1)} %copy-done, bf16[128,2048]{1,0:T(8,128)(2,1)} %copy-done.5, bf16[128,2048]{1,0:T(8,128)(2,1)} %copy-done.9, bf16[128,2048]{1,0:T(8,128)(2,1)} %copy-done.8, ...), custom_call_target="tpu_custom_call" | custom-call | flops 1 | bytes 1 | tf_op jit(solution)/shard_map/gate_back/pallas_call | solution.py:68
  275.3 21.7 %rows_back.1 = (bf16[128,2048]{1,0:T(8,128)(2,1)}, bf16[128,2048]{1,0:T(8,128)(2,1)}, bf16[128,2048]{1,0:T(8,128)(2,1)}, bf16[128,2048]{1,0:T(8,128)(2,1)}, bf16...) custom-call(bf16[1024,704]{1,0:T(8,128)(2,1)} %get-tuple-element.182.refs_11_.refs_0_, ...), custom_call_target="tpu_custom_call" | custom-call | flops 1 | bytes 1 | tf_op jit(solution)/shard_map/rows_back/pallas_call | solution.py:68
  300.0 13.8 %hidden_sums.6 = (bf16[176,2048]{1,0:T(8,128)(2,1)}, bf16[176,2048]{1,0:T(8,128)(2,1)}, bf16[176,2048]{1,0:T(8,128)(2,1)}, bf16[176,2048]{1,0:T(8,128)(2,1)}, bf...) custom-call(bf16[1024,704]{1,0:T(8,128)(2,1)} %get-tuple-element.186, ...), custom_call_target="tpu_custom_call" | custom-call | flops 1 | bytes 1 | tf_op jit(solution)/shard_map/hidden_sums/pallas_call | solution.py:68
  327.5 14.2 %hidden_sums.7.refs_10_ = bf16[1408,2048]{1,0:T(8,128)(2,1)} custom-call(bf16[1024,704]{1,0:T(8,128)(2,1)} %get-tuple-element.182.refs_11_.refs_0_, bf16[1024,704]{1,0:T(8,128)(2,1)} %get-tuple-element.183.refs_1_, bf16[128,2048]{1,0:T(8,128)(2,1)} %get-tuple-element.168.refs_0_.refs_2_, bf16[128,2048]{1,0:T(8,128)(2,1)} %get-tuple-element.169.refs_1_.refs_3_, ...), custom_call_target="tpu_custom_call" | custom-call | flops 1 | bytes 1 | tf_op jit(solution)/shard_map/hidden_sums/pallas_call | solution.py:68
  344.8 11.3 %collective-permute-done.49.refs_9_ = bf16[128,2048]{1,0:T(8,128)(2,1)S(1)} collective-permute-done((bf16[128,2048]{1,0:T(8,128)(2,1)S(1)}, bf16[128,2048]{1,0:T(8,128)(2,1)S(1)}, u32[]{:S(2)}, u32[]{:S(2)}) %collective-permute-start.49) | collective-permute-done | bytes 524320 | tf_op jit(solution)/shard_map/ppermute | solution.py:899
  384.1 19.1 %attend_back.1 = (bf16[256,2304]{1,0:T(8,128)(2,1)}, f32[256,256]{1,0:T(8,128)}) custom-call(s32[2]{0:T(128)} %pad_add_fusion.refs_0_, f32[1]{0:T(128)} %bitcast.9.refs_0_.refs_1_, bf16[256,2048]{1,0:T(8,128)(2,1)} %get-tuple-element.206.refs_1_.refs_2_, bf16[256,256]{1,0:T(8,128)(2,1)} %refs_3_.3, bf16[256,2048]{1,0:T(8,128)(2,1)} %get-tuple-element.140.refs_1_.refs_4_, ...), custom_call_target="tpu_custom_call" | custom-call | flops 1 | bytes 1 | tf_op jit(solution)/shard_map/attend_back/pallas_call | solution.py:68
  436.3 12.8 %finish.1 = (f32[256,2048]{1,0:T(8,128)}, f32[8,2048]{1,0:T(8,128)}) custom-call(s32[2]{0:T(128)} %pad_add_fusion.refs_0_, bf16[256,2048]{1,0:T(8,128)(2,1)} %refs_1_.5, f32[8,2048]{1,0:T(8,128)} %get-tuple-element.144.refs_3_.refs_1_.refs_2_, bf16[256,2304]{1,0:T(8,128)(2,1)} %get-tuple-element.212.refs_4_.refs_1_.refs_3_, ...), custom_call_target="tpu_custom_call" | custom-call | flops 1 | bytes 1 | tf_op jit(solution)/shard_map/finish/pallas_call | solution.py:68
  450.1 9.8 %collective-permute-done.64.refs_3_ = bf16[256,2304]{1,0:T(8,128)(2,1)S(1)} collective-permute-done((bf16[256,2304]{1,0:T(8,128)(2,1)}, bf16[256,2304]{1,0:T(8,128)(2,1)S(1)}, u32[]{:S(2)}, u32[]{:S(2)}) %collective-permute-start.64) | collective-permute-done | bytes 1179680 | tf_op jit(solution)/shard_map/ppermute | solution.py:899
  470.5 11.8 %down.1 = (bf16[128,2048]{1,0:T(8,128)(2,1)}, bf16[128,2048]{1,0:T(8,128)(2,1)}, bf16[128,2048]{1,0:T(8,128)(2,1)}, bf16[128,2048]{1,0:T(8,128)(2,1)}, bf16[256,...) custom-call(bf16[1024,704]{1,0:T(8,128)(2,1)} %get-tuple-element.173.refs_9_.refs_0_, ...), custom_call_target="tpu_custom_call" | custom-call | flops 1 | bytes 1 | tf_op jit(solution)/shard_map/down/pallas_call | solution.py:68
  487.8 19.3 %collective-permute-done.68.refs_3_ = bf16[256,2048]{1,0:T(8,128)(2,1)S(1)} collective-permute-done((bf16[256,2048]{1,0:T(8,128)(2,1)}, bf16[256,2048]{1,0:T(8,128)(2,1)S(1)}, u32[]{:S(2)}, u32[]{:S(2)}) %collective-permute-start.68) | collective-permute-done | bytes 1048608 | tf_op jit(solution)/shard_map/ppermute | solution.py:899
  (351 shorter events, 217.8 us)
Async XLA Ops:
  7.2 38.3 %all-gather.5.cloned.1.call-start = ((), (), s32[]{:S(2)}) async-start(), calls=%async_computation.4 | async-start | bytes 1556480 | tf_op jit(solution)/shard_map/all_gather | solution.py:918
  9.8 83.4 %all-gather.7.cloned.1.call-start = ((), (), s32[]{:S(2)}) async-start(), calls=%async_computation.5 | async-start | bytes 1310720 | tf_op jit(solution)/shard_map/all_gather | solution.py:918
  10.5 186.2 %all-gather.9.cloned.1.call-start = ((), (), s32[]{:S(2)}) async-start(), calls=%async_computation.6 | async-start | bytes 7208960 | tf_op jit(solution)/shard_map/all_gather | solution.py:918
  13.7 242.0 %all-gather.11.cloned.1.call-start = ((), (), s32[]{:S(2)}) async-start(), calls=%async_computation.7 | async-start | bytes 3604480 | tf_op jit(solution)/shard_map/all_gather | solution.py:918
  65.3 27.9 %collective-permute-start.8 = (bf16[2,64,2432]{2,1,0:T(8,128)(2,1)}, bf16[2,64,2432]{2,1,0:T(8,128)(2,1)}, u32[]{:S(2)}, u32[]{:S(2)}) collective-permute-start(bf16[2,64,2432]{2,1,0:T(8,128)(2,1)} %collective-permute-done.4.refs_8_.refs_9_), channel_id=1, source_target_pairs={{0,1},{1,0},{2,3},{3,2},{4,5},{5,4},{6,7},{7,6},{8,9},{9,8},{10,11... | collective-permute-start | bytes 1867784 | tf_op jit(solution)/shard_map/ppermute | solution.py:899
  65.9 27.3 %collective-permute-start.11 = (bf16[2,64,2432]{2,1,0:T(8,128)(2,1)}, bf16[2,64,2432]{2,1,0:T(8,128)(2,1)}, u32[]{:S(2)}, u32[]{:S(2)}) collective-permute-start(bf16[2,64,2432]{2,1,0:T(8,128)(2,1)} %bitcast.6.refs_5_.refs_6_), channel_id=1, source_target_pairs={{0,8},{8,0},{16,24},{24,16},{1,9},{9,1},{17,25},{25,17},{2,10},{10... | collective-permute-start | bytes 1867784 | tf_op jit(solution)/shard_map/ppermute | solution.py:885
  65.9 28.7 %collective-permute-start.7 = (bf16[2,64,2432]{2,1,0:T(8,128)(2,1)}, bf16[2,64,2432]{2,1,0:T(8,128)(2,1)}, u32[]{:S(2)}, u32[]{:S(2)}) collective-permute-start(bf16[2,64,2432]{2,1,0:T(8,128)(2,1)} %bitcast.6.refs_5_.refs_6_), channel_id=1, source_target_pairs={{0,16},{8,24},{16,0},{24,8},{1,17},{9,25},{17,1},{25,9},{2,18},{10... | collective-permute-start | bytes 1867784 | tf_op jit(solution)/shard_map/ppermute | solution.py:896
  114.8 22.8 %collective-permute-start.23 = (bf16[2,64,2048]{2,1,0:T(8,128)(2,1)S(1)}, bf16[2,64,2048]{2,1,0:T(8,128)(2,1)}, u32[]{:S(2)}, u32[]{:S(2)}) collective-permute-start(bf16[2,64,2048]{2,1,0:T(8,128)(2,1)S(1)} %collective-permute-done.19.refs_7_.refs_12_), channel_id=1, source_target_pairs={{0,16},{8,24},{16,0},{24,8},{1,17},{9,25},{17,1},{25,9},{2,18},{10... | collective-permute-start | bytes 1572872 | tf_op jit(solution)/shard_map/ppermute | solution.py:896
  172.8 23.1 %collective-permute-start.38 = (bf16[128,2048]{1,0:T(8,128)(2,1)S(1)}, bf16[128,2048]{1,0:T(8,128)(2,1)S(1)}, u32[]{:S(2)}, u32[]{:S(2)}) collective-permute-start(bf16[128,2048]{1,0:T(8,128)(2,1)S(1)} %collective-permute-done.34.refs_2_.refs_4_), channel_id=1, source_target_pairs={{0,1},{1,0},{2,3},{3,2},{4,5},{5,4},{6,7},{7,6},{8,9},{9,8},{10,11... | collective-permute-start | bytes 1572872 | tf_op jit(solution)/shard_map/ppermute | solution.py:899
  174.2 22.6 %collective-permute-start.39 = (bf16[128,2048]{1,0:T(8,128)(2,1)S(1)}, bf16[128,2048]{1,0:T(8,128)(2,1)}, u32[]{:S(2)}, u32[]{:S(2)}) collective-permute-start(bf16[128,2048]{1,0:T(8,128)(2,1)S(1)} %collective-permute-done.35.refs_5_.refs_7_), channel_id=1, source_target_pairs={{0,16},{8,24},{16,0},{24,8},{1,17},{9,25},{17,1},{25,9},{2,18},{10... | collective-permute-start | bytes 1572872 | tf_op jit(solution)/shard_map/ppermute | solution.py:896
  196.8 145.0 %reduce-scatter.5.cloned.1.call-start = ((), (), s32[]{:S(2)}) async-start(), calls=%async_computation.8 | async-start | bytes 3604480 | tf_op jit(solution)/shard_map/reduce_scatter | solution.py:921
  197.0 27.4 %collective-permute-start.33 = (bf16[128,2048]{1,0:T(8,128)(2,1)S(1)}, bf16[128,2048]{1,0:T(8,128)(2,1)S(1)}, u32[]{:S(2)}, u32[]{:S(2)}) collective-permute-start(bf16[128,2048]{1,0:T(8,128)(2,1)S(1)} %get-tuple-element.164.refs_1_.refs_0_), channel_id=1, source_target_pairs={{0,1},{1,0},{2,3},{3,2},{4,5},{5,4},{6,7},{7,6},{8,9},{9,8},{10,11... | collective-permute-start | bytes 1572872 | tf_op jit(solution)/shard_map/ppermute | solution.py:899
  198.1 26.3 %collective-permute-start.32 = (bf16[128,2048]{1,0:T(8,128)(2,1)S(1)}, bf16[128,2048]{1,0:T(8,128)(2,1)S(1)}, u32[]{:S(2)}, u32[]{:S(2)}) collective-permute-start(bf16[128,2048]{1,0:T(8,128)(2,1)S(1)} %get-tuple-element.165.refs_2_.refs_1_), channel_id=1, source_target_pairs={{0,16},{8,24},{16,0},{24,8},{1,17},{9,25},{17,1},{25,9},{2,18},{10... | collective-permute-start | bytes 1572872 | tf_op jit(solution)/shard_map/ppermute | solution.py:896
  255.7 204.5 %reduce-scatter.7.cloned.1.call-start = ((), (), s32[]{:S(2)}) async-start(), calls=%async_computation.9 | async-start | bytes 7208960 | tf_op jit(solution)/shard_map/reduce_scatter | solution.py:921
  297.0 25.9 %collective-permute-start.46 = (bf16[256,2048]{1,0:T(8,128)(2,1)}, bf16[256,2048]{1,0:T(8,128)(2,1)S(1)}, u32[]{:S(2)}, u32[]{:S(2)}) collective-permute-start(bf16[256,2048]{1,0:T(8,128)(2,1)} %get-tuple-element.189), channel_id=1, source_target_pairs={{0,1},{1,0},{2,3},{3,2},{4,5},{5,4},{6,7},{7,6},{8,9},{9,8},{10,11... | collective-permute-start | bytes 3145736 | tf_op jit(solution)/shard_map/ppermute | solution.py:899
  298.5 25.6 %collective-permute-start.47 = (bf16[256,2048]{1,0:T(8,128)(2,1)}, bf16[256,2048]{1,0:T(8,128)(2,1)S(1)}, u32[]{:S(2)}, u32[]{:S(2)}) collective-permute-start(bf16[256,2048]{1,0:T(8,128)(2,1)} %get-tuple-element.192), channel_id=1, source_target_pairs={{0,16},{8,24},{16,0},{24,8},{1,17},{9,25},{17,1},{25,9},{2,18},{10... | collective-permute-start | bytes 3145736 | tf_op jit(solution)/shard_map/ppermute | solution.py:896
  341.8 173.5 %reduce-scatter.11.cloned.1.call-start = ((), (), s32[]{:S(2)}) async-start(), calls=%async_computation.11 | async-start | bytes 1310720 | tf_op jit(solution)/shard_map/reduce_scatter | solution.py:921
  381.9 25.5 %collective-permute-start.60 = (bf16[256,2048]{1,0:T(8,128)(2,1)}, bf16[256,2048]{1,0:T(8,128)(2,1)S(1)}, u32[]{:S(2)}, u32[]{:S(2)}) collective-permute-start(bf16[256,2048]{1,0:T(8,128)(2,1)} %get-tuple-element.215), channel_id=1, source_target_pairs={{0,16},{8,24},{16,0},{24,8},{1,17},{9,25},{17,1},{25,9},{2,18},{10... | collective-permute-start | bytes 3145736 | tf_op jit(solution)/shard_map/ppermute | solution.py:896
  383.5 25.1 %collective-permute-start.61 = (bf16[256,2048]{1,0:T(8,128)(2,1)}, bf16[256,2048]{1,0:T(8,128)(2,1)S(1)}, u32[]{:S(2)}, u32[]{:S(2)}) collective-permute-start(bf16[256,2048]{1,0:T(8,128)(2,1)} %get-tuple-element.216), channel_id=1, source_target_pairs={{0,1},{1,0},{2,3},{3,2},{4,5},{5,4},{6,7},{7,6},{8,9},{9,8},{10,11... | collective-permute-start | bytes 3145736 | tf_op jit(solution)/shard_map/ppermute | solution.py:899
  431.5 28.3 %collective-permute-start.64 = (bf16[256,2304]{1,0:T(8,128)(2,1)}, bf16[256,2304]{1,0:T(8,128)(2,1)S(1)}, u32[]{:S(2)}, u32[]{:S(2)}) collective-permute-start(bf16[256,2304]{1,0:T(8,128)(2,1)} %get-tuple-element.221), channel_id=1, source_target_pairs={{0,1},{1,0},{2,3},{3,2},{4,5},{5,4},{6,7},{7,6},{8,9},{9,8},{10,11... | collective-permute-start | bytes 3538952 | tf_op jit(solution)/shard_map/ppermute | solution.py:899
  432.3 27.9 %collective-permute-start.65 = (bf16[256,2304]{1,0:T(8,128)(2,1)}, bf16[256,2304]{1,0:T(8,128)(2,1)S(1)}, u32[]{:S(2)}, u32[]{:S(2)}) collective-permute-start(bf16[256,2304]{1,0:T(8,128)(2,1)} %get-tuple-element.224), channel_id=1, source_target_pairs={{0,16},{8,24},{16,0},{24,8},{1,17},{9,25},{17,1},{25,9},{2,18},{10... | collective-permute-start | bytes 3538952 | tf_op jit(solution)/shard_map/ppermute | solution.py:896
  465.6 59.9 %reduce-scatter.9.cloned.1.call-start = ((), (), s32[]{:S(2)}) async-start(), calls=%async_computation.10 | async-start | bytes 1556480 | tf_op jit(solution)/shard_map/reduce_scatter | solution.py:921
  484.0 23.1 %collective-permute-start.68 = (bf16[256,2048]{1,0:T(8,128)(2,1)}, bf16[256,2048]{1,0:T(8,128)(2,1)S(1)}, u32[]{:S(2)}, u32[]{:S(2)}) collective-permute-start(bf16[256,2048]{1,0:T(8,128)(2,1)} %get-tuple-element.237), channel_id=1, source_target_pairs={{0,1},{1,0},{2,3},{3,2},{4,5},{5,4},{6,7},{7,6},{8,9},{9,8},{10,11... | collective-permute-start | bytes 3145736 | tf_op jit(solution)/shard_map/ppermute | solution.py:899
  485.0 22.9 %collective-permute-start.69 = (bf16[256,2048]{1,0:T(8,128)(2,1)}, bf16[256,2048]{1,0:T(8,128)(2,1)S(1)}, u32[]{:S(2)}, u32[]{:S(2)}) collective-permute-start(bf16[256,2048]{1,0:T(8,128)(2,1)} %get-tuple-element.240), channel_id=1, source_target_pairs={{0,16},{8,24},{16,0},{24,8},{1,17},{9,25},{17,1},{25,9},{2,18},{10... | collective-permute-start | bytes 3145736 | tf_op jit(solution)/shard_map/ppermute | solution.py:896
  (130 other events, 1694.4 us)
Sparse Core Ops, SparseCore 0:
  10.2 34.2 all-gather.4
  46.0 26.9 all-gather.6
  75.2 106.1 all-gather.8
  196.9 58.7 all-gather.10
  258.4 54.8 reduce-scatter.4
  341.9 100.0 reduce-scatter.6
  465.7 25.5 reduce-scatter.10
  493.7 28.8 reduce-scatter.8

commit v8 on v7

--- a/solution.py
+++ b/solution.py
@@ -596,7 +596,7 @@
 def rows_back_body(shard, *refs):
     grads, boths, outs = refs[:4], refs[4:6], refs[6:12]
     weights, held, sems, out_sem = refs[12:16], refs[16], refs[17], refs[18]
-    size, chunk = held.shape[0] // 8, 2 * step
+    size, chunk = held.shape[0] // 8, 4 * step
     chunks = held.shape[1] // chunk
 
     @pl.loop(0, chunks)
@@ -640,7 +640,7 @@
         [pltpu.VMEM((hidden, width), bf16)] * 4
         + [
             pltpu.VMEM((total, width), bf16),
-            pltpu.SemaphoreType.DMA((width // (2 * step),)),
+            pltpu.SemaphoreType.DMA((width // (4 * step),)),
             pltpu.SemaphoreType.DMA,
         ],
         [vmem_spec()] * 4 + [any_spec()] * 2,

time: 535 us -> 535 us (level)
  no operation moved by 1% of the time
where the time goes in v8:
time: 535 us; the launch traced here: 534 us
  Pallas kernels  231 us (43%)
  waiting for transfers between devices  193 us (36%)
  starting transfers between devices  54.1 us (10%)
  local copies, waits for them, and re-layouts  23.1 us (4%)
  other arithmetic  16.6 us (3%)
  between operations  15.6 us (3%)
    pallas_call x26, Pallas kernels, run(): pl.pallas_call(whole_body, out_shape=out_shapes, in_specs=in_specs + [any...  231 us
    ppermute x21, waiting for transfers between devices, y_swap(): return lax.ppermute(value, 'fsdp', [(i, i ^ 1) for i in range(self.fsdp)])  115 us
    ppermute x21, waiting for transfers between devices, x_swap(): return lax.ppermute(value, 'dp', [(i, i ^ 2) for i in range(self.dp)])  45.9 us
    ppermute x35, waiting for transfers between devices, core(): return lax.ppermute(value, 'dp', [(i, i ^ 1) for i in range(self.dp)])  26.4 us
    ppermute x21, starting transfers between devices, x_swap(): return lax.ppermute(value, 'dp', [(i, i ^ 2) for i in range(self.dp)])  23.8 us
    ppermute x21, starting transfers between devices, y_swap(): return lax.ppermute(value, 'fsdp', [(i, i ^ 1) for i in range(self.fsdp)])  22.1 us
    unnamed x138, local copies, waits for them, and re-layouts  13.7 us
  transfers between devices with their start and end apart: 86, of which 48 were waited for; matrix products, arithmetic and copies ran while one was open for 4% of the time, Pallas kernels for 43%

profile of v8, /device:TPU:0, one launch (start us, length us, event | category | flops | bytes accessed | tf_op | source)
XLA Modules:
  0.0 533.6 jit_solution(10318925125625630489)
XLA Ops:
  20.6 10.4 %collective-permute-done.1.refs_6_.refs_5_ = bf16[128,2048]{1,0:T(8,128)(2,1)S(1)} collective-permute-done((bf16[128,2048]{1,0:T(8,128)(2,1)S(1)}, bf16[128,2048]{1,0:T(8,128)(2,1)S(1)}, u32[]{:S(2)}, u32[]{:S(2)}) %collective-permute-start.1) | collective-permute-done | bytes 524320 | tf_op jit(solution)/shard_map/ppermute | solution.py:899
  34.4 10.6 %collective-permute-done.2.refs_7_.refs_6_ = bf16[128,2048]{1,0:T(8,128)(2,1)S(1)} collective-permute-done((bf16[128,2048]{1,0:T(8,128)(2,1)S(1)}, bf16[128,2048]{1,0:T(8,128)(2,1)S(1)}, u32[]{:S(2)}, u32[]{:S(2)}) %collective-permute-start.2) | collective-permute-done | bytes 524320 | tf_op jit(solution)/shard_map/ppermute | solution.py:899
  50.6 11.3 %collective-permute-done.4.refs_8_.refs_9_ = bf16[2,64,2432]{2,1,0:T(8,128)(2,1)} collective-permute-done((bf16[2,64,2432]{2,1,0:T(8,128)(2,1)S(1)}, bf16[2,64,2432]{2,1,0:T(8,128)(2,1)}, u32[]{:S(2)}, u32[]{:S(2)}) %collective-permute-start.4) | collective-permute-done | bytes 622624 | tf_op jit(solution)/shard_map/ppermute | solution.py:896
  67.4 12.8 %collective-permute-done.6.refs_6_.refs_7_ = bf16[2,64,2432]{2,1,0:T(8,128)(2,1)} collective-permute-done((bf16[2,64,2432]{2,1,0:T(8,128)(2,1)S(1)}, bf16[2,64,2432]{2,1,0:T(8,128)(2,1)}, u32[]{:S(2)}, u32[]{:S(2)}) %collective-permute-start.6) | collective-permute-done | bytes 622624 | tf_op jit(solution)/shard_map/ppermute | solution.py:899
  81.9 11.2 %collective-permute-done.8.refs_10_.refs_11_ = bf16[2,64,2432]{2,1,0:T(8,128)(2,1)} collective-permute-done((bf16[2,64,2432]{2,1,0:T(8,128)(2,1)}, bf16[2,64,2432]{2,1,0:T(8,128)(2,1)}, u32[]{:S(2)}, u32[]{:S(2)}) %collective-permute-start.8) | collective-permute-done | bytes 622624 | tf_op jit(solution)/shard_map/ppermute | solution.py:899
  100.4 11.4 %project.1 = (bf16[256,2048]{1,0:T(8,128)(2,1)}, bf16[256,2048]{1,0:T(8,128)(2,1)}, bf16[256,256]{1,0:T(8,128)(2,1)}, f32[8,2048]{1,0:T(8,128)}) custom-call(s32[2]{0:T(128)} %pad_add_fusion.refs_0_, bf16[256,2048]{1,0:T(8,128)(2,1)} %refs_1_.5, f32[256,128]{1,0:T(8,128)} %get-tuple-element.264.refs_2_.refs_7_, ...), custom_call_target="tpu_custom_call" | custom-call | flops 1 | bytes 1 | tf_op jit(solution)/shard_map/project/pallas_call | solution.py:68
  115.9 13.2 %attend.1 = (bf16[16,256,256]{2,1,0:T(8,128)(2,1)}, bf16[256,2048]{1,0:T(8,128)(2,1)}, bf16[2048,256]{1,0:T(8,128)(2,1)}, bf16[2048,256]{1,0:T(8,128)(2,1)}) custom-call(s32[2]{0:T(128)} %pad_add_fusion.refs_0_, bf16[256,2048]{1,0:T(8,128)(2,1)} %get-tuple-element.140.refs_1_.refs_4_, bf16[256,256]{1,0:T(8,128)(2,1)} %get-tuple-element.124.refs_2_.refs_5_, ...), custom_call_target="tpu_custom_call" | custom-call | flops 1 | bytes 1 | tf_op jit(solution)/shard_map/attend/pallas_call | solution.py:68
  146.4 9.7 %mix.1 = (f32[256,2048]{1,0:T(8,128)}, bf16[128,2048]{1,0:T(8,128)(2,1)}, bf16[128,2048]{1,0:T(8,128)(2,1)}) custom-call(s32[2]{0:T(128)} %pad_add_fusion.refs_0_, bf16[256,2048]{1,0:T(8,128)(2,1)} %refs_1_.5, bf16[256,2048]{1,0:T(8,128)(2,1)} %get-tuple-element.143.refs_2_, f32[8,2048]{1,0:T(8,128)} %get-tuple-element.144.refs_3_.refs_1_.refs_2_, ...), custom_call_target="tpu_custom_call" | custom-call | flops 1 | bytes 1 | tf_op jit(solution)/shard_map/mix/pallas_call | solution.py:68
  158.4 12.0 %collective-permute-done.34.refs_2_.refs_4_ = bf16[128,2048]{1,0:T(8,128)(2,1)S(1)} collective-permute-done((bf16[128,2048]{1,0:T(8,128)(2,1)}, bf16[128,2048]{1,0:T(8,128)(2,1)S(1)}, u32[]{:S(2)}, u32[]{:S(2)}) %collective-permute-start.34) | collective-permute-done | bytes 524320 | tf_op jit(solution)/shard_map/ppermute | solution.py:896
  175.6 11.0 %collective-permute-done.37.refs_4_.refs_6_ = bf16[128,2048]{1,0:T(8,128)(2,1)S(1)} collective-permute-done((bf16[128,2048]{1,0:T(8,128)(2,1)}, bf16[128,2048]{1,0:T(8,128)(2,1)S(1)}, u32[]{:S(2)}, u32[]{:S(2)}) %collective-permute-start.37) | collective-permute-done | bytes 524320 | tf_op jit(solution)/shard_map/ppermute | solution.py:899
  198.8 12.7 %gate.2 = (bf16[1024,704]{1,0:T(8,128)(2,1)}, bf16[1024,704]{1,0:T(8,128)(2,1)}, bf16[1024,704]{1,0:T(8,128)(2,1)}) custom-call(bf16[128,2048]{1,0:T(8,128)(2,1)} %get-tuple-element.168.refs_0_.refs_2_, bf16[128,2048]{1,0:T(8,128)(2,1)} %get-tuple-element.169.refs_1_.refs_3_, bf16[128,2048]{1,0:T(8,128)(2,1)} %copy-done.10, bf16[128,2048]{1,0:T(8,128)(2,1)} %copy-done.13, ...), custom_call_target="tpu_custom_call" | custom-call | flops 1 | bytes 1 | tf_op jit(solution)/shard_map/gate/pallas_call | solution.py:68
  211.5 12.8 %gate.3 = (bf16[1024,704]{1,0:T(8,128)(2,1)}, bf16[1024,704]{1,0:T(8,128)(2,1)}, bf16[1024,704]{1,0:T(8,128)(2,1)}) custom-call(bf16[128,2048]{1,0:T(8,128)(2,1)} %get-tuple-element.168.refs_0_.refs_2_, bf16[128,2048]{1,0:T(8,128)(2,1)} %get-tuple-element.169.refs_1_.refs_3_, bf16[128,2048]{1,0:T(8,128)(2,1)} %copy-done.10, bf16[128,2048]{1,0:T(8,128)(2,1)} %copy-done.13, ...), custom_call_target="tpu_custom_call" | custom-call | flops 1 | bytes 1 | tf_op jit(solution)/shard_map/gate/pallas_call | solution.py:68
  225.4 9.4 %hidden_sums.4 = (bf16[176,2048]{1,0:T(8,128)(2,1)}, bf16[176,2048]{1,0:T(8,128)(2,1)}, bf16[176,2048]{1,0:T(8,128)(2,1)}, bf16[176,2048]{1,0:T(8,128)(2,1)}) custom-call(bf16[1024,704]{1,0:T(8,128)(2,1)} %get-tuple-element.174.refs_0_.refs_1_, bf16[128,2048]{1,0:T(8,128)(2,1)} %copy-done.1, bf16[128,2048]{1,0:T(8,128)(2,1)} %copy-done, ...), custom_call_target="tpu_custom_call" | custom-call | flops 1 | bytes 1 | tf_op jit(solution)/shard_map/hidden_sums/pallas_call | solution.py:68
  241.3 9.6 %hidden_sums.5 = bf16[704,2048]{1,0:T(8,128)(2,1)} custom-call(bf16[1024,704]{1,0:T(8,128)(2,1)} %get-tuple-element.173.refs_9_.refs_0_, bf16[128,2048]{1,0:T(8,128)(2,1)} %copy-done.1, bf16[128,2048]{1,0:T(8,128)(2,1)} %copy-done, bf16[128,2048]{1,0:T(8,128)(2,1)} %copy-done.5, bf16[128,2048]{1,0:T(8,128)(2,1)} %copy-done.9, bf16[128,2048]{1,0:T(8,128)(2,1)} %copy-done.8, ...), custom_call_target="tpu_custom_call" | custom-call | flops 1 | bytes 1 | tf_op jit(solution)/shard_map/hidden_sums/pallas_call | solution.py:68
  266.4 8.9 %gate_back.3 = (bf16[1024,704]{1,0:T(8,128)(2,1)}, bf16[1024,704]{1,0:T(8,128)(2,1)}) custom-call(bf16[128,2048]{1,0:T(8,128)(2,1)} %copy-done.1, bf16[128,2048]{1,0:T(8,128)(2,1)} %copy-done, bf16[128,2048]{1,0:T(8,128)(2,1)} %copy-done.5, bf16[128,2048]{1,0:T(8,128)(2,1)} %copy-done.9, bf16[128,2048]{1,0:T(8,128)(2,1)} %copy-done.8, ...), custom_call_target="tpu_custom_call" | custom-call | flops 1 | bytes 1 | tf_op jit(solution)/shard_map/gate_back/pallas_call | solution.py:68
  275.3 21.1 %rows_back.1 = (bf16[128,2048]{1,0:T(8,128)(2,1)}, bf16[128,2048]{1,0:T(8,128)(2,1)}, bf16[128,2048]{1,0:T(8,128)(2,1)}, bf16[128,2048]{1,0:T(8,128)(2,1)}, bf16...) custom-call(bf16[1024,704]{1,0:T(8,128)(2,1)} %get-tuple-element.182.refs_11_.refs_0_, ...), custom_call_target="tpu_custom_call" | custom-call | flops 1 | bytes 1 | tf_op jit(solution)/shard_map/rows_back/pallas_call | solution.py:68
  299.4 13.8 %hidden_sums.6 = (bf16[176,2048]{1,0:T(8,128)(2,1)}, bf16[176,2048]{1,0:T(8,128)(2,1)}, bf16[176,2048]{1,0:T(8,128)(2,1)}, bf16[176,2048]{1,0:T(8,128)(2,1)}, bf...) custom-call(bf16[1024,704]{1,0:T(8,128)(2,1)} %get-tuple-element.186, ...), custom_call_target="tpu_custom_call" | custom-call | flops 1 | bytes 1 | tf_op jit(solution)/shard_map/hidden_sums/pallas_call | solution.py:68
  327.0 14.1 %hidden_sums.7.refs_10_ = bf16[1408,2048]{1,0:T(8,128)(2,1)} custom-call(bf16[1024,704]{1,0:T(8,128)(2,1)} %get-tuple-element.182.refs_11_.refs_0_, bf16[1024,704]{1,0:T(8,128)(2,1)} %get-tuple-element.183.refs_1_, bf16[128,2048]{1,0:T(8,128)(2,1)} %get-tuple-element.168.refs_0_.refs_2_, bf16[128,2048]{1,0:T(8,128)(2,1)} %get-tuple-element.169.refs_1_.refs_3_, ...), custom_call_target="tpu_custom_call" | custom-call | flops 1 | bytes 1 | tf_op jit(solution)/shard_map/hidden_sums/pallas_call | solution.py:68
  344.2 11.3 %collective-permute-done.49.refs_9_ = bf16[128,2048]{1,0:T(8,128)(2,1)S(1)} collective-permute-done((bf16[128,2048]{1,0:T(8,128)(2,1)S(1)}, bf16[128,2048]{1,0:T(8,128)(2,1)S(1)}, u32[]{:S(2)}, u32[]{:S(2)}) %collective-permute-start.49) | collective-permute-done | bytes 524320 | tf_op jit(solution)/shard_map/ppermute | solution.py:899
  383.6 19.1 %attend_back.1 = (bf16[256,2304]{1,0:T(8,128)(2,1)}, f32[256,256]{1,0:T(8,128)}) custom-call(s32[2]{0:T(128)} %pad_add_fusion.refs_0_, f32[1]{0:T(128)} %bitcast.9.refs_0_.refs_1_, bf16[256,2048]{1,0:T(8,128)(2,1)} %get-tuple-element.206.refs_1_.refs_2_, bf16[256,256]{1,0:T(8,128)(2,1)} %refs_3_.3, bf16[256,2048]{1,0:T(8,128)(2,1)} %get-tuple-element.140.refs_1_.refs_4_, ...), custom_call_target="tpu_custom_call" | custom-call | flops 1 | bytes 1 | tf_op jit(solution)/shard_map/attend_back/pallas_call | solution.py:68
  435.7 12.8 %finish.1 = (f32[256,2048]{1,0:T(8,128)}, f32[8,2048]{1,0:T(8,128)}) custom-call(s32[2]{0:T(128)} %pad_add_fusion.refs_0_, bf16[256,2048]{1,0:T(8,128)(2,1)} %refs_1_.5, f32[8,2048]{1,0:T(8,128)} %get-tuple-element.144.refs_3_.refs_1_.refs_2_, bf16[256,2304]{1,0:T(8,128)(2,1)} %get-tuple-element.212.refs_4_.refs_1_.refs_3_, ...), custom_call_target="tpu_custom_call" | custom-call | flops 1 | bytes 1 | tf_op jit(solution)/shard_map/finish/pallas_call | solution.py:68
  449.5 9.7 %collective-permute-done.64.refs_3_ = bf16[256,2304]{1,0:T(8,128)(2,1)S(1)} collective-permute-done((bf16[256,2304]{1,0:T(8,128)(2,1)}, bf16[256,2304]{1,0:T(8,128)(2,1)S(1)}, u32[]{:S(2)}, u32[]{:S(2)}) %collective-permute-start.64) | collective-permute-done | bytes 1179680 | tf_op jit(solution)/shard_map/ppermute | solution.py:899
  469.9 11.8 %down.1 = (bf16[128,2048]{1,0:T(8,128)(2,1)}, bf16[128,2048]{1,0:T(8,128)(2,1)}, bf16[128,2048]{1,0:T(8,128)(2,1)}, bf16[128,2048]{1,0:T(8,128)(2,1)}, bf16[256,...) custom-call(bf16[1024,704]{1,0:T(8,128)(2,1)} %get-tuple-element.173.refs_9_.refs_0_, ...), custom_call_target="tpu_custom_call" | custom-call | flops 1 | bytes 1 | tf_op jit(solution)/shard_map/down/pallas_call | solution.py:68
  487.2 19.3 %collective-permute-done.68.refs_3_ = bf16[256,2048]{1,0:T(8,128)(2,1)S(1)} collective-permute-done((bf16[256,2048]{1,0:T(8,128)(2,1)}, bf16[256,2048]{1,0:T(8,128)(2,1)S(1)}, u32[]{:S(2)}, u32[]{:S(2)}) %collective-permute-start.68) | collective-permute-done | bytes 1048608 | tf_op jit(solution)/shard_map/ppermute | solution.py:899
  (351 shorter events, 217.8 us)
Async XLA Ops:
  7.2 38.3 %all-gather.5.cloned.1.call-start = ((), (), s32[]{:S(2)}) async-start(), calls=%async_computation.4 | async-start | bytes 1556480 | tf_op jit(solution)/shard_map/all_gather | solution.py:918
  9.8 83.4 %all-gather.7.cloned.1.call-start = ((), (), s32[]{:S(2)}) async-start(), calls=%async_computation.5 | async-start | bytes 1310720 | tf_op jit(solution)/shard_map/all_gather | solution.py:918
  10.5 186.2 %all-gather.9.cloned.1.call-start = ((), (), s32[]{:S(2)}) async-start(), calls=%async_computation.6 | async-start | bytes 7208960 | tf_op jit(solution)/shard_map/all_gather | solution.py:918
  13.7 242.0 %all-gather.11.cloned.1.call-start = ((), (), s32[]{:S(2)}) async-start(), calls=%async_computation.7 | async-start | bytes 3604480 | tf_op jit(solution)/shard_map/all_gather | solution.py:918
  65.3 27.9 %collective-permute-start.8 = (bf16[2,64,2432]{2,1,0:T(8,128)(2,1)}, bf16[2,64,2432]{2,1,0:T(8,128)(2,1)}, u32[]{:S(2)}, u32[]{:S(2)}) collective-permute-start(bf16[2,64,2432]{2,1,0:T(8,128)(2,1)} %collective-permute-done.4.refs_8_.refs_9_), channel_id=1, source_target_pairs={{0,1},{1,0},{2,3},{3,2},{4,5},{5,4},{6,7},{7,6},{8,9},{9,8},{10,11... | collective-permute-start | bytes 1867784 | tf_op jit(solution)/shard_map/ppermute | solution.py:899
  65.9 27.3 %collective-permute-start.11 = (bf16[2,64,2432]{2,1,0:T(8,128)(2,1)}, bf16[2,64,2432]{2,1,0:T(8,128)(2,1)}, u32[]{:S(2)}, u32[]{:S(2)}) collective-permute-start(bf16[2,64,2432]{2,1,0:T(8,128)(2,1)} %bitcast.6.refs_5_.refs_6_), channel_id=1, source_target_pairs={{0,8},{8,0},{16,24},{24,16},{1,9},{9,1},{17,25},{25,17},{2,10},{10... | collective-permute-start | bytes 1867784 | tf_op jit(solution)/shard_map/ppermute | solution.py:885
  65.9 28.7 %collective-permute-start.7 = (bf16[2,64,2432]{2,1,0:T(8,128)(2,1)}, bf16[2,64,2432]{2,1,0:T(8,128)(2,1)}, u32[]{:S(2)}, u32[]{:S(2)}) collective-permute-start(bf16[2,64,2432]{2,1,0:T(8,128)(2,1)} %bitcast.6.refs_5_.refs_6_), channel_id=1, source_target_pairs={{0,16},{8,24},{16,0},{24,8},{1,17},{9,25},{17,1},{25,9},{2,18},{10... | collective-permute-start | bytes 1867784 | tf_op jit(solution)/shard_map/ppermute | solution.py:896
  114.8 22.8 %collective-permute-start.23 = (bf16[2,64,2048]{2,1,0:T(8,128)(2,1)S(1)}, bf16[2,64,2048]{2,1,0:T(8,128)(2,1)}, u32[]{:S(2)}, u32[]{:S(2)}) collective-permute-start(bf16[2,64,2048]{2,1,0:T(8,128)(2,1)S(1)} %collective-permute-done.19.refs_7_.refs_12_), channel_id=1, source_target_pairs={{0,16},{8,24},{16,0},{24,8},{1,17},{9,25},{17,1},{25,9},{2,18},{10... | collective-permute-start | bytes 1572872 | tf_op jit(solution)/shard_map/ppermute | solution.py:896
  172.8 23.1 %collective-permute-start.38 = (bf16[128,2048]{1,0:T(8,128)(2,1)S(1)}, bf16[128,2048]{1,0:T(8,128)(2,1)S(1)}, u32[]{:S(2)}, u32[]{:S(2)}) collective-permute-start(bf16[128,2048]{1,0:T(8,128)(2,1)S(1)} %collective-permute-done.34.refs_2_.refs_4_), channel_id=1, source_target_pairs={{0,1},{1,0},{2,3},{3,2},{4,5},{5,4},{6,7},{7,6},{8,9},{9,8},{10,11... | collective-permute-start | bytes 1572872 | tf_op jit(solution)/shard_map/ppermute | solution.py:899
  174.2 22.6 %collective-permute-start.39 = (bf16[128,2048]{1,0:T(8,128)(2,1)S(1)}, bf16[128,2048]{1,0:T(8,128)(2,1)}, u32[]{:S(2)}, u32[]{:S(2)}) collective-permute-start(bf16[128,2048]{1,0:T(8,128)(2,1)S(1)} %collective-permute-done.35.refs_5_.refs_7_), channel_id=1, source_target_pairs={{0,16},{8,24},{16,0},{24,8},{1,17},{9,25},{17,1},{25,9},{2,18},{10... | collective-permute-start | bytes 1572872 | tf_op jit(solution)/shard_map/ppermute | solution.py:896
  196.8 144.4 %reduce-scatter.5.cloned.1.call-start = ((), (), s32[]{:S(2)}) async-start(), calls=%async_computation.8 | async-start | bytes 3604480 | tf_op jit(solution)/shard_map/reduce_scatter | solution.py:921
  197.0 27.4 %collective-permute-start.33 = (bf16[128,2048]{1,0:T(8,128)(2,1)S(1)}, bf16[128,2048]{1,0:T(8,128)(2,1)S(1)}, u32[]{:S(2)}, u32[]{:S(2)}) collective-permute-start(bf16[128,2048]{1,0:T(8,128)(2,1)S(1)} %get-tuple-element.164.refs_1_.refs_0_), channel_id=1, source_target_pairs={{0,1},{1,0},{2,3},{3,2},{4,5},{5,4},{6,7},{7,6},{8,9},{9,8},{10,11... | collective-permute-start | bytes 1572872 | tf_op jit(solution)/shard_map/ppermute | solution.py:899
  198.1 26.3 %collective-permute-start.32 = (bf16[128,2048]{1,0:T(8,128)(2,1)S(1)}, bf16[128,2048]{1,0:T(8,128)(2,1)S(1)}, u32[]{:S(2)}, u32[]{:S(2)}) collective-permute-start(bf16[128,2048]{1,0:T(8,128)(2,1)S(1)} %get-tuple-element.165.refs_2_.refs_1_), channel_id=1, source_target_pairs={{0,16},{8,24},{16,0},{24,8},{1,17},{9,25},{17,1},{25,9},{2,18},{10... | collective-permute-start | bytes 1572872 | tf_op jit(solution)/shard_map/ppermute | solution.py:896
  255.7 203.9 %reduce-scatter.7.cloned.1.call-start = ((), (), s32[]{:S(2)}) async-start(), calls=%async_computation.9 | async-start | bytes 7208960 | tf_op jit(solution)/shard_map/reduce_scatter | solution.py:921
  296.4 25.9 %collective-permute-start.46 = (bf16[256,2048]{1,0:T(8,128)(2,1)}, bf16[256,2048]{1,0:T(8,128)(2,1)S(1)}, u32[]{:S(2)}, u32[]{:S(2)}) collective-permute-start(bf16[256,2048]{1,0:T(8,128)(2,1)} %get-tuple-element.189), channel_id=1, source_target_pairs={{0,1},{1,0},{2,3},{3,2},{4,5},{5,4},{6,7},{7,6},{8,9},{9,8},{10,11... | collective-permute-start | bytes 3145736 | tf_op jit(solution)/shard_map/ppermute | solution.py:899
  298.0 25.6 %collective-permute-start.47 = (bf16[256,2048]{1,0:T(8,128)(2,1)}, bf16[256,2048]{1,0:T(8,128)(2,1)S(1)}, u32[]{:S(2)}, u32[]{:S(2)}) collective-permute-start(bf16[256,2048]{1,0:T(8,128)(2,1)} %get-tuple-element.192), channel_id=1, source_target_pairs={{0,16},{8,24},{16,0},{24,8},{1,17},{9,25},{17,1},{25,9},{2,18},{10... | collective-permute-start | bytes 3145736 | tf_op jit(solution)/shard_map/ppermute | solution.py:896
  341.2 173.5 %reduce-scatter.11.cloned.1.call-start = ((), (), s32[]{:S(2)}) async-start(), calls=%async_computation.11 | async-start | bytes 1310720 | tf_op jit(solution)/shard_map/reduce_scatter | solution.py:921
  381.3 25.5 %collective-permute-start.60 = (bf16[256,2048]{1,0:T(8,128)(2,1)}, bf16[256,2048]{1,0:T(8,128)(2,1)S(1)}, u32[]{:S(2)}, u32[]{:S(2)}) collective-permute-start(bf16[256,2048]{1,0:T(8,128)(2,1)} %get-tuple-element.215), channel_id=1, source_target_pairs={{0,16},{8,24},{16,0},{24,8},{1,17},{9,25},{17,1},{25,9},{2,18},{10... | collective-permute-start | bytes 3145736 | tf_op jit(solution)/shard_map/ppermute | solution.py:896
  382.8 25.1 %collective-permute-start.61 = (bf16[256,2048]{1,0:T(8,128)(2,1)}, bf16[256,2048]{1,0:T(8,128)(2,1)S(1)}, u32[]{:S(2)}, u32[]{:S(2)}) collective-permute-start(bf16[256,2048]{1,0:T(8,128)(2,1)} %get-tuple-element.216), channel_id=1, source_target_pairs={{0,1},{1,0},{2,3},{3,2},{4,5},{5,4},{6,7},{7,6},{8,9},{9,8},{10,11... | collective-permute-start | bytes 3145736 | tf_op jit(solution)/shard_map/ppermute | solution.py:899
  430.9 28.3 %collective-permute-start.64 = (bf16[256,2304]{1,0:T(8,128)(2,1)}, bf16[256,2304]{1,0:T(8,128)(2,1)S(1)}, u32[]{:S(2)}, u32[]{:S(2)}) collective-permute-start(bf16[256,2304]{1,0:T(8,128)(2,1)} %get-tuple-element.221), channel_id=1, source_target_pairs={{0,1},{1,0},{2,3},{3,2},{4,5},{5,4},{6,7},{7,6},{8,9},{9,8},{10,11... | collective-permute-start | bytes 3538952 | tf_op jit(solution)/shard_map/ppermute | solution.py:899
  431.7 27.9 %collective-permute-start.65 = (bf16[256,2304]{1,0:T(8,128)(2,1)}, bf16[256,2304]{1,0:T(8,128)(2,1)S(1)}, u32[]{:S(2)}, u32[]{:S(2)}) collective-permute-start(bf16[256,2304]{1,0:T(8,128)(2,1)} %get-tuple-element.224), channel_id=1, source_target_pairs={{0,16},{8,24},{16,0},{24,8},{1,17},{9,25},{17,1},{25,9},{2,18},{10... | collective-permute-start | bytes 3538952 | tf_op jit(solution)/shard_map/ppermute | solution.py:896
  465.0 59.9 %reduce-scatter.9.cloned.1.call-start = ((), (), s32[]{:S(2)}) async-start(), calls=%async_computation.10 | async-start | bytes 1556480 | tf_op jit(solution)/shard_map/reduce_scatter | solution.py:921
  483.4 23.1 %collective-permute-start.68 = (bf16[256,2048]{1,0:T(8,128)(2,1)}, bf16[256,2048]{1,0:T(8,128)(2,1)S(1)}, u32[]{:S(2)}, u32[]{:S(2)}) collective-permute-start(bf16[256,2048]{1,0:T(8,128)(2,1)} %get-tuple-element.237), channel_id=1, source_target_pairs={{0,1},{1,0},{2,3},{3,2},{4,5},{5,4},{6,7},{7,6},{8,9},{9,8},{10,11... | collective-permute-start | bytes 3145736 | tf_op jit(solution)/shard_map/ppermute | solution.py:899
  484.4 22.8 %collective-permute-start.69 = (bf16[256,2048]{1,0:T(8,128)(2,1)}, bf16[256,2048]{1,0:T(8,128)(2,1)S(1)}, u32[]{:S(2)}, u32[]{:S(2)}) collective-permute-start(bf16[256,2048]{1,0:T(8,128)(2,1)} %get-tuple-element.240), channel_id=1, source_target_pairs={{0,16},{8,24},{16,0},{24,8},{1,17},{9,25},{17,1},{25,9},{2,18},{10... | collective-permute-start | bytes 3145736 | tf_op jit(solution)/shard_map/ppermute | solution.py:896
  (130 other events, 1694.8 us)
Sparse Core Ops, SparseCore 0:
  10.2 34.2 all-gather.4
  46.0 26.9 all-gather.6
  75.2 106.1 all-gather.8
  196.9 58.7 all-gather.10
  258.4 54.8 reduce-scatter.4
  341.3 100.0 reduce-scatter.6
  465.2 25.4 reduce-scatter.10
  493.1 28.8 reduce-scatter.8
